TPU v7x, 32 devices: a whole 2x2x4 slice. The times are simulated.
32 devices in a mesh: ep: 8 (over z, x), tp: 4 (over y, core).
Axes of the slice: x: 2, y: 2, z: 4, core: 2. Of those that a mesh axis runs over, the one named last changes fastest.
Arguments:
- tokens: bfloat16 [1024, 1024], P('ep'), may hold values from -6 to 6
- segment_ids: int32 [8, 128], P('ep'), may hold values from 0 to 15, never falling along the last dimension, each value on 1 to 64 neighbouring positions
- route_ids: int32 [1024, 8], P('ep'), may hold values from 0 to 31, all different within a row; in each aligned block of 128 rows (0 to 127, 128 to 255, ...) at most 64 rows name the same one
- route_weights: float32 [1024, 8], P('ep'), may hold values from 0.03 to 0.3
- attn_gain: bfloat16 [1024], P('ep'), may hold values from 0.099609375 to 1.8984375
- query_weight: bfloat16 [1024, 1024], P('ep', 'tp'), may hold values from -0.1875 to 0.1875
- key_projection_matrix: bfloat16 [1024, 512], P('ep', 'tp'), may hold values from -0.1875 to 0.1875
- value_projection_matrix: bfloat16 [1024, 512], P('ep', 'tp'), may hold values from -0.1875 to 0.1875
- out_weight: bfloat16 [1024, 1024], P('ep', 'tp'), may hold values from -0.75 to 0.75
- ffn_gain: bfloat16 [1024], P('ep'), may hold values from 0.099609375 to 1.8984375
- gate_weight: bfloat16 [32, 1024, 512], P('ep', None, 'tp'), may hold values from -0.1875 to 0.1875
- up_weight: bfloat16 [32, 1024, 512], P('ep', None, 'tp'), may hold values from -0.1875 to 0.1875
- down_weight: bfloat16 [32, 512, 1024], P('ep', 'tp'), may hold values from -0.5 to 0.5
- cotangent: bfloat16 [1024, 1024], P('ep'), may hold values from -6 to 6
Outputs:
- mixed: bfloat16 [1024, 1024], P('ep')
- tokens_grad: float32 [1024, 1024], P('ep')
- attn_gain_grad: float32 [1024], P('ep')
- query_grad: float32 [1024, 1024], P('ep', 'tp')
- key_grad: float32 [1024, 512], P('ep', 'tp')
- value_grad: float32 [1024, 512], P('ep', 'tp')
- out_grad: float32 [1024, 1024], P('ep', 'tp')
- ffn_gain_grad: float32 [1024], P('ep')
- gate_grad: float32 [32, 1024, 512], P('ep', None, 'tp')
- up_grad: float32 [32, 1024, 512], P('ep', None, 'tp')
- down_grad: float32 [32, 512, 1024], P('ep', 'tp')
Inputs may be any that keep to these rules, and one draw needn't show every extreme that they name: `segment_ids`: each row is non-decreasing; every sequence has 1 to 64 tokens and some sequence has exactly 64. `route_ids`: the 8 experts of a token differ; among the rows of one ep group no expert is named more than 64 times, and in some group some expert exactly 64 times.
All inputs are finite; a program needn't handle non-finite values.
Results may differ from a plain program's by a relative error of at most 0.012.
Values may be sent and summed in bfloat16 or wider, within the bound.
No kernel may reach another device: no remote copies, remote signals or barrier semaphores. Data moves between devices by JAX's collectives and lax.ppermute only.
A program may use at most 128 MiB of HBM per device.

v0:
```python
import jax
import jax.numpy as jnp
from jax import lax
from jax.sharding import PartitionSpec as P

HEAD_SIZE = 64
EXPERTS = 32
TOP = 8
CAP = 64


NORM_EPSILON = 1e-06
ROPE_BASE = 10000.0
MASKED = -1e30


def positions_and_mask(segment_row):
    count = segment_row.shape[0]
    index = jnp.arange(count, dtype=jnp.int32)
    same = segment_row[:, None] == segment_row[None, :]
    before = index[None, :] < index[:, None]
    position = jnp.sum((same & before).astype(jnp.int32), axis=1)
    allowed = same & (index[None, :] <= index[:, None])
    return (position, allowed)


def rope_tables(position):
    half = HEAD_SIZE // 2
    steps = jnp.arange(half, dtype=jnp.float32) * (2.0 / HEAD_SIZE)
    frequency = jnp.exp(-jnp.log(jnp.float32(ROPE_BASE)) * steps)
    angle = position.astype(jnp.float32)[:, None] * frequency[None, :]
    return (jnp.cos(angle)[:, None, :], jnp.sin(angle)[:, None, :])


def rotate(values, cosine, sine):
    half = values.shape[-1] // 2
    first = values[..., :half]
    second = values[..., half:]
    return jnp.concatenate(
        [first * cosine - second * sine, second * cosine + first * sine], axis=-1
    )


def rotate_back(values, cosine, sine):
    half = values.shape[-1] // 2
    first = values[..., :half]
    second = values[..., half:]
    return jnp.concatenate(
        [first * cosine + second * sine, second * cosine - first * sine], axis=-1
    )


def rms_inverse(values):
    return lax.rsqrt(jnp.mean(values * values, axis=-1, keepdims=True) + NORM_EPSILON)


def rms_backward(values, inverse, gain, upstream):
    gain_term = jnp.sum(upstream * values * inverse, axis=0)
    inner = jnp.mean(values * gain * upstream, axis=-1, keepdims=True)
    input_term = inverse * (gain * upstream) - values * inverse * inverse * inverse * inner
    return (input_term, gain_term)


def dispatch_table(route_rows):
    flat = route_rows.reshape(-1)
    onehot = (flat[:, None] == jnp.arange(EXPERTS, dtype=jnp.int32)[None, :]).astype(jnp.int32)
    before = jnp.cumsum(onehot, axis=0) - onehot
    slot = jnp.sum(before * onehot, axis=1)
    dest = flat * CAP + slot
    table = (
        jnp.full((EXPERTS * CAP,), -1, jnp.int32)
        .at[dest]
        .set(jnp.arange(flat.shape[0], dtype=jnp.int32))
    )
    return (dest, table)


def attend(grouped, key_rot, value_rows, allowed, scale):
    scores = (
        jnp.einsum("thgd,uhd->hgtu", grouped, key_rot, preferred_element_type=jnp.float32) * scale
    )
    scores = jnp.where(allowed, scores, MASKED)
    peak = jnp.max(scores, axis=-1, keepdims=True)
    logsum = peak[..., 0] + jnp.log(jnp.sum(jnp.exp(scores - peak), axis=-1))
    probs = jnp.exp(scores - logsum[..., None]).astype(jnp.bfloat16)
    attended = jnp.einsum(
        "hgtu,uhd->thgd", probs, value_rows, preferred_element_type=jnp.float32
    ).astype(jnp.bfloat16)
    return (attended, logsum)


def attend_back(grouped, key_rot, value_rows, attended, logsum, grad_attended, allowed, scale):
    scores = (
        jnp.einsum("thgd,uhd->hgtu", grouped, key_rot, preferred_element_type=jnp.float32) * scale
    )
    scores = jnp.where(allowed, scores, MASKED)
    probs = jnp.exp(scores - logsum[..., None])
    probs_low = probs.astype(jnp.bfloat16)
    value_grad = jnp.einsum(
        "hgtu,thgd->uhd", probs_low, grad_attended, preferred_element_type=jnp.float32
    )
    grad_probs = jnp.einsum(
        "thgd,uhd->hgtu", grad_attended, value_rows, preferred_element_type=jnp.float32
    )
    delta = jnp.einsum(
        "thgd,thgd->hgt", grad_attended, attended, preferred_element_type=jnp.float32
    )
    grad_scores = (probs * (grad_probs - delta[..., None]) * scale).astype(jnp.bfloat16)
    query_grad = jnp.einsum(
        "hgtu,uhd->thgd", grad_scores, key_rot, preferred_element_type=jnp.float32
    )
    key_grad = jnp.einsum(
        "hgtu,thgd->uhd", grad_scores, grouped, preferred_element_type=jnp.float32
    )
    return (query_grad, key_grad, value_grad)


def body(
    tokens,
    segment_ids,
    route_ids,
    route_weights,
    attn_gain,
    query_weight,
    key_projection_matrix,
    value_projection_matrix,
    out_weight,
    ffn_gain,
    gate_weight,
    up_weight,
    down_weight,
    cotangent,
):
    gain_low_one, query_full, key_full, value_full, out_full, gain_low_two = (
        lax.all_gather(attn_gain, "ep", axis=0, tiled=True),
        lax.all_gather(query_weight, "ep", axis=0, tiled=True),
        lax.all_gather(key_projection_matrix, "ep", axis=0, tiled=True),
        lax.all_gather(value_projection_matrix, "ep", axis=0, tiled=True),
        lax.all_gather(out_weight, "ep", axis=0, tiled=True),
        lax.all_gather(ffn_gain, "ep", axis=0, tiled=True),
    )
    gain_one = gain_low_one.astype(jnp.float32)
    second_norm_gain = gain_low_two.astype(jnp.float32)
    scale = HEAD_SIZE ** (-0.5)
    rows = tokens.shape[0]
    width = tokens.shape[1]
    position, allowed = positions_and_mask(segment_ids[0])
    cosine, sine = rope_tables(position)
    tokens_float = tokens.astype(jnp.float32)
    inverse_one = rms_inverse(tokens_float)
    normed_one = (tokens_float * inverse_one * gain_one).astype(jnp.bfloat16)
    query = jnp.dot(normed_one, query_full, preferred_element_type=jnp.float32).reshape(
        rows, -1, HEAD_SIZE
    )
    keys = jnp.dot(normed_one, key_full, preferred_element_type=jnp.float32).reshape(
        rows, -1, HEAD_SIZE
    )
    query_rot = rotate(query, cosine, sine).astype(jnp.bfloat16)
    key_rot = rotate(keys, cosine, sine).astype(jnp.bfloat16)
    value_rows = (
        jnp.dot(normed_one, value_full, preferred_element_type=jnp.float32)
        .astype(jnp.bfloat16)
        .reshape(rows, -1, HEAD_SIZE)
    )
    grouped = query_rot.reshape(rows, key_rot.shape[1], -1, HEAD_SIZE)
    attended, logsum = attend(grouped, key_rot, value_rows, allowed, scale)
    attended_flat = attended.reshape(rows, -1)
    branch_part = jnp.einsum(
        "tk,dk->td", attended_flat, out_full, preferred_element_type=jnp.float32
    )
    branch = lax.psum(branch_part, "tp")
    hidden_one = tokens_float + branch
    inverse_two = rms_inverse(hidden_one)
    normed_two = (hidden_one * inverse_two * second_norm_gain).astype(jnp.bfloat16)
    gate_use, up_use, down_use = (gate_weight, up_weight, down_weight)
    member = 0
    spread = 1
    units = gate_use.shape[2]
    capacity = CAP // spread
    local_experts = gate_weight.shape[0]
    dest, table = dispatch_table(route_ids)
    values = table.reshape(EXPERTS, CAP)
    shaped = values.reshape((EXPERTS, capacity, spread) + values.shape[2:])
    table_own = lax.dynamic_index_in_dim(shaped, member, 2, keepdims=False)
    valid = table_own >= 0
    source = jnp.maximum(table_own, 0)
    token_slot = source // TOP
    send = jnp.where(valid[..., None], normed_two[token_slot], jnp.zeros((), jnp.bfloat16))
    route_expert = dest // CAP
    route_slot = dest % CAP
    route_index = route_expert * capacity + route_slot // spread
    owned = (route_slot % spread == member).astype(jnp.float32)
    received = lax.all_to_all(send, "ep", split_axis=0, concat_axis=0, tiled=True)
    sources = received.shape[0] // local_experts
    count = received.shape[1]
    inner = received.reshape(sources, local_experts, count, width)
    gate_pre = jnp.einsum("slcd,ldf->slcf", inner, gate_use, preferred_element_type=jnp.float32)
    up_pre = jnp.einsum("slcd,ldf->slcf", inner, up_use, preferred_element_type=jnp.float32)
    hidden = (gate_pre * jax.nn.sigmoid(gate_pre) * up_pre).astype(jnp.bfloat16)
    hidden_blocks = hidden.reshape(sources, local_experts, count, spread, units // spread)
    down_blocks = down_use.reshape(local_experts, spread, units // spread, width)
    pieces = jnp.einsum(
        "slcjf,ljfd->slcjd", hidden_blocks, down_blocks, preferred_element_type=jnp.float32
    ).astype(jnp.bfloat16)
    total = jnp.sum(pieces.astype(jnp.float32), axis=3)
    lead = received.shape[:2]
    expert_total = total.reshape(received.shape)
    gate_kept = gate_pre.reshape(lead + (units,))
    up_kept = up_pre.reshape(lead + (units,))
    returned = lax.all_to_all(
        expert_total.astype(jnp.bfloat16), "ep", split_axis=0, concat_axis=0, tiled=True
    )
    routed = (
        returned.reshape(EXPERTS * capacity, width)[route_index].astype(jnp.float32)
        * owned[:, None]
    )
    moe_part = jnp.sum(route_weights[:, :, None] * routed.reshape(rows, TOP, width), axis=1)
    moe = lax.psum(moe_part.astype(jnp.bfloat16), "tp").astype(jnp.float32)
    mixed = (hidden_one + moe).astype(jnp.bfloat16)
    grad_out = cotangent.astype(jnp.float32)
    slot_weight = jnp.where(valid, route_weights.reshape(-1)[source], 0.0)
    grad_send = (grad_out[token_slot] * slot_weight[..., None]).astype(jnp.bfloat16)
    sources = EXPERTS // local_experts
    gradient_received = lax.all_to_all(grad_send, "ep", split_axis=0, concat_axis=0, tiled=True)
    inner = received.reshape(sources, local_experts, capacity, width)
    gate_pre = gate_kept.reshape(sources, local_experts, capacity, units)
    up_pre = up_kept.reshape(sources, local_experts, capacity, units)
    grad_inner = gradient_received.reshape(sources, local_experts, capacity, width)
    sigma = jax.nn.sigmoid(gate_pre)
    active = gate_pre * sigma
    hidden = (active * up_pre).astype(jnp.bfloat16)
    grad_hidden = jnp.einsum(
        "slcd,lfd->slcf", grad_inner, down_use, preferred_element_type=jnp.float32
    )
    down_part = jnp.einsum("slcf,slcd->lfd", hidden, grad_inner, preferred_element_type=jnp.float32)
    grad_gate = (grad_hidden * up_pre * sigma * (1.0 + gate_pre * (1.0 - sigma))).astype(
        jnp.bfloat16
    )
    grad_up = (grad_hidden * active).astype(jnp.bfloat16)
    gate_part = jnp.einsum("slcd,slcf->ldf", inner, grad_gate, preferred_element_type=jnp.float32)
    up_part = jnp.einsum("slcd,slcf->ldf", inner, grad_up, preferred_element_type=jnp.float32)
    gate_blocks = grad_gate.reshape(sources, local_experts, capacity, spread, units // spread)
    up_blocks = grad_up.reshape(sources, local_experts, capacity, spread, units // spread)
    back_pieces = jnp.einsum(
        "slcjf,ldjf->slcjd",
        gate_blocks,
        gate_use.reshape(local_experts, width, spread, units // spread),
        preferred_element_type=jnp.float32,
    )
    back_pieces = back_pieces + jnp.einsum(
        "slcjf,ldjf->slcjd",
        up_blocks,
        up_use.reshape(local_experts, width, spread, units // spread),
        preferred_element_type=jnp.float32,
    )
    grad_total = jnp.sum(back_pieces.astype(jnp.bfloat16).astype(jnp.float32), axis=3).reshape(
        EXPERTS, capacity, width
    )
    grad_back = lax.all_to_all(
        grad_total.astype(jnp.bfloat16), "ep", split_axis=0, concat_axis=0, tiled=True
    )
    gate_grad, up_grad, down_grad = (gate_part, up_part, down_part)
    grad_routed = (
        grad_back.reshape(EXPERTS * capacity, width)[route_index].astype(jnp.float32)
        * owned[:, None]
    )
    grad_part = jnp.sum(grad_routed.reshape(rows, TOP, width), axis=1)
    grad_normed_two = lax.psum(grad_part, "tp")
    norm_term, ffn_gain_part = rms_backward(
        hidden_one, inverse_two, second_norm_gain, grad_normed_two
    )
    grad_hidden_one = grad_out + norm_term
    grad_branch = grad_hidden_one.astype(jnp.bfloat16)
    out_part = jnp.einsum(
        "td,tk->dk", grad_branch, attended_flat, preferred_element_type=jnp.float32
    )
    grad_attended = (
        jnp.dot(grad_branch, out_full, preferred_element_type=jnp.float32)
        .astype(jnp.bfloat16)
        .reshape(attended.shape)
    )
    query_grad_rot, key_grad_rot, value_grad_rows = attend_back(
        grouped, key_rot, value_rows, attended, logsum, grad_attended, allowed, scale
    )
    query_grad_rows = (
        rotate_back(query_grad_rot.reshape(rows, -1, HEAD_SIZE), cosine, sine)
        .astype(jnp.bfloat16)
        .reshape(rows, -1)
    )
    key_grad_rows = rotate_back(key_grad_rot, cosine, sine).astype(jnp.bfloat16).reshape(rows, -1)
    value_low = value_grad_rows.astype(jnp.bfloat16).reshape(rows, -1)
    grad_normed_part = jnp.einsum(
        "tk,dk->td", query_grad_rows, query_full, preferred_element_type=jnp.float32
    )
    grad_normed_part = grad_normed_part + jnp.einsum(
        "tk,dk->td", key_grad_rows, key_full, preferred_element_type=jnp.float32
    )
    grad_normed_part = grad_normed_part + jnp.einsum(
        "tk,dk->td", value_low, value_full, preferred_element_type=jnp.float32
    )
    grad_normed_one = lax.psum(grad_normed_part, "tp")
    query_part = jnp.einsum(
        "td,tk->dk", normed_one, query_grad_rows, preferred_element_type=jnp.float32
    )
    key_part = jnp.einsum(
        "td,tk->dk", normed_one, key_grad_rows, preferred_element_type=jnp.float32
    )
    value_part = jnp.einsum("td,tk->dk", normed_one, value_low, preferred_element_type=jnp.float32)
    input_term, attn_gain_part = rms_backward(tokens_float, inverse_one, gain_one, grad_normed_one)
    tokens_grad = grad_hidden_one + input_term
    attn_gain_grad, query_grad, key_grad, value_grad, out_grad, ffn_gain_grad = (
        lax.psum_scatter(attn_gain_part, "ep", scatter_dimension=0, tiled=True),
        lax.psum_scatter(query_part, "ep", scatter_dimension=0, tiled=True),
        lax.psum_scatter(key_part, "ep", scatter_dimension=0, tiled=True),
        lax.psum_scatter(value_part, "ep", scatter_dimension=0, tiled=True),
        lax.psum_scatter(out_part, "ep", scatter_dimension=0, tiled=True),
        lax.psum_scatter(ffn_gain_part, "ep", scatter_dimension=0, tiled=True),
    )
    return (
        mixed,
        tokens_grad,
        attn_gain_grad,
        query_grad,
        key_grad,
        value_grad,
        out_grad,
        ffn_gain_grad,
        gate_grad,
        up_grad,
        down_grad,
    )


def solution(mesh):
    placed = (
        P("ep", None),
        P("ep", None),
        P("ep", None),
        P("ep", None),
        P("ep"),
        P("ep", "tp"),
        P("ep", "tp"),
        P("ep", "tp"),
        P("ep", "tp"),
        P("ep"),
        P("ep", None, "tp"),
        P("ep", None, "tp"),
        P("ep", "tp", None),
        P("ep", None),
    )
    return jax.shard_map(
        body,
        mesh=mesh,
        in_specs=placed,
        out_specs=(
            P("ep", None),
            P("ep", None),
            P("ep"),
            P("ep", "tp"),
            P("ep", "tp"),
            P("ep", "tp"),
            P("ep", "tp"),
            P("ep"),
            P("ep", None, "tp"),
            P("ep", None, "tp"),
            P("ep", "tp", None),
        ),
        check_vma=False,
    )
```

profile of v0, /device:TPU:0, one launch (start us, length us, event | category | flops | bytes accessed | tf_op | source)
XLA Modules:
  0.0 966.3 jit_solution(1501945466416267839)
XLA Ops:
  10.1 22.4 %all-gather = bf16[8,1,128]{2,1,0:T(2,128)(2,1)S(1)} all-gather(bf16[1,1,128]{2,1,0:T(2,128)(2,1)} %bitcast.222), channel_id=1, replica_groups=mesh['ep'=8,'tp'=4] {'ep'}, dimensions={0}, use_global_device_ids=true | all-gather | bytes 2304 | tf_op jit(solution)/shard_map/all_gather | solution.py:135
  32.5 31.0 %all_gather.20 = bf16[1024,128]{1,0:T(8,128)(2,1)S(1)} all-gather(bf16[128,128]{1,0:T(8,128)(2,1)} %param.20), channel_id=1, replica_groups=mesh['ep'=8,'tp'=4] {'ep'}, dimensions={0}, use_global_device_ids=true | all-gather | bytes 294912 | tf_op jit(solution)/shard_map/all_gather | solution.py:137
  63.5 31.1 %all_gather.19 = bf16[1024,128]{1,0:T(8,128)(2,1)S(1)} all-gather(bf16[128,128]{1,0:T(8,128)(2,1)} %param.21), channel_id=1, replica_groups=mesh['ep'=8,'tp'=4] {'ep'}, dimensions={0}, use_global_device_ids=true | all-gather | bytes 294912 | tf_op jit(solution)/shard_map/all_gather | solution.py:138
  97.3 31.7 %all_gather.21 = bf16[1024,256]{1,0:T(8,128)(2,1)S(1)} all-gather(bf16[128,256]{1,0:T(8,128)(2,1)} %param.19), channel_id=1, replica_groups=mesh['ep'=8,'tp'=4] {'ep'}, dimensions={0}, use_global_device_ids=true | all-gather | bytes 589824 | tf_op jit(solution)/shard_map/all_gather | solution.py:136
  132.2 31.2 %all_gather.22 = bf16[1024,256]{1,0:T(8,128)(2,1)S(1)} all-gather(bf16[128,256]{1,0:T(8,128)(2,1)S(1)} %copy-done.32), channel_id=1, replica_groups=mesh['ep'=8,'tp'=4] {'ep'}, dimensions={0}, use_global_device_ids=true | all-gather | bytes 589824 | tf_op jit(solution)/shard_map/all_gather | solution.py:139
  165.9 9.0 reduce-window.6
  180.6 16.7 %all-gather.1 = bf16[8,1,128]{2,1,0:T(2,128)(2,1)S(1)} all-gather(bf16[1,1,128]{2,1,0:T(2,128)(2,1)S(1)} %bitcast.223), channel_id=1, replica_groups=mesh['ep'=8,'tp'=4] {'ep'}, dimensions={0}, use_global_device_ids=true | all-gather | bytes 2304 | tf_op jit(solution)/shard_map/all_gather | solution.py:140
  199.6 9.7 gather_fusion
  213.0 4.7 all-to-all-start
  217.9 8.6 gather_fusion.3
  226.7 9.8 %gather_fusion.2 = f32[2048,1024]{1,0:T(8,128)} fusion(f32[128,1024]{1,0:T(8,128)S(1)} %convert_element_type.176, s32[2048]{0:T(1024)S(1)} %broadcast_clamp_fusion), kind=kCustom, calls=%fused_computation.2 | custom fusion | bytes 16785408 | tf_op jit(solution)/shard_map/gather | solution.py:222
  236.5 5.9 multiply_convert_fusion
  242.4 67.4 %all-to-all-done = bf16[32,64,1024]{2,1,0:T(8,128)(2,1)} async-done(((bf16[32,64,1024]{2,1,0:T(8,128)(2,1)}), bf16[32,64,1024]{2,1,0:T(8,128)(2,1)}, u32[]{:S(2)}, u32[]{:S(2)}) %all-to-all-start) | async-done | bytes 4194336 | tf_op jit(solution)/shard_map/all_to_all | solution.py:193
  309.8 4.7 all-to-all-start.2
  314.5 4.8 fusion.16
  319.3 4.4 fusion.13
  323.8 83.2 %all-to-all-done.2 = bf16[32,64,1024]{2,1,0:T(8,128)(2,1)} async-done(((bf16[32,64,1024]{2,1,0:T(8,128)(2,1)}), bf16[32,64,1024]{2,1,0:T(8,128)(2,1)}, u32[]{:S(2)}, u32[]{:S(2)}) %all-to-all-start.2) | async-done | bytes 4194336 | tf_op jit(solution)/shard_map/all_to_all | solution.py:224
  416.8 4.6 all-to-all-start.3
  425.1 88.7 %all-to-all-done.3 = bf16[32,64,1024]{2,1,0:T(8,128)(2,1)} async-done(((bf16[32,64,1024]{2,1,0:T(8,128)(2,1)}), bf16[32,64,1024]{2,1,0:T(8,128)(2,1)}, u32[]{:S(2)}, u32[]{:S(2)}) %all-to-all-start.3) | async-done | bytes 4194336 | tf_op jit(solution)/shard_map/all_to_all | solution.py:259
  513.8 4.7 all-to-all-start.1
  519.2 8.1 gather_fusion.4
  529.8 81.3 %all-to-all-done.1 = bf16[32,64,1024]{2,1,0:T(8,128)(2,1)} async-done(((bf16[32,64,1024]{2,1,0:T(8,128)(2,1)}), bf16[32,64,1024]{2,1,0:T(8,128)(2,1)}, u32[]{:S(2)}, u32[]{:S(2)}) %all-to-all-start.1) | async-done | bytes 4194336 | tf_op jit(solution)/shard_map/all_to_all | solution.py:210
  611.0 8.1 gather_fusion.1
  622.8 29.4 %all-reduce.10.cloned.1.call-done = bf16[128,1024]{1,0:T(8,128)(2,1)} async-done(((bf16[128,1024]{1,0:T(8,128)(2,1)}), bf16[128,1024]{1,0:T(8,128)(2,1)}) %all-reduce.10.cloned.1.call-update) | async-done | bytes 262160 | tf_op jit(solution)/shard_map/psum | solution.py:218
  670.1 5.2 convolution_bitcast_fusion
  675.4 5.1 convolution_bitcast_fusion.1
  680.5 12.4 %all-reduce.14.cloned.1.call-done = f32[128,1024]{1,0:T(8,128)} async-done(((f32[128,1024]{1,0:T(8,128)}), f32[128,1024]{1,0:T(8,128)}) %all-reduce.14.cloned.1.call-update) | async-done | bytes 524304 | tf_op jit(solution)/shard_map/psum | solution.py:301
  694.1 21.7 %all-reduce.2 = (f32[1024]{0:T(1024)S(1)}, f32[1024]{0:T(1024)S(1)}) all-reduce(f32[1024]{0:T(1024)S(1)} %get-tuple-element.13, f32[1024]{0:T(1024)S(1)} %get-tuple-element.11), channel_id=2, replica_groups=mesh['ep'=8,'tp'=4] {'ep'}, use_global_device_ids=true, to_apply=%region_18.19.clone | all-reduce | flops 2048 | bytes 16384
  719.0 40.4 %reduce-scatter.9.cloned.1.call-done = f32[128,128]{1,0:T(8,128)} async-done(((f32[1024,128]{1,0:T(8,128)}), f32[128,128]{1,0:T(8,128)}) %reduce-scatter.9.cloned.1.call-update) | async-done | bytes 65552 | tf_op jit(solution)/shard_map/reduce_scatter | solution.py:315
  759.5 65.4 %reduce-scatter.7.cloned.1.call-done = f32[128,128]{1,0:T(8,128)} async-done(((f32[1024,128]{1,0:T(8,128)}), f32[128,128]{1,0:T(8,128)}) %reduce-scatter.7.cloned.1.call-update) | async-done | bytes 65552 | tf_op jit(solution)/shard_map/reduce_scatter | solution.py:314
  824.9 67.2 %reduce-scatter.11.cloned.1.call-done = f32[128,256]{1,0:T(8,128)} async-done(((f32[1024,256]{1,0:T(8,128)}), f32[128,256]{1,0:T(8,128)}) %reduce-scatter.11.cloned.1.call-update) | async-done | bytes 131088 | tf_op jit(solution)/shard_map/reduce_scatter | solution.py:316
  892.1 67.3 %reduce-scatter.5.cloned.1.call-done = f32[128,256]{1,0:T(8,128)} async-done(((f32[1024,256]{1,0:T(8,128)}), f32[128,256]{1,0:T(8,128)}) %reduce-scatter.5.cloned.1.call-update) | async-done | bytes 131088 | tf_op jit(solution)/shard_map/reduce_scatter | solution.py:313
  (198 shorter events, 64.6 us)
Async XLA Ops:
  7.2 399.8 %copy-start = (bf16[4,128,1024]{2,1,0:T(8,128)(2,1)S(1)}, bf16[4,128,1024]{2,1,0:T(8,128)(2,1)}, u32[]{:S(2)}) copy-start(bf16[4,128,1024]{2,1,0:T(8,128)(2,1)} %param.26) | copy-start | bytes 3145732
  7.2 125.0 %copy-start.32 = (bf16[128,256]{1,0:T(8,128)(2,1)S(1)}, bf16[128,256]{1,0:T(8,128)(2,1)}, u32[]{:S(2)}) copy-start(bf16[128,256]{1,0:T(8,128)(2,1)} %param.22) | copy-start | bytes 196612
  7.2 158.2 %copy-start.39 = (s32[128,8]{0,1:T(8,128)S(1)}, s32[128,8]{0,1:T(8,128)}, u32[]{:S(2)}) copy-start(s32[128,8]{0,1:T(8,128)} %param.16) | copy-start | bytes 12292
  7.2 190.2 %all-reduce.8.cloned.1.call-start = ((), (), s32[]{:S(2)}) async-start(), calls=%async_computation.8 | async-start | bytes 1048576 | tf_op jit(solution)/shard_map/psum | solution.py:171
  10.0 155.8 %copy-start.37 = (f32[128]{0:T(128)}, f32[128]{0:T(128)S(1)}, u32[]{:S(2)}) copy-start(f32[128]{0:T(128)S(1)} %add_rsqrt_fusion.1) | copy-start | bytes 1540
  32.5 131.1 %copy-start.23 = (f32[8,1,128]{2,1,0:T(1,128)}, f32[8,1,128]{2,1,0:T(1,128)S(1)}, u32[]{:S(2)}) copy-start(f32[8,1,128]{2,1,0:T(1,128)S(1)} %convert_element_type.196) | copy-start | bytes 12292
  63.5 32.5 %copy-start.17 = (bf16[1024,128]{1,0:T(8,128)(2,1)}, bf16[1024,128]{1,0:T(8,128)(2,1)S(1)}, u32[]{:S(2)}) copy-start(bf16[1024,128]{1,0:T(8,128)(2,1)S(1)} %all_gather.20) | copy-start | bytes 786436
  63.5 117.2 %copy-start.43 = (bf16[128]{0:T(256)(128)(2,1)S(1)}, bf16[128]{0:T(256)(128)(2,1)}, u32[]{:S(2)}) copy-start(bf16[128]{0:T(256)(128)(2,1)} %param.23) | copy-start | bytes 772
  94.6 102.8 %copy-start.1 = (bf16[128,1024]{1,0:T(8,128)(2,1)S(1)}, bf16[128,1024]{1,0:T(8,128)(2,1)}, u32[]{:S(2)}) copy-start(bf16[128,1024]{1,0:T(8,128)(2,1)} %param.14) | copy-start | bytes 786436
  97.3 68.3 %copy-start.29 = (bf16[128,128]{0,1:T(8,128)(2,1)}, bf16[128,128]{0,1:T(8,128)(2,1)S(1)}, u32[]{:S(2)}) copy-start(bf16[128,128]{0,1:T(8,128)(2,1)S(1)} %convolution_convert_fusion.2) | copy-start | bytes 98308
  131.3 34.3 %copy-start.33 = (bf16[128,2,32]{0,2,1:T(8,128)(2,1)}, bf16[128,2,32]{0,2,1:T(8,128)(2,1)S(1)}, u32[]{:S(2)}) copy-start(bf16[128,2,32]{0,2,1:T(8,128)(2,1)S(1)} %get-tuple-element.30) | copy-start | bytes 49156
  131.3 34.3 %copy-start.34 = (bf16[128,2,32]{0,2,1:T(8,128)(2,1)}, bf16[128,2,32]{0,2,1:T(8,128)(2,1)S(1)}, u32[]{:S(2)}) copy-start(bf16[128,2,32]{0,2,1:T(8,128)(2,1)S(1)} %get-tuple-element.31) | copy-start | bytes 49156
  213.0 96.8 %all-to-all-start = ((bf16[32,64,1024]{2,1,0:T(8,128)(2,1)}), bf16[32,64,1024]{2,1,0:T(8,128)(2,1)}, u32[]{:S(2)}, u32[]{:S(2)}) async-start(bf16[32,64,1024]{2,1,0:T(8,128)(2,1)} %broadcast_select_fusion), calls=%async_computation | async-start | bytes 8388608 | tf_op jit(solution)/shard_map/all_to_all | solution.py:193
  309.8 97.2 %all-to-all-start.2 = ((bf16[32,64,1024]{2,1,0:T(8,128)(2,1)}), bf16[32,64,1024]{2,1,0:T(8,128)(2,1)}, u32[]{:S(2)}, u32[]{:S(2)}) async-start(bf16[32,64,1024]{2,1,0:T(8,128)(2,1)} %multiply_convert_fusion), calls=%async_computation.2 | async-start | bytes 8388608 | tf_op jit(solution)/shard_map/all_to_all | solution.py:224
  416.8 96.9 %all-to-all-start.3 = ((bf16[32,64,1024]{2,1,0:T(8,128)(2,1)}), bf16[32,64,1024]{2,1,0:T(8,128)(2,1)}, u32[]{:S(2)}, u32[]{:S(2)}) async-start(bf16[32,64,1024]{2,1,0:T(8,128)(2,1)} %bitcast.184), calls=%async_computation.3 | async-start | bytes 8388608 | tf_op jit(solution)/shard_map/all_to_all | solution.py:259
  513.8 97.2 %all-to-all-start.1 = ((bf16[32,64,1024]{2,1,0:T(8,128)(2,1)}), bf16[32,64,1024]{2,1,0:T(8,128)(2,1)}, u32[]{:S(2)}, u32[]{:S(2)}) async-start(bf16[32,64,1024]{2,1,0:T(8,128)(2,1)} %bitcast.183), calls=%async_computation.1 | async-start | bytes 8388608 | tf_op jit(solution)/shard_map/all_to_all | solution.py:210
  518.5 102.8 %all-reduce.12.cloned.1.call-start = ((), (), s32[]{:S(2)}) async-start(), calls=%async_computation.10 | async-start | bytes 1048576 | tf_op jit(solution)/shard_map/psum | solution.py:268
  529.5 122.8 %all-reduce.10.cloned.1.call-start = ((), (), s32[]{:S(2)}) async-start(), calls=%async_computation.9 | async-start | bytes 524288 | tf_op jit(solution)/shard_map/psum | solution.py:218
  621.2 34.9 %copy-start.7 = (f32[2,2,128,128]{2,3,1,0:T(8,128)S(1)}, f32[2,2,128,128]{2,3,1,0:T(8,128)}, u32[]{:S(2)}) copy-start(f32[2,2,128,128]{2,3,1,0:T(8,128)} %copy-done.6) | copy-start | bytes 786436
  621.2 34.9 %copy-start.36 = (f32[2,2,128]{2,1,0:T(2,128)S(1)}, f32[2,2,128]{2,1,0:T(2,128)}, u32[]{:S(2)}) copy-start(f32[2,2,128]{2,1,0:T(2,128)} %copy-done.35) | copy-start | bytes 6148
  621.2 35.0 %copy-start.30 = (bf16[128,128]{0,1:T(8,128)(2,1)S(1)}, bf16[128,128]{0,1:T(8,128)(2,1)}, u32[]{:S(2)}) copy-start(bf16[128,128]{0,1:T(8,128)(2,1)} %copy-done.29) | copy-start | bytes 98308
  621.2 35.3 %copy-start.26 = (bf16[128,4,32]{0,2,1:T(8,128)(2,1)S(1)}, bf16[128,4,32]{0,2,1:T(8,128)(2,1)}, u32[]{:S(2)}) copy-start(bf16[128,4,32]{0,2,1:T(8,128)(2,1)} %copy-done.25) | copy-start | bytes 98308
  621.2 35.3 %copy-start.28 = (bf16[128,4,32]{0,2,1:T(8,128)(2,1)S(1)}, bf16[128,4,32]{0,2,1:T(8,128)(2,1)}, u32[]{:S(2)}) copy-start(bf16[128,4,32]{0,2,1:T(8,128)(2,1)} %copy-done.27) | copy-start | bytes 98308
  621.2 36.4 %copy-start.22 = (f32[128,32]{0,1:T(8,128)S(1)}, f32[128,32]{0,1:T(8,128)}, u32[]{:S(2)}) copy-start(f32[128,32]{0,1:T(8,128)} %copy-done.21) | copy-start | bytes 49156
  621.2 36.4 %copy-start.4 = (bf16[1024,256]{1,0:T(8,128)(2,1)S(1)}, bf16[1024,256]{1,0:T(8,128)(2,1)}, u32[]{:S(2)}) copy-start(bf16[1024,256]{1,0:T(8,128)(2,1)} %copy-done.3) | copy-start | bytes 1572868
  621.2 36.8 %copy-start.18 = (bf16[1024,128]{1,0:T(8,128)(2,1)S(1)}, bf16[1024,128]{1,0:T(8,128)(2,1)}, u32[]{:S(2)}) copy-start(bf16[1024,128]{1,0:T(8,128)(2,1)} %copy-done.17) | copy-start | bytes 786436
  621.2 71.6 %all-reduce.14.cloned.1.call-start = ((), (), s32[]{:S(2)}) async-start(), calls=%async_computation.11 | async-start | bytes 1048576 | tf_op jit(solution)/shard_map/psum | solution.py:301
  622.8 35.4 %copy-start.16 = (bf16[1024,128]{1,0:T(8,128)(2,1)S(1)}, bf16[1024,128]{1,0:T(8,128)(2,1)}, u32[]{:S(2)}) copy-start(bf16[1024,128]{1,0:T(8,128)(2,1)} %copy-done.15) | copy-start | bytes 786436
  659.3 100.2 %reduce-scatter.9.cloned.1.call-start = ((), (), s32[]{:S(2)}) async-start(), calls=%async_computation.14 | async-start | bytes 589824 | tf_op jit(solution)/shard_map/reduce_scatter | solution.py:315
  660.5 164.3 %reduce-scatter.7.cloned.1.call-start = ((), (), s32[]{:S(2)}) async-start(), calls=%async_computation.13 | async-start | bytes 589824 | tf_op jit(solution)/shard_map/reduce_scatter | solution.py:314
  661.7 230.4 %reduce-scatter.11.cloned.1.call-start = ((), (), s32[]{:S(2)}) async-start(), calls=%async_computation.15 | async-start | bytes 1179648 | tf_op jit(solution)/shard_map/reduce_scatter | solution.py:316
  663.1 296.3 %reduce-scatter.5.cloned.1.call-start = ((), (), s32[]{:S(2)}) async-start(), calls=%async_computation.12 | async-start | bytes 1179648 | tf_op jit(solution)/shard_map/reduce_scatter | solution.py:313
  (25 other events, 223.8 us)
Sparse Core Ops, SparseCore 0:
  165.5 30.7 all-reduce.7
  529.6 34.3 all-reduce.11
  621.3 30.8 all-reduce.9
  659.4 33.3 all-reduce.13
  696.6 62.8 reduce-scatter.8
  763.2 61.5 reduce-scatter.6
  828.8 63.2 reduce-scatter.10
  896.1 63.3 reduce-scatter.4
where the time goes:
time: 968 us; the launch traced here: 966 us
  waiting for transfers between devices  603 us (62%)
  blocking collectives  186 us (19%)
  local copies, waits for them, and re-layouts  59.9 us (6%)
  matrix products  46.8 us (5%)
  other arithmetic  35.8 us (4%)
  starting transfers between devices  19.3 us (2%)
  between operations  15.6 us (2%)
    all_to_all x1, waiting for transfers between devices, body(): lax.all_to_all(grad_total.astype(jnp.bfloat16), 'ep', split_axis=0, conca...  88.7 us
    all_to_all x1, waiting for transfers between devices, body(): lax.all_to_all(grad_send, 'ep', split_axis=0, concat_axis=0, tiled=True)  83.2 us
    all_to_all x1, waiting for transfers between devices, body(): lax.all_to_all(expert_total.astype(jnp.bfloat16), 'ep', split_axis=0, con...  81.3 us
    all_to_all x1, waiting for transfers between devices, body(): lax.all_to_all(send, 'ep', split_axis=0, concat_axis=0, tiled=True)  67.4 us
    reduce_scatter x1, waiting for transfers between devices, body(): lax.psum_scatter(query_part, 'ep', scatter_dimension=0, tiled=True)  67.3 us
    reduce_scatter x1, waiting for transfers between devices, body(): lax.psum_scatter(out_part, 'ep', scatter_dimension=0, tiled=True)  67.2 us
    reduce_scatter x1, waiting for transfers between devices, body(): lax.psum_scatter(key_part, 'ep', scatter_dimension=0, tiled=True)  65.4 us
    reduce_scatter x1, waiting for transfers between devices, body(): lax.psum_scatter(value_part, 'ep', scatter_dimension=0, tiled=True)  40.4 us
  transfers between devices with their start and end apart: 12, of which 10 were waited for; matrix products, arithmetic and copies ran while one was open for 10% of the time, Pallas kernels for 0%

commit v1 on v0

v1 whole, which is shorter than its diff:
```python
import jax
import jax.numpy as jnp
from jax import lax
from jax.sharding import PartitionSpec as P

HEAD_SIZE = 64
NORM_EPSILON = 1e-06
ROPE_BASE = 10000.0
MASKED = -1e30
LANES = 128
SUBLANES = 16
bf16 = jnp.bfloat16
f32 = jnp.float32


def positions_and_mask(segment_row):
    count = segment_row.shape[0]
    index = jnp.arange(count, dtype=jnp.int32)
    same = segment_row[:, None] == segment_row[None, :]
    before = index[None, :] < index[:, None]
    position = jnp.sum((same & before).astype(jnp.int32), axis=1)
    allowed = same & (index[None, :] <= index[:, None])
    return (position, allowed)


def rope_tables(position):
    half = HEAD_SIZE // 2
    steps = jnp.arange(half, dtype=f32) * (2.0 / HEAD_SIZE)
    frequency = jnp.exp(-jnp.log(f32(ROPE_BASE)) * steps)
    angle = position.astype(f32)[:, None] * frequency[None, :]
    return (jnp.cos(angle)[:, None, :], jnp.sin(angle)[:, None, :])


def rotate(values, cosine, sine):
    half = values.shape[-1] // 2
    first = values[..., :half]
    second = values[..., half:]
    return jnp.concatenate(
        [first * cosine - second * sine, second * cosine + first * sine], axis=-1
    )


def rotate_back(values, cosine, sine):
    return rotate(values, cosine, -sine)


def rms_inverse(values):
    return lax.rsqrt(jnp.mean(values * values, axis=-1, keepdims=True) + NORM_EPSILON)


def rms_backward(values, inverse, gain, upstream):
    gain_term = jnp.sum(upstream * values * inverse, axis=0)
    inner = jnp.mean(values * gain * upstream, axis=-1, keepdims=True)
    input_term = inverse * (gain * upstream) - values * inverse * inverse * inverse * inner
    return (input_term, gain_term)


def exchange(blocks, axis):
    return lax.all_to_all(blocks, axis, split_axis=0, concat_axis=0, tiled=True)


def gather_blocks(value, axis):
    count = lax.axis_size(axis)
    return exchange(jnp.broadcast_to(value[None], (count,) + value.shape), axis)


def flip(value, axis, bit):
    count = lax.axis_size(axis)
    return lax.ppermute(value, axis, [(i, i ^ bit) for i in range(count)])


def bits_of(axis):
    count = lax.axis_size(axis)
    return [1 << i for i in range(count.bit_length() - 1)]


def gather_relative(value, axis):
    for bit in reversed(bits_of(axis)):
        value = jnp.stack([value, flip(value, axis, bit)])
    return value


def reduce_relative(value, axis):
    for bit in bits_of(axis):
        value = value[0] + flip(value[1].astype(bf16), axis, bit).astype(f32)
    return value


def split_pair(value):
    high = lax.reduce_precision(value, 8, 7)
    return (high.astype(bf16), (value - high).astype(bf16))


def pad_to(value, axis, size):
    widths = [(0, 0)] * value.ndim
    widths[axis] = (0, size - value.shape[axis])
    return jnp.pad(value, widths)


def body(
    tokens,
    segment_ids,
    route_ids,
    route_weights,
    attn_gain,
    query_weight,
    key_projection_matrix,
    value_projection_matrix,
    out_weight,
    ffn_gain,
    gate_weight,
    up_weight,
    down_weight,
    cotangent,
):
    n_ep = lax.axis_size("ep")
    n_tp = lax.axis_size("tp")
    tp_at = lax.axis_index("tp")
    rows, width = tokens.shape
    sub = rows // n_tp
    piece = width // n_ep
    local_experts, _, units = gate_weight.shape
    experts = local_experts * n_ep
    total = rows * n_ep
    scale = HEAD_SIZE ** (-0.5)
    q_cols = query_weight.shape[1]
    k_cols = key_projection_matrix.shape[1]

    def own_rows(value):
        return lax.dynamic_slice_in_dim(value, tp_at * sub, sub, 0)

    qkv_shard = jnp.concatenate([query_weight, key_projection_matrix, value_projection_matrix], 1)
    cols = qkv_shard.shape[1]
    gain_rows = pad_to(pad_to(jnp.stack([attn_gain, ffn_gain]), 1, cols), 0, SUBLANES)
    packed = gather_blocks(jnp.concatenate([qkv_shard, gain_rows], 0), "ep")
    qkv_full = packed[:, :piece].reshape(width, cols)
    gain_one = packed[:, piece, :piece].reshape(width).astype(f32)
    gain_two = packed[:, piece + 1, :piece].reshape(width).astype(f32)
    out_full = gather_blocks(out_weight, "ep").reshape(width, -1)

    expert_index = jnp.arange(experts, dtype=jnp.int32)
    own_ids = own_rows(route_ids)
    own_weights = own_rows(route_weights)
    dense = jnp.sum(
        jnp.where(own_ids[:, :, None] == expert_index, own_weights[:, :, None], 0.0), axis=1
    )
    dense = dense.reshape(sub, n_ep, local_experts).swapaxes(0, 1)
    dense_high, dense_low = split_pair(dense)
    dense_pack = pad_to(jnp.concatenate([dense_high, dense_low], -1), 2, LANES)
    cot_own = own_rows(cotangent)
    cot_pack = jnp.concatenate(
        [jnp.broadcast_to(cot_own[None], (n_ep, sub, width)), dense_pack], axis=-1
    )
    cot_all = gather_relative(exchange(cot_pack, "ep"), "tp").reshape(total, -1)
    weights_all = cot_all[:, width : width + local_experts].astype(f32) + cot_all[
        :, width + local_experts : width + 2 * local_experts
    ].astype(f32)
    cot_all = cot_all[:, :width]

    position, allowed = positions_and_mask(segment_ids[0])
    cosine, sine = rope_tables(position)
    tokens_float = tokens.astype(f32)
    inverse_one = rms_inverse(tokens_float)
    normed_one = (tokens_float * inverse_one * gain_one).astype(bf16)
    qkv = jnp.dot(normed_one, qkv_full, preferred_element_type=f32)
    query = qkv[:, :q_cols].reshape(rows, -1, HEAD_SIZE)
    keys = qkv[:, q_cols : q_cols + k_cols].reshape(rows, -1, HEAD_SIZE)
    query_rot = rotate(query, cosine, sine).astype(bf16)
    key_rot = rotate(keys, cosine, sine).astype(bf16)
    value_rows = qkv[:, q_cols + k_cols :].astype(bf16).reshape(rows, -1, HEAD_SIZE)
    grouped = query_rot.reshape(rows, key_rot.shape[1], -1, HEAD_SIZE)
    scores = jnp.einsum("thgd,uhd->hgtu", grouped, key_rot, preferred_element_type=f32) * scale
    scores = jnp.where(allowed, scores, MASKED)
    peak = jnp.max(scores, axis=-1, keepdims=True)
    logsum = peak + jnp.log(jnp.sum(jnp.exp(scores - peak), axis=-1, keepdims=True))
    probs = jnp.exp(scores - logsum)
    probs_low = probs.astype(bf16)
    attended = jnp.einsum(
        "hgtu,uhd->thgd", probs_low, value_rows, preferred_element_type=f32
    ).astype(bf16)
    attended_flat = attended.reshape(rows, -1)
    branch_part = jnp.einsum("tk,dk->td", attended_flat, out_full, preferred_element_type=f32)
    branch = exchange(branch_part.astype(bf16).reshape(n_tp, sub, width), "tp")
    branch = jnp.sum(branch.astype(f32), axis=0)
    tokens_own = own_rows(tokens).astype(f32)
    hidden_one = tokens_own + branch
    inverse_two = rms_inverse(hidden_one)
    normed_two = (hidden_one * inverse_two * gain_two).astype(bf16)

    rows_in = gather_relative(gather_blocks(normed_two, "ep"), "tp").reshape(total, width)
    gate_pre = jnp.einsum("td,edf->tef", rows_in, gate_weight, preferred_element_type=f32)
    up_pre = jnp.einsum("td,edf->tef", rows_in, up_weight, preferred_element_type=f32)
    sigma = jax.nn.sigmoid(gate_pre)
    active = gate_pre * sigma
    route = weights_all[:, :, None]
    hidden = (active * up_pre * route).astype(bf16)
    grad_hidden = (
        jnp.einsum("td,efd->tef", cot_all, down_weight, preferred_element_type=f32) * route
    )
    grad_gate = (grad_hidden * up_pre * sigma * (1.0 + gate_pre * (1.0 - sigma))).astype(bf16)
    grad_up = (grad_hidden * active).astype(bf16)
    grad_in = jnp.einsum("tef,edf->td", grad_gate, gate_weight, preferred_element_type=f32)
    grad_in = grad_in + jnp.einsum("tef,edf->td", grad_up, up_weight, preferred_element_type=f32)
    blocks = (2,) * (n_tp.bit_length() - 1) + (n_ep, sub, width)
    grad_part = reduce_relative(grad_in.reshape(blocks), "tp")
    grad_normed_two = jnp.sum(exchange(grad_part.astype(bf16), "ep").astype(f32), axis=0)

    moe = jnp.einsum("tef,efd->td", hidden, down_weight, preferred_element_type=f32)
    moe_part = reduce_relative(moe.reshape(blocks), "tp")
    moe_own = jnp.sum(exchange(moe_part.astype(bf16), "ep").astype(f32), axis=0)
    mixed = lax.all_gather((hidden_one + moe_own).astype(bf16), "tp", axis=0, tiled=True)
    down_grad = jnp.einsum("tef,td->efd", hidden, cot_all, preferred_element_type=f32)
    gate_grad = jnp.einsum("td,tef->edf", rows_in, grad_gate, preferred_element_type=f32)
    up_grad = jnp.einsum("td,tef->edf", rows_in, grad_up, preferred_element_type=f32)

    norm_term, ffn_gain_part = rms_backward(hidden_one, inverse_two, gain_two, grad_normed_two)
    grad_hidden_one = cot_own.astype(f32) + norm_term
    ffn_rows = pad_to(jnp.stack(split_pair(ffn_gain_part)), 0, SUBLANES)
    branch_rows = lax.all_gather(
        jnp.concatenate([grad_hidden_one.astype(bf16), ffn_rows], 0), "tp", axis=0
    )
    grad_branch = branch_rows[:, :sub].reshape(rows, width)
    ffn_gain_part = jnp.sum(branch_rows[:, sub : sub + 2].astype(f32), axis=(0, 1))

    grad_attended = (
        jnp.dot(grad_branch, out_full, preferred_element_type=f32)
        .astype(bf16)
        .reshape(attended.shape)
    )
    value_grad = jnp.einsum("hgtu,thgd->uhd", probs_low, grad_attended, preferred_element_type=f32)
    grad_probs = jnp.einsum("thgd,uhd->hgtu", grad_attended, value_rows, preferred_element_type=f32)
    delta = jnp.einsum("thgd,thgd->hgt", grad_attended, attended, preferred_element_type=f32)
    grad_scores = (probs * (grad_probs - delta[..., None]) * scale).astype(bf16)
    query_grad_rot = jnp.einsum("hgtu,uhd->thgd", grad_scores, key_rot, preferred_element_type=f32)
    key_grad_rot = jnp.einsum("hgtu,thgd->uhd", grad_scores, grouped, preferred_element_type=f32)
    query_back = rotate_back(query_grad_rot.reshape(rows, -1, HEAD_SIZE), cosine, sine)
    key_back = rotate_back(key_grad_rot, cosine, sine)
    qkv_grad = jnp.concatenate(
        [
            query_back.reshape(rows, -1).astype(bf16),
            key_back.reshape(rows, -1).astype(bf16),
            value_grad.reshape(rows, -1).astype(bf16),
        ],
        axis=1,
    )

    grad_normed_part = jnp.einsum("tk,dk->td", qkv_grad, qkv_full, preferred_element_type=f32)
    grad_normed_one = exchange(grad_normed_part.astype(bf16).reshape(n_tp, sub, width), "tp")
    grad_normed_one = jnp.sum(grad_normed_one.astype(f32), axis=0)
    input_term, attn_gain_part = rms_backward(
        tokens_own, own_rows(inverse_one), gain_one, grad_normed_one
    )
    attn_rows = pad_to(jnp.stack(split_pair(attn_gain_part)), 0, SUBLANES)
    last_rows = lax.all_gather(
        jnp.concatenate([(grad_hidden_one + input_term).astype(bf16), attn_rows], 0), "tp", axis=0
    )
    tokens_grad = last_rows[:, :sub].reshape(rows, width).astype(f32)
    attn_gain_part = jnp.sum(last_rows[:, sub : sub + 2].astype(f32), axis=(0, 1))
    attn_gain_grad = jnp.sum(exchange(attn_gain_part.reshape(n_ep, 1, piece), "ep"), axis=(0, 1))

    def by_piece(value):
        return value.reshape(rows, n_ep, piece).swapaxes(0, 1)

    early = exchange(
        jnp.concatenate(
            [
                jnp.broadcast_to(attended_flat[None], (n_ep,) + attended_flat.shape),
                by_piece(normed_one),
            ],
            axis=-1,
        ),
        "ep",
    ).reshape(total, -1)
    late = jnp.concatenate(
        [jnp.broadcast_to(qkv_grad[None], (n_ep,) + qkv_grad.shape), by_piece(grad_branch)], axis=-1
    )
    ffn_pair = jnp.stack(split_pair(ffn_gain_part)).reshape(2, n_ep, piece).swapaxes(0, 1)
    ffn_pair = pad_to(pad_to(ffn_pair, 2, late.shape[2]), 1, SUBLANES)
    late = exchange(jnp.concatenate([late, ffn_pair], axis=1), "ep")
    ffn_gain_grad = jnp.sum(late[:, rows : rows + 2, :piece].astype(f32), axis=(0, 1))
    late = late[:, :rows].reshape(total, -1)
    out_grad = jnp.einsum(
        "td,tk->dk", late[:, cols:], early[:, :q_cols], preferred_element_type=f32
    )
    qkv_weight_grad = jnp.einsum(
        "td,tk->dk", early[:, q_cols:], late[:, :cols], preferred_element_type=f32
    )
    return (
        mixed,
        tokens_grad,
        attn_gain_grad,
        qkv_weight_grad[:, :q_cols],
        qkv_weight_grad[:, q_cols : q_cols + k_cols],
        qkv_weight_grad[:, q_cols + k_cols :],
        out_grad,
        ffn_gain_grad,
        gate_grad,
        up_grad,
        down_grad,
    )


def solution(mesh):
    placed = (
        P("ep", None),
        P("ep", None),
        P("ep", None),
        P("ep", None),
        P("ep"),
        P("ep", "tp"),
        P("ep", "tp"),
        P("ep", "tp"),
        P("ep", "tp"),
        P("ep"),
        P("ep", None, "tp"),
        P("ep", None, "tp"),
        P("ep", "tp", None),
        P("ep", None),
    )
    return jax.shard_map(
        body,
        mesh=mesh,
        in_specs=placed,
        out_specs=(
            P("ep", None),
            P("ep", None),
            P("ep"),
            P("ep", "tp"),
            P("ep", "tp"),
            P("ep", "tp"),
            P("ep", "tp"),
            P("ep"),
            P("ep", None, "tp"),
            P("ep", None, "tp"),
            P("ep", "tp", None),
        ),
        check_vma=False,
    )
```

time: 968 us -> 310 us (0.32)
  waiting for transfers between devices: 603 us -> 142 us
  blocking collectives: 186 us -> 18.5 us
  starting transfers between devices: 19.3 us -> 56 us
  local copies, waits for them, and re-layouts: 59.9 us -> 27.7 us
  matrix products: 46.8 us -> 30.8 us
  between operations: 15.6 us -> 1.66 us
    reduce_scatter x4 -> x0, waiting for transfers between devices: 240 us -> none  [the longest x1 67.3 us: body(): lax.psum_scatter(query_part, 'ep', scatter_dimension=0, tiled=True)]
    all_to_all x4 -> x11, waiting for transfers between devices: 321 us -> 101 us  [exchange(): return lax.all_to_all(blocks, axis, split_axis=0, concat_axis=0, tiled=True)]
    all_gather x6 -> x3, blocking collectives: 164 us -> 18.5 us  [the longest x1 6.55 us: body(): lax.all_gather(jnp.concatenate([grad_hidden_one.astype(bf16), ffn_rows],...]
    gather x6 -> x0, local copies, waits for them, and re-layouts: 44.3 us -> none  [the longest x1 9.83 us: body(): grad_out[token_slot] * slot_weight[..., None]]
    psum x4 -> x0, waiting for transfers between devices: 41.8 us -> none  [the longest x1 29.4 us: body(): moe = lax.psum(moe_part.astype(jnp.bfloat16), 'tp').astype(jnp.float32)]
    ppermute x0 -> x8, waiting for transfers between devices: none -> 41 us  [flip(): return lax.ppermute(value, axis, [(i, i ^ bit) for i in range(count)])]
    all_to_all x4 -> x11, starting transfers between devices: 18.8 us -> 50 us  [exchange(): return lax.all_to_all(blocks, axis, split_axis=0, concat_axis=0, tiled=True)]
    unnamed x1 -> x0, blocking collectives: 21.7 us -> none
  transfers between devices with their start and end apart: 12 -> 19, of which waited for: 10 -> 14; matrix products, arithmetic and copies ran while one was open for 10% -> 20% of each run, Pallas kernels for 0% -> 0%
where the time goes in v1:
time: 310 us; the launch traced here: 308 us
  waiting for transfers between devices  142 us (46%)
  starting transfers between devices  56 us (18%)
  other arithmetic  31.7 us (10%)
  matrix products  30.8 us (10%)
  local copies, waits for them, and re-layouts  27.7 us (9%)
  blocking collectives  18.5 us (6%)
    all_to_all x11, waiting for transfers between devices, exchange(): return lax.all_to_all(blocks, axis, split_axis=0, concat_axis=0, tiled=True)  101 us
    all_to_all x11, starting transfers between devices, exchange(): return lax.all_to_all(blocks, axis, split_axis=0, concat_axis=0, tiled=True)  50 us
    ppermute x8, waiting for transfers between devices, flip(): return lax.ppermute(value, axis, [(i, i ^ bit) for i in range(count)])  41 us
    unnamed x105, local copies, waits for them, and re-layouts  12.5 us
    another operation x4, other arithmetic, gather_relative(): value = jnp.stack([value, flip(value, axis, bit)])  7.21 us
    all_gather x1, blocking collectives, body(): lax.all_gather(jnp.concatenate([grad_hidden_one.astype(bf16), ffn_rows],...  6.55 us
  transfers between devices with their start and end apart: 19, of which 14 were waited for; matrix products, arithmetic and copies ran while one was open for 20% of the time, Pallas kernels for 0%

profile of v1, /device:TPU:0, one launch (start us, length us, event | category | flops | bytes accessed | tf_op | source)
XLA Modules:
  0.0 308.2 jit_solution(16746384580877743601)
XLA Ops:
  3.5 7.4 %all-to-all-start = ((bf16[8,144,512]{2,1,0:T(8,128)(2,1)}), bf16[8,144,512]{2,1,0:T(8,128)(2,1)S(1)}, u32[]{:S(2)}, u32[]{:S(2)}) async-start(bf16[8,144,512]{2,1,0:T(8,128)(2,1)} %broadcast_in_dim.30), calls=%async_computation | async-start | bytes 2359296 | tf_op jit(solution)/shard_map/all_to_all | solution.py:59
  14.5 25.0 %all-to-all-done = bf16[8,144,512]{2,1,0:T(8,128)(2,1)S(1)} async-done(((bf16[8,144,512]{2,1,0:T(8,128)(2,1)}), bf16[8,144,512]{2,1,0:T(8,128)(2,1)S(1)}, u32[]{:S(2)}, u32[]{:S(2)}) %all-to-all-start) | async-done | bytes 1179680 | tf_op jit(solution)/shard_map/all_to_all | solution.py:59
  40.3 3.6 %all-to-all-start.1 = ((bf16[8,128,256]{2,1,0:T(8,128)(2,1)}), bf16[8,128,256]{2,1,0:T(8,128)(2,1)S(1)}, u32[]{:S(2)}, u32[]{:S(2)}) async-start(bf16[8,128,256]{2,1,0:T(8,128)(2,1)} %broadcast_in_dim.33), calls=%async_computation.1 | async-start | bytes 1048576 | tf_op jit(solution)/shard_map/all_to_all | solution.py:59
  45.9 12.7 %all-to-all-done.1 = bf16[8,128,256]{2,1,0:T(8,128)(2,1)S(1)} async-done(((bf16[8,128,256]{2,1,0:T(8,128)(2,1)}), bf16[8,128,256]{2,1,0:T(8,128)(2,1)S(1)}, u32[]{:S(2)}, u32[]{:S(2)}) %all-to-all-start.1) | async-done | bytes 524320 | tf_op jit(solution)/shard_map/all_to_all | solution.py:59
  58.6 3.6 %all-to-all-start.4 = ((bf16[8,32,1152]{2,1,0:T(8,128)(2,1)}), bf16[8,32,1152]{2,1,0:T(8,128)(2,1)S(1)}, u32[]{:S(2)}, u32[]{:S(2)}) async-start(bf16[8,32,1152]{2,1,0:T(8,128)(2,1)} %fusion.19), calls=%async_computation.4 | async-start | bytes 1179648 | tf_op jit(solution)/shard_map/all_to_all | solution.py:59
  63.8 14.5 %all-to-all-done.4 = bf16[8,32,1152]{2,1,0:T(8,128)(2,1)S(1)} async-done(((bf16[8,32,1152]{2,1,0:T(8,128)(2,1)}), bf16[8,32,1152]{2,1,0:T(8,128)(2,1)S(1)}, u32[]{:S(2)}, u32[]{:S(2)}) %all-to-all-start.4) | async-done | bytes 589856 | tf_op jit(solution)/shard_map/all_to_all | solution.py:59
  78.3 3.4 %all-to-all-start.2 = ((bf16[4,32,1024]{2,1,0:T(8,128)(2,1)}), bf16[4,32,1024]{2,1,0:T(8,128)(2,1)S(1)}, u32[]{:S(2)}, u32[]{:S(2)}) async-start(bf16[4,32,1024]{2,1,0:T(8,128)(2,1)} %bitcast.20), calls=%async_computation.2 | async-start | bytes 524288 | tf_op jit(solution)/shard_map/all_to_all | solution.py:59
  83.7 4.6 %all-to-all-done.2 = bf16[4,32,1024]{2,1,0:T(8,128)(2,1)S(1)} async-done(((bf16[4,32,1024]{2,1,0:T(8,128)(2,1)}), bf16[4,32,1024]{2,1,0:T(8,128)(2,1)S(1)}, u32[]{:S(2)}, u32[]{:S(2)}) %all-to-all-start.2) | async-done | bytes 262176 | tf_op jit(solution)/shard_map/all_to_all | solution.py:59
  89.5 3.6 %all-to-all-start.3 = ((bf16[8,32,1024]{2,1,0:T(8,128)(2,1)}), bf16[8,32,1024]{2,1,0:T(8,128)(2,1)S(1)}, u32[]{:S(2)}, u32[]{:S(2)}) async-start(bf16[8,32,1024]{2,1,0:T(8,128)(2,1)} %broadcast_in_dim.34), calls=%async_computation.3 | async-start | bytes 1048576 | tf_op jit(solution)/shard_map/all_to_all | solution.py:59
  93.1 7.4 %collective-permute-done.2 = bf16[8,32,1152]{2,1,0:T(8,128)(2,1)} collective-permute-done((bf16[8,32,1152]{2,1,0:T(8,128)(2,1)S(1)}, bf16[8,32,1152]{2,1,0:T(8,128)(2,1)}, u32[]{:S(2)}, u32[]{:S(2)}) %collective-permute-start.2) | collective-permute-done | bytes 589856 | tf_op jit(solution)/shard_map/ppermute | solution.py:69
  100.5 2.4 fusion.68
  102.9 3.9 %all-to-all-done.3 = bf16[8,32,1024]{2,1,0:T(8,128)(2,1)S(1)} async-done(((bf16[8,32,1024]{2,1,0:T(8,128)(2,1)}), bf16[8,32,1024]{2,1,0:T(8,128)(2,1)S(1)}, u32[]{:S(2)}, u32[]{:S(2)}) %all-to-all-start.3) | async-done | bytes 524320 | tf_op jit(solution)/shard_map/all_to_all | solution.py:59
  107.5 11.5 %collective-permute-done = bf16[8,32,1024]{2,1,0:T(8,128)(2,1)S(1)} collective-permute-done((bf16[8,32,1024]{2,1,0:T(8,128)(2,1)S(1)}, bf16[8,32,1024]{2,1,0:T(8,128)(2,1)S(1)}, u32[]{:S(2)}, u32[]{:S(2)}) %collective-permute-start) | collective-permute-done | bytes 524320 | tf_op jit(solution)/shard_map/ppermute | solution.py:69
  128.7 2.6 multiply_convert_fusion
  140.4 11.2 %collective-permute-done.7 = bf16[8,32,1024]{2,1,0:T(8,128)(2,1)S(1)} collective-permute-done((bf16[8,32,1024]{2,1,0:T(8,128)(2,1)S(1)}, bf16[8,32,1024]{2,1,0:T(8,128)(2,1)S(1)}, u32[]{:S(2)}, u32[]{:S(2)}) %collective-permute-start.7) | collective-permute-done | bytes 524320 | tf_op jit(solution)/shard_map/ppermute | solution.py:69
  152.6 4.4 %all-to-all-start.6 = ((bf16[8,32,1024]{2,1,0:T(8,128)(2,1)}), bf16[8,32,1024]{2,1,0:T(8,128)(2,1)S(1)}, u32[]{:S(2)}, u32[]{:S(2)}) async-start(bf16[8,32,1024]{2,1,0:T(8,128)(2,1)} %fusion.16), calls=%async_computation.6 | async-start | bytes 1048576 | tf_op jit(solution)/shard_map/all_to_all | solution.py:59
  161.2 10.2 %collective-permute-done.5 = bf16[8,32,1024]{2,1,0:T(8,128)(2,1)S(1)} collective-permute-done((bf16[8,32,1024]{2,1,0:T(8,128)(2,1)S(1)}, bf16[8,32,1024]{2,1,0:T(8,128)(2,1)S(1)}, u32[]{:S(2)}, u32[]{:S(2)}) %collective-permute-start.5) | collective-permute-done | bytes 524320 | tf_op jit(solution)/shard_map/ppermute | solution.py:69
  173.5 5.9 %all-to-all-start.5 = ((bf16[8,32,1024]{2,1,0:T(8,128)(2,1)}), bf16[8,32,1024]{2,1,0:T(8,128)(2,1)}, u32[]{:S(2)}, u32[]{:S(2)}) async-start(bf16[8,32,1024]{2,1,0:T(8,128)(2,1)} %fusion.18), calls=%async_computation.5 | async-start | bytes 1048576 | tf_op jit(solution)/shard_map/all_to_all | solution.py:59
  181.5 6.6 %all-gather = bf16[192,1024]{1,0:T(8,128)(2,1)S(1)} all-gather(bf16[48,1024]{1,0:T(8,128)(2,1)S(1)} %pad_maximum_fusion.6), channel_id=2, replica_groups=mesh['ep'=8,'tp'=4] {'tp'}, dimensions={0}, use_global_device_ids=true | all-gather | bytes 491520 | tf_op jit(solution)/shard_map/all_gather | solution.py:219
  203.9 3.5 %all-to-all-start.7 = ((bf16[4,32,1024]{2,1,0:T(8,128)(2,1)}), bf16[4,32,1024]{2,1,0:T(8,128)(2,1)S(1)}, u32[]{:S(2)}, u32[]{:S(2)}) async-start(bf16[4,32,1024]{2,1,0:T(8,128)(2,1)} %bitcast.207), calls=%async_computation.7 | async-start | bytes 524288 | tf_op jit(solution)/shard_map/all_to_all | solution.py:59
  216.0 6.1 %all-gather.1 = bf16[192,1024]{1,0:T(8,128)(2,1)S(1)} all-gather(bf16[48,1024]{1,0:T(8,128)(2,1)S(1)} %pad_maximum_fusion.7), channel_id=3, replica_groups=mesh['ep'=8,'tp'=4] {'tp'}, dimensions={0}, use_global_device_ids=true | all-gather | bytes 491520 | tf_op jit(solution)/shard_map/all_gather | solution.py:254
  222.8 6.0 %all-to-all-start.8 = ((f32[8,1,128]{2,1,0:T(1,128)}), f32[8,1,128]{2,1,0:T(1,128)S(1)}, u32[]{:S(2)}, u32[]{:S(2)}) async-start(f32[8,1,128]{2,1,0:T(1,128)} %bitcast.77), calls=%async_computation.8 | async-start | bytes 8192 | tf_op jit(solution)/shard_map/all_to_all | solution.py:59
  230.0 5.1 %all-to-all-done.8 = f32[8,1,128]{2,1,0:T(1,128)S(1)} async-done(((f32[8,1,128]{2,1,0:T(1,128)}), f32[8,1,128]{2,1,0:T(1,128)S(1)}, u32[]{:S(2)}, u32[]{:S(2)}) %all-to-all-start.8) | async-done | bytes 4128 | tf_op jit(solution)/shard_map/all_to_all | solution.py:59
  235.2 4.3 %all-to-all-start.10 = ((bf16[8,144,640]{2,1,0:T(8,128)(2,1)}), bf16[8,144,640]{2,1,0:T(8,128)(2,1)}, u32[]{:S(2)}, u32[]{:S(2)}) async-start(bf16[8,144,640]{2,1,0:T(8,128)(2,1)} %fusion.4), calls=%async_computation.10 | async-start | bytes 2949120 | tf_op jit(solution)/shard_map/all_to_all | solution.py:59
  240.9 32.9 %all-to-all-done.10 = bf16[8,144,640]{2,1,0:T(8,128)(2,1)} async-done(((bf16[8,144,640]{2,1,0:T(8,128)(2,1)}), bf16[8,144,640]{2,1,0:T(8,128)(2,1)}, u32[]{:S(2)}, u32[]{:S(2)}) %all-to-all-start.10) | async-done | bytes 1474592 | tf_op jit(solution)/shard_map/all_to_all | solution.py:59
  273.7 4.2 %all-to-all-start.9 = ((bf16[8,128,384]{2,1,0:T(8,128)(2,1)}), bf16[8,128,384]{2,1,0:T(8,128)(2,1)}, u32[]{:S(2)}, u32[]{:S(2)}) async-start(bf16[8,128,384]{2,1,0:T(8,128)(2,1)} %pad_maximum_fusion.4), calls=%async_computation.9 | async-start | bytes 1572864 | tf_op jit(solution)/shard_map/all_to_all | solution.py:59
  278.0 3.8 %convolution_bitcast_fusion.2 = f32[4,1024,128]{1,2,0:T(8,128)} fusion(bf16[1024,4,128]{2,0,1:T(8,128)(2,1)} %copy-done.22, bf16[1024,1024,1]{1,0,2:T(8,128)(2,1)S(1)} %bitcast.180), kind=kOutput, calls=%fused_computation.17 | convolution fusion | flops 1073741824 | bytes 5242880 | tf_op jit(solution)/shard_map/td,tef->edf/dot_general | solution.py:213
  281.8 3.0 copy.241
  284.7 2.6 convolution_bitcast_fusion.1
  287.3 3.0 copy.242
  290.4 2.6 fusion.2
  293.0 5.8 %all_gather.15 = bf16[128,1024]{1,0:T(8,128)(2,1)S(1)} all-gather(bf16[32,1024]{1,0:T(8,128)(2,1)S(1)} %copy-done.29), channel_id=1, replica_groups=mesh['ep'=8,'tp'=4] {'tp'}, dimensions={0}, use_global_device_ids=true | all-gather | bytes 327680 | tf_op jit(solution)/shard_map/all_gather | solution.py:211
  (235 shorter events, 79.1 us)
Async XLA Ops:
  0.6 127.6 %copy-start = (bf16[4,128,1024]{2,1,0:T(8,128)(2,1)S(1)}, bf16[4,128,1024]{2,1,0:T(8,128)(2,1)}, u32[]{:S(2)}) copy-start(bf16[4,128,1024]{2,1,0:T(8,128)(2,1)} %param.26) | copy-start | bytes 3145732
  3.5 36.0 %copy-start.36 = (bf16[128,256]{1,0:T(8,128)(2,1)S(1)}, bf16[128,256]{1,0:T(8,128)(2,1)}, u32[]{:S(2)}) copy-start(bf16[128,256]{1,0:T(8,128)(2,1)} %param.22) | copy-start | bytes 196612
  3.5 36.0 %all-to-all-start = ((bf16[8,144,512]{2,1,0:T(8,128)(2,1)}), bf16[8,144,512]{2,1,0:T(8,128)(2,1)S(1)}, u32[]{:S(2)}, u32[]{:S(2)}) async-start(bf16[8,144,512]{2,1,0:T(8,128)(2,1)} %broadcast_in_dim.30), calls=%async_computation | async-start | bytes 2359296 | tf_op jit(solution)/shard_map/all_to_all | solution.py:59
  12.7 32.0 %copy-start.43 = (f32[128]{0:T(128)}, f32[128]{0:T(128)S(1)}, u32[]{:S(2)}) copy-start(f32[128]{0:T(128)S(1)} %add_rsqrt_fusion.1) | copy-start | bytes 1540
  40.3 18.3 %all-to-all-start.1 = ((bf16[8,128,256]{2,1,0:T(8,128)(2,1)}), bf16[8,128,256]{2,1,0:T(8,128)(2,1)S(1)}, u32[]{:S(2)}, u32[]{:S(2)}) async-start(bf16[8,128,256]{2,1,0:T(8,128)(2,1)} %broadcast_in_dim.33), calls=%async_computation.1 | async-start | bytes 1048576 | tf_op jit(solution)/shard_map/all_to_all | solution.py:59
  45.7 42.6 %copy-start.28 = (bf16[128,128]{0,1:T(8,128)(2,1)}, bf16[128,128]{0,1:T(8,128)(2,1)S(1)}, u32[]{:S(2)}) copy-start(bf16[128,128]{0,1:T(8,128)(2,1)S(1)} %copy.217) | copy-start | bytes 98308
  45.8 42.5 %copy-start.37 = (bf16[128,2,32]{0,2,1:T(8,128)(2,1)}, bf16[128,2,32]{0,2,1:T(8,128)(2,1)S(1)}, u32[]{:S(2)}) copy-start(bf16[128,2,32]{0,2,1:T(8,128)(2,1)S(1)} %get-tuple-element.137) | copy-start | bytes 49156
  45.8 42.5 %copy-start.38 = (bf16[128,2,32]{0,2,1:T(8,128)(2,1)}, bf16[128,2,32]{0,2,1:T(8,128)(2,1)S(1)}, u32[]{:S(2)}) copy-start(bf16[128,2,32]{0,2,1:T(8,128)(2,1)S(1)} %get-tuple-element.138) | copy-start | bytes 49156
  45.8 16.7 %copy-start.31 = (bf16[128,4,32]{0,2,1:T(8,128)(2,1)}, bf16[128,4,32]{0,2,1:T(8,128)(2,1)S(1)}, u32[]{:S(2)}) copy-start(bf16[128,4,32]{0,2,1:T(8,128)(2,1)S(1)} %get-tuple-element.132) | copy-start | bytes 98308
  45.8 42.6 %copy-start.30 = (bf16[128,4,32]{0,2,1:T(8,128)(2,1)}, bf16[128,4,32]{0,2,1:T(8,128)(2,1)S(1)}, u32[]{:S(2)}) copy-start(bf16[128,4,32]{0,2,1:T(8,128)(2,1)S(1)} %get-tuple-element.131) | copy-start | bytes 98308
  45.9 42.7 %copy-start.34 = (f32[8,1,128]{2,1,0:T(1,128)S(1)}, f32[8,1,128]{2,1,0:T(1,128)}, u32[]{:S(2)}) copy-start(f32[8,1,128]{2,1,0:T(1,128)} %get-tuple-element.123) | copy-start | bytes 12292
  58.6 29.9 %copy-start.7 = (bf16[8,128,256]{2,1,0:T(8,128)(2,1)}, bf16[8,128,256]{2,1,0:T(8,128)(2,1)S(1)}, u32[]{:S(2)}) copy-start(bf16[8,128,256]{2,1,0:T(8,128)(2,1)S(1)} %all-to-all-done.1) | copy-start | bytes 1572868
  58.6 19.7 %all-to-all-start.4 = ((bf16[8,32,1152]{2,1,0:T(8,128)(2,1)}), bf16[8,32,1152]{2,1,0:T(8,128)(2,1)S(1)}, u32[]{:S(2)}, u32[]{:S(2)}) async-start(bf16[8,32,1152]{2,1,0:T(8,128)(2,1)} %fusion.19), calls=%async_computation.4 | async-start | bytes 1179648 | tf_op jit(solution)/shard_map/all_to_all | solution.py:59
  62.6 25.7 %copy-start.39 = (f32[2,2,128]{2,1,0:T(2,128)}, f32[2,2,128]{2,1,0:T(2,128)S(1)}, u32[]{:S(2)}) copy-start(f32[2,2,128]{2,1,0:T(2,128)S(1)} %log_add_fusion) | copy-start | bytes 6148
  62.8 40.1 %copy-start.23 = (bf16[2,64,2,128]{3,1,2,0:T(8,128)(2,1)}, bf16[2,64,2,128]{3,1,2,0:T(8,128)(2,1)S(1)}, u32[]{:S(2)}) copy-start(bf16[2,64,2,128]{3,1,2,0:T(8,128)(2,1)S(1)} %convolution_convert_fusion.3) | copy-start | bytes 196612
  78.3 22.1 %copy-start.12 = (bf16[8,32,1152]{2,1,0:T(8,128)(2,1)}, bf16[8,32,1152]{2,1,0:T(8,128)(2,1)S(1)}, u32[]{:S(2)}) copy-start(bf16[8,32,1152]{2,1,0:T(8,128)(2,1)S(1)} %all-to-all-done.4) | copy-start | bytes 1769476
  78.3 10.0 %all-to-all-start.2 = ((bf16[4,32,1024]{2,1,0:T(8,128)(2,1)}), bf16[4,32,1024]{2,1,0:T(8,128)(2,1)S(1)}, u32[]{:S(2)}, u32[]{:S(2)}) async-start(bf16[4,32,1024]{2,1,0:T(8,128)(2,1)} %bitcast.20), calls=%async_computation.2 | async-start | bytes 524288 | tf_op jit(solution)/shard_map/all_to_all | solution.py:59
  81.7 18.7 %collective-permute-start.2 = (bf16[8,32,1152]{2,1,0:T(8,128)(2,1)S(1)}, bf16[8,32,1152]{2,1,0:T(8,128)(2,1)}, u32[]{:S(2)}, u32[]{:S(2)}) collective-permute-start(bf16[8,32,1152]{2,1,0:T(8,128)(2,1)S(1)} %all-to-all-done.4), channel_id=1, source_target_pairs={{0,2},{1,3},{2,0},{3,1},{4,6},{5,7},{6,4},{7,5},{8,10},{9,11},{10,... | collective-permute-start | bytes 1769480 | tf_op jit(solution)/shard_map/ppermute | solution.py:69
  89.5 17.4 %all-to-all-start.3 = ((bf16[8,32,1024]{2,1,0:T(8,128)(2,1)}), bf16[8,32,1024]{2,1,0:T(8,128)(2,1)S(1)}, u32[]{:S(2)}, u32[]{:S(2)}) async-start(bf16[8,32,1024]{2,1,0:T(8,128)(2,1)} %broadcast_in_dim.34), calls=%async_computation.3 | async-start | bytes 1048576 | tf_op jit(solution)/shard_map/all_to_all | solution.py:59
  102.9 17.6 %collective-permute-start.3 = (bf16[2,8,32,1152]{3,2,1,0:T(8,128)(2,1)}, bf16[2,8,32,1152]{3,2,1,0:T(8,128)(2,1)}, u32[]{:S(2)}, u32[]{:S(2)}) collective-permute-start(bf16[2,8,32,1152]{3,2,1,0:T(8,128)(2,1)} %get-tuple-element.122), channel_id=1, source_target_pairs={{0,1},{1,0},{2,3},{3,2},{4,5},{5,4},{6,7},{7,6},{8,9},{9,8},{10,11... | collective-permute-start | bytes 3538952 | tf_op jit(solution)/shard_map/ppermute | solution.py:69
  106.8 12.2 %collective-permute-start = (bf16[8,32,1024]{2,1,0:T(8,128)(2,1)S(1)}, bf16[8,32,1024]{2,1,0:T(8,128)(2,1)S(1)}, u32[]{:S(2)}, u32[]{:S(2)}) collective-permute-start(bf16[8,32,1024]{2,1,0:T(8,128)(2,1)S(1)} %all-to-all-done.3), channel_id=1, source_target_pairs={{0,2},{1,3},{2,0},{3,1},{4,6},{5,7},{6,4},{7,5},{8,10},{9,11},{10,... | collective-permute-start | bytes 1572872 | tf_op jit(solution)/shard_map/ppermute | solution.py:69
  120.5 3.4 %collective-permute-start.1 = (bf16[2,8,32,1024]{3,2,1,0:T(8,128)(2,1)}, bf16[2,8,32,1024]{3,2,1,0:T(8,128)(2,1)}, u32[]{:S(2)}, u32[]{:S(2)}) collective-permute-start(bf16[2,8,32,1024]{3,2,1,0:T(8,128)(2,1)} %get-tuple-element.126), channel_id=1, source_target_pairs={{0,1},{1,0},{2,3},{3,2},{4,5},{5,4},{6,7},{7,6},{8,9},{9,8},{10,11... | collective-permute-start | bytes 3145736 | tf_op jit(solution)/shard_map/ppermute | solution.py:69
  134.1 2.9 collective-permute-start.6
  136.1 2.7 collective-permute-start.4
  137.4 14.3 %collective-permute-start.7 = (bf16[8,32,1024]{2,1,0:T(8,128)(2,1)S(1)}, bf16[8,32,1024]{2,1,0:T(8,128)(2,1)S(1)}, u32[]{:S(2)}, u32[]{:S(2)}) collective-permute-start(bf16[8,32,1024]{2,1,0:T(8,128)(2,1)S(1)} %fusion.24), channel_id=1, source_target_pairs={{0,2},{1,3},{2,0},{3,1},{4,6},{5,7},{6,4},{7,5},{8,10},{9,11},{10,... | collective-permute-start | bytes 1572872 | tf_op jit(solution)/shard_map/ppermute | solution.py:69
  152.6 21.0 %all-to-all-start.6 = ((bf16[8,32,1024]{2,1,0:T(8,128)(2,1)}), bf16[8,32,1024]{2,1,0:T(8,128)(2,1)S(1)}, u32[]{:S(2)}, u32[]{:S(2)}) async-start(bf16[8,32,1024]{2,1,0:T(8,128)(2,1)} %fusion.16), calls=%async_computation.6 | async-start | bytes 1048576 | tf_op jit(solution)/shard_map/all_to_all | solution.py:59
  158.3 13.1 %collective-permute-start.5 = (bf16[8,32,1024]{2,1,0:T(8,128)(2,1)S(1)}, bf16[8,32,1024]{2,1,0:T(8,128)(2,1)S(1)}, u32[]{:S(2)}, u32[]{:S(2)}) collective-permute-start(bf16[8,32,1024]{2,1,0:T(8,128)(2,1)S(1)} %fusion.23), channel_id=1, source_target_pairs={{0,2},{1,3},{2,0},{3,1},{4,6},{5,7},{6,4},{7,5},{8,10},{9,11},{10,... | collective-permute-start | bytes 1572872 | tf_op jit(solution)/shard_map/ppermute | solution.py:69
  173.5 30.3 %all-to-all-start.5 = ((bf16[8,32,1024]{2,1,0:T(8,128)(2,1)}), bf16[8,32,1024]{2,1,0:T(8,128)(2,1)}, u32[]{:S(2)}, u32[]{:S(2)}) async-start(bf16[8,32,1024]{2,1,0:T(8,128)(2,1)} %fusion.18), calls=%async_computation.5 | async-start | bytes 1048576 | tf_op jit(solution)/shard_map/all_to_all | solution.py:59
  203.9 9.5 %all-to-all-start.7 = ((bf16[4,32,1024]{2,1,0:T(8,128)(2,1)}), bf16[4,32,1024]{2,1,0:T(8,128)(2,1)S(1)}, u32[]{:S(2)}, u32[]{:S(2)}) async-start(bf16[4,32,1024]{2,1,0:T(8,128)(2,1)} %bitcast.207), calls=%async_computation.7 | async-start | bytes 524288 | tf_op jit(solution)/shard_map/all_to_all | solution.py:59
  222.8 12.4 %all-to-all-start.8 = ((f32[8,1,128]{2,1,0:T(1,128)}), f32[8,1,128]{2,1,0:T(1,128)S(1)}, u32[]{:S(2)}, u32[]{:S(2)}) async-start(f32[8,1,128]{2,1,0:T(1,128)} %bitcast.77), calls=%async_computation.8 | async-start | bytes 8192 | tf_op jit(solution)/shard_map/all_to_all | solution.py:59
  235.2 38.6 %all-to-all-start.10 = ((bf16[8,144,640]{2,1,0:T(8,128)(2,1)}), bf16[8,144,640]{2,1,0:T(8,128)(2,1)}, u32[]{:S(2)}, u32[]{:S(2)}) async-start(bf16[8,144,640]{2,1,0:T(8,128)(2,1)} %fusion.4), calls=%async_computation.10 | async-start | bytes 2949120 | tf_op jit(solution)/shard_map/all_to_all | solution.py:59
  273.7 28.0 %all-to-all-start.9 = ((bf16[8,128,384]{2,1,0:T(8,128)(2,1)}), bf16[8,128,384]{2,1,0:T(8,128)(2,1)}, u32[]{:S(2)}, u32[]{:S(2)}) async-start(bf16[8,128,384]{2,1,0:T(8,128)(2,1)} %pad_maximum_fusion.4), calls=%async_computation.9 | async-start | bytes 1572864 | tf_op jit(solution)/shard_map/all_to_all | solution.py:59
  (35 other events, 191.5 us)

commit v2 on v1

--- a/solution.py
+++ b/solution.py
@@ -86,6 +86,29 @@
     return value
 
 
+def reduce_own(value):
+    c_at = lax.axis_index("c")
+    y_at = lax.axis_index("y")
+    n_y = lax.axis_size("y")
+
+    def step(value, at, axis, bit):
+        kept = lax.dynamic_index_in_dim(value, at, 0, False)
+        sent = lax.dynamic_index_in_dim(value.astype(bf16), 1 - at, 0, False)
+        return kept + flip(sent, axis, bit).astype(f32)
+
+    rows, width = value.shape
+    value = value.reshape(n_y, 2, rows // (2 * n_y), width).swapaxes(0, 1)
+    value = step(value, c_at, "c", 1)
+    for bit in reversed(bits_of("y")):
+        value = value.reshape((2, bit) + value.shape[-2:])
+        value = step(value, (y_at // bit) % 2, "y", bit)
+    return value.reshape(value.shape[-2:])
+
+
+def after(value, *others):
+    return lax.optimization_barrier((value,) + others)[0]
+
+
 def split_pair(value):
     high = lax.reduce_precision(value, 8, 7)
     return (high.astype(bf16), (value - high).astype(bf16))
@@ -95,6 +118,10 @@
     widths = [(0, 0)] * value.ndim
     widths[axis] = (0, size - value.shape[axis])
     return jnp.pad(value, widths)
+
+
+EP = ("z", "x")
+TP = ("y", "c")
 
 
 def body(
@@ -113,13 +140,16 @@
     down_weight,
     cotangent,
 ):
-    n_ep = lax.axis_size("ep")
-    n_tp = lax.axis_size("tp")
-    tp_at = lax.axis_index("tp")
+    n_z = lax.axis_size("z")
+    n_ep = lax.axis_size(EP)
+    n_tp = lax.axis_size(TP)
+    tp_at = lax.axis_index(TP)
+    x_at = lax.axis_index("x")
     rows, width = tokens.shape
     sub = rows // n_tp
     piece = width // n_ep
-    local_experts, _, units = gate_weight.shape
+    half = width // 2
+    local_experts, _, _ = gate_weight.shape
     experts = local_experts * n_ep
     total = rows * n_ep
     scale = HEAD_SIZE ** (-0.5)
@@ -129,14 +159,46 @@
     def own_rows(value):
         return lax.dynamic_slice_in_dim(value, tp_at * sub, sub, 0)
 
-    qkv_shard = jnp.concatenate([query_weight, key_projection_matrix, value_projection_matrix], 1)
-    cols = qkv_shard.shape[1]
-    gain_rows = pad_to(pad_to(jnp.stack([attn_gain, ffn_gain]), 1, cols), 0, SUBLANES)
-    packed = gather_blocks(jnp.concatenate([qkv_shard, gain_rows], 0), "ep")
-    qkv_full = packed[:, :piece].reshape(width, cols)
-    gain_one = packed[:, piece, :piece].reshape(width).astype(f32)
-    gain_two = packed[:, piece + 1, :piece].reshape(width).astype(f32)
-    out_full = gather_blocks(out_weight, "ep").reshape(width, -1)
+    def features(value, at):
+        lead = value.shape[:-1]
+        value = value.reshape(lead + (n_z, 2, piece))
+        axis = len(lead) + 1
+        return lax.dynamic_index_in_dim(value, at, axis, False).reshape(lead + (half,))
+
+    def whole_features(own, other):
+        lead = own.shape[:-1]
+        own = own.reshape(lead + (n_z, 1, piece))
+        other = other.reshape(lead + (n_z, 1, piece))
+        first = jnp.where(x_at == 0, own, other)
+        second = jnp.where(x_at == 0, other, own)
+        return jnp.concatenate([first, second], axis=-2).reshape(lead + (width,))
+
+    shard = jnp.concatenate(
+        [query_weight, key_projection_matrix, value_projection_matrix, out_weight], 1
+    )
+    cols = q_cols + 2 * k_cols
+    out_cols = out_weight.shape[1]
+    gain_rows = jnp.pad(
+        jnp.stack([attn_gain, ffn_gain]), ((0, SUBLANES - 2), (cols, out_cols - piece))
+    )
+    packed = gather_blocks(jnp.concatenate([shard, gain_rows], 0), "z")
+    other_tokens = flip(tokens, "x", 1)
+    qkv_half = packed[:, :piece, :cols].reshape(half, cols)
+    gain_half = packed[:, piece, cols : cols + piece].reshape(half).astype(f32)
+    pair_tokens = jnp.concatenate([tokens, other_tokens], 0).astype(f32)
+    pair_inverse = rms_inverse(pair_tokens)
+    pair_normed = (features(pair_tokens, x_at) * pair_inverse * gain_half).astype(bf16)
+    qkv_part = jnp.dot(pair_normed, qkv_half, preferred_element_type=f32)
+    qkv = qkv_part[:rows] + flip(qkv_part[rows:].astype(bf16), "x", 1).astype(f32)
+
+    out_own = packed[:, :, cols:]
+    out_other = flip(out_own, "x", 1)
+    out_packed = jnp.where(
+        x_at == 0, jnp.stack([out_own, out_other], 1), jnp.stack([out_other, out_own], 1)
+    )
+    out_full = out_packed[:, :, :piece].reshape(width, out_cols)
+    gain_one = out_packed[:, :, piece, :piece].reshape(width).astype(f32)
+    gain_two = out_packed[:, :, piece + 1, :piece].reshape(width).astype(f32)
 
     expert_index = jnp.arange(experts, dtype=jnp.int32)
     own_ids = own_rows(route_ids)
@@ -151,18 +213,10 @@
     cot_pack = jnp.concatenate(
         [jnp.broadcast_to(cot_own[None], (n_ep, sub, width)), dense_pack], axis=-1
     )
-    cot_all = gather_relative(exchange(cot_pack, "ep"), "tp").reshape(total, -1)
-    weights_all = cot_all[:, width : width + local_experts].astype(f32) + cot_all[
-        :, width + local_experts : width + 2 * local_experts
-    ].astype(f32)
-    cot_all = cot_all[:, :width]
+    cot_ep = exchange(after(cot_pack, packed), EP)
 
     position, allowed = positions_and_mask(segment_ids[0])
     cosine, sine = rope_tables(position)
-    tokens_float = tokens.astype(f32)
-    inverse_one = rms_inverse(tokens_float)
-    normed_one = (tokens_float * inverse_one * gain_one).astype(bf16)
-    qkv = jnp.dot(normed_one, qkv_full, preferred_element_type=f32)
     query = qkv[:, :q_cols].reshape(rows, -1, HEAD_SIZE)
     keys = qkv[:, q_cols : q_cols + k_cols].reshape(rows, -1, HEAD_SIZE)
     query_rot = rotate(query, cosine, sine).astype(bf16)
@@ -180,14 +234,20 @@
     ).astype(bf16)
     attended_flat = attended.reshape(rows, -1)
     branch_part = jnp.einsum("tk,dk->td", attended_flat, out_full, preferred_element_type=f32)
-    branch = exchange(branch_part.astype(bf16).reshape(n_tp, sub, width), "tp")
-    branch = jnp.sum(branch.astype(f32), axis=0)
+    branch = reduce_own(branch_part)
     tokens_own = own_rows(tokens).astype(f32)
     hidden_one = tokens_own + branch
     inverse_two = rms_inverse(hidden_one)
     normed_two = (hidden_one * inverse_two * gain_two).astype(bf16)
 
-    rows_in = gather_relative(gather_blocks(normed_two, "ep"), "tp").reshape(total, width)
+    rows_ep = gather_blocks(normed_two, EP)
+    cot_all = gather_relative(gather_relative(after(cot_ep, normed_two), "y"), "c")
+    rows_in = gather_relative(gather_relative(rows_ep, "y"), "c").reshape(total, width)
+    cot_all = cot_all.reshape(total, -1)
+    weights_all = cot_all[:, width : width + local_experts].astype(f32) + cot_all[
+        :, width + local_experts : width + 2 * local_experts
+    ].astype(f32)
+    cot_all = cot_all[:, :width]
     gate_pre = jnp.einsum("td,edf->tef", rows_in, gate_weight, preferred_element_type=f32)
     up_pre = jnp.einsum("td,edf->tef", rows_in, up_weight, preferred_element_type=f32)
     sigma = jax.nn.sigmoid(gate_pre)
@@ -202,25 +262,45 @@
     grad_in = jnp.einsum("tef,edf->td", grad_gate, gate_weight, preferred_element_type=f32)
     grad_in = grad_in + jnp.einsum("tef,edf->td", grad_up, up_weight, preferred_element_type=f32)
     blocks = (2,) * (n_tp.bit_length() - 1) + (n_ep, sub, width)
-    grad_part = reduce_relative(grad_in.reshape(blocks), "tp")
-    grad_normed_two = jnp.sum(exchange(grad_part.astype(bf16), "ep").astype(f32), axis=0)
+    grad_c = reduce_relative(grad_in.reshape(blocks), "c")
+    grad_y = reduce_relative(grad_c, "y")
+    grad_ep = exchange(grad_y.astype(bf16), EP)
 
     moe = jnp.einsum("tef,efd->td", hidden, down_weight, preferred_element_type=f32)
-    moe_part = reduce_relative(moe.reshape(blocks), "tp")
-    moe_own = jnp.sum(exchange(moe_part.astype(bf16), "ep").astype(f32), axis=0)
-    mixed = lax.all_gather((hidden_one + moe_own).astype(bf16), "tp", axis=0, tiled=True)
+    moe_c = reduce_relative(after(moe, grad_c).reshape(blocks), "c")
+    moe_y = reduce_relative(after(moe_c, grad_y), "y")
     down_grad = jnp.einsum("tef,td->efd", hidden, cot_all, preferred_element_type=f32)
     gate_grad = jnp.einsum("td,tef->edf", rows_in, grad_gate, preferred_element_type=f32)
     up_grad = jnp.einsum("td,tef->edf", rows_in, grad_up, preferred_element_type=f32)
+    grad_ep, down_grad, gate_grad, up_grad, moe_y = lax.optimization_barrier(
+        (grad_ep, down_grad, gate_grad, up_grad, moe_y)
+    )
+    grad_normed_two = jnp.sum(grad_ep.astype(f32), axis=0)
 
     norm_term, ffn_gain_part = rms_backward(hidden_one, inverse_two, gain_two, grad_normed_two)
     grad_hidden_one = cot_own.astype(f32) + norm_term
     ffn_rows = pad_to(jnp.stack(split_pair(ffn_gain_part)), 0, SUBLANES)
     branch_rows = lax.all_gather(
-        jnp.concatenate([grad_hidden_one.astype(bf16), ffn_rows], 0), "tp", axis=0
+        jnp.concatenate([grad_hidden_one.astype(bf16), ffn_rows], 0), TP, axis=0
     )
     grad_branch = branch_rows[:, :sub].reshape(rows, width)
     ffn_gain_part = jnp.sum(branch_rows[:, sub : sub + 2].astype(f32), axis=(0, 1))
+
+    attended_other = flip(after(attended_flat, normed_two), "x", 1)
+    ffn_pair = pad_to(jnp.stack(split_pair(ffn_gain_part)), 0, SUBLANES)
+    branch_pack = jnp.concatenate([grad_branch, ffn_pair], 0)
+    branch_other = flip(features(branch_pack, 1 - x_at), "x", 1)
+    branch_half = features(branch_pack, x_at)
+    out_part = jnp.einsum(
+        "td,tk->dk",
+        jnp.concatenate([branch_half[:rows], branch_other[:rows]], 0),
+        jnp.concatenate([attended_flat, attended_other], 0),
+        preferred_element_type=f32,
+    )
+    ffn_half = jnp.sum(
+        branch_half[rows : rows + 2].astype(f32) + branch_other[rows : rows + 2].astype(f32), axis=0
+    )
+    ffn_half = jnp.stack(split_pair(ffn_half)).reshape(2, n_z, piece).swapaxes(0, 1)
 
     grad_attended = (
         jnp.dot(grad_branch, out_full, preferred_element_type=f32)
@@ -244,55 +324,54 @@
         axis=1,
     )
 
-    grad_normed_part = jnp.einsum("tk,dk->td", qkv_grad, qkv_full, preferred_element_type=f32)
-    grad_normed_one = exchange(grad_normed_part.astype(bf16).reshape(n_tp, sub, width), "tp")
-    grad_normed_one = jnp.sum(grad_normed_one.astype(f32), axis=0)
-    input_term, attn_gain_part = rms_backward(
-        tokens_own, own_rows(inverse_one), gain_one, grad_normed_one
-    )
-    attn_rows = pad_to(jnp.stack(split_pair(attn_gain_part)), 0, SUBLANES)
+    qkv_grad_other = flip(qkv_grad, "x", 1)
+    qkv_part = jnp.einsum(
+        "td,tk->dk",
+        pair_normed,
+        jnp.concatenate([qkv_grad, qkv_grad_other], 0),
+        preferred_element_type=f32,
+    )
+    grad_part = jnp.concatenate([qkv_part, out_part], 1).astype(bf16)
+    ffn_half = pad_to(pad_to(ffn_half, 2, cols + out_cols), 1, SUBLANES)
+    grad_blocks = exchange(
+        jnp.concatenate([grad_part.reshape(n_z, piece, cols + out_cols), ffn_half], 1), "z"
+    )
+    ffn_gain_grad = jnp.sum(grad_blocks[:, piece : piece + 2, :piece].astype(f32), axis=(0, 1))
+
+    def block_sum(start, size):
+        return jnp.sum(grad_blocks[:, :piece, start : start + size].astype(f32), axis=0)
+
+    qkv_other_half = flip(after(qkv_half, rows_ep), "x", 1)
+    normed_part = whole_features(
+        jnp.einsum("tk,dk->td", qkv_grad, qkv_half, preferred_element_type=f32),
+        jnp.einsum("tk,dk->td", qkv_grad, qkv_other_half, preferred_element_type=f32),
+    )
+    grad_normed_one = reduce_own(normed_part)
+    input_term = rms_backward(
+        tokens_own, own_rows(pair_inverse[:rows]), gain_one, grad_normed_one
+    )[0]
+    moe_ep = exchange(after(moe_y, grad_ep).astype(bf16), EP)
+    moe_own = jnp.sum(moe_ep.astype(f32), axis=0)
+    mixed_own = (hidden_one + moe_own).astype(bf16)
     last_rows = lax.all_gather(
-        jnp.concatenate([(grad_hidden_one + input_term).astype(bf16), attn_rows], 0), "tp", axis=0
+        jnp.concatenate([(grad_hidden_one + input_term).astype(bf16), mixed_own], 0),
+        TP,
+        axis=0,
     )
     tokens_grad = last_rows[:, :sub].reshape(rows, width).astype(f32)
-    attn_gain_part = jnp.sum(last_rows[:, sub : sub + 2].astype(f32), axis=(0, 1))
-    attn_gain_grad = jnp.sum(exchange(attn_gain_part.reshape(n_ep, 1, piece), "ep"), axis=(0, 1))
-
-    def by_piece(value):
-        return value.reshape(rows, n_ep, piece).swapaxes(0, 1)
-
-    early = exchange(
-        jnp.concatenate(
-            [
-                jnp.broadcast_to(attended_flat[None], (n_ep,) + attended_flat.shape),
-                by_piece(normed_one),
-            ],
-            axis=-1,
-        ),
-        "ep",
-    ).reshape(total, -1)
-    late = jnp.concatenate(
-        [jnp.broadcast_to(qkv_grad[None], (n_ep,) + qkv_grad.shape), by_piece(grad_branch)], axis=-1
-    )
-    ffn_pair = jnp.stack(split_pair(ffn_gain_part)).reshape(2, n_ep, piece).swapaxes(0, 1)
-    ffn_pair = pad_to(pad_to(ffn_pair, 2, late.shape[2]), 1, SUBLANES)
-    late = exchange(jnp.concatenate([late, ffn_pair], axis=1), "ep")
-    ffn_gain_grad = jnp.sum(late[:, rows : rows + 2, :piece].astype(f32), axis=(0, 1))
-    late = late[:, :rows].reshape(total, -1)
-    out_grad = jnp.einsum(
-        "td,tk->dk", late[:, cols:], early[:, :q_cols], preferred_element_type=f32
-    )
-    qkv_weight_grad = jnp.einsum(
-        "td,tk->dk", early[:, q_cols:], late[:, :cols], preferred_element_type=f32
-    )
+    mixed = last_rows[:, sub : 2 * sub].reshape(rows, width)
+
+    gain_part = jnp.sum(block_sum(0, cols) * shard[:, :cols].astype(f32), axis=1)
+    gain_part = (gain_part / attn_gain.astype(f32)).reshape(1, piece)
+    attn_gain_grad = jnp.sum(lax.all_gather(gain_part, TP, axis=0), axis=(0, 1))
     return (
         mixed,
         tokens_grad,
         attn_gain_grad,
-        qkv_weight_grad[:, :q_cols],
-        qkv_weight_grad[:, q_cols : q_cols + k_cols],
-        qkv_weight_grad[:, q_cols + k_cols :],
-        out_grad,
+        block_sum(0, q_cols),
+        block_sum(q_cols, k_cols),
+        block_sum(q_cols + k_cols, k_cols),
+        block_sum(cols, out_cols),
         ffn_gain_grad,
         gate_grad,
         up_grad,
@@ -301,38 +380,41 @@
 
 
 def solution(mesh):
-    placed = (
-        P("ep", None),
-        P("ep", None),
-        P("ep", None),
-        P("ep", None),
-        P("ep"),
-        P("ep", "tp"),
-        P("ep", "tp"),
-        P("ep", "tp"),
-        P("ep", "tp"),
-        P("ep"),
-        P("ep", None, "tp"),
-        P("ep", None, "tp"),
-        P("ep", "tp", None),
-        P("ep", None),
+    n_ep, n_tp = mesh.devices.shape
+    split = jax.sharding.Mesh(
+        mesh.devices.reshape(n_ep // 2, 2, n_tp // 2, 2), ("z", "x", "y", "c")
     )
     return jax.shard_map(
         body,
-        mesh=mesh,
-        in_specs=placed,
+        mesh=split,
+        in_specs=(
+            P(EP, None),
+            P(EP, None),
+            P(EP, None),
+            P(EP, None),
+            P(EP),
+            P(EP, TP),
+            P(EP, TP),
+            P(EP, TP),
+            P(EP, TP),
+            P(EP),
+            P(EP, None, TP),
+            P(EP, None, TP),
+            P(EP, TP, None),
+            P(EP, None),
+        ),
         out_specs=(
-            P("ep", None),
-            P("ep", None),
-            P("ep"),
-            P("ep", "tp"),
-            P("ep", "tp"),
-            P("ep", "tp"),
-            P("ep", "tp"),
-            P("ep"),
-            P("ep", None, "tp"),
-            P("ep", None, "tp"),
-            P("ep", "tp", None),
+            P(EP, None),
+            P(EP, None),
+            P(EP),
+            P(EP, TP),
+            P(EP, TP),
+            P(EP, TP),
+            P(EP, TP),
+            P(EP),
+            P(EP, None, TP),
+            P(EP, None, TP),
+            P(EP, TP, None),
         ),
         check_vma=False,
     )

time: 310 us -> 252 us (0.81)
  waiting for transfers between devices: 142 us -> 88.1 us
  local copies, waits for them, and re-layouts: 27.7 us -> 40.1 us
  starting transfers between devices: 56 us -> 44.1 us
  matrix products: 30.8 us -> 25.4 us
    all_to_all x11 -> x6, waiting for transfers between devices: 101 us -> 45.4 us  [exchange(): return lax.all_to_all(blocks, axis, split_axis=0, concat_axis=0, tiled=True)]
    all_to_all x11 -> x6, starting transfers between devices: 50 us -> 28 us  [exchange(): return lax.all_to_all(blocks, axis, split_axis=0, concat_axis=0, tiled=True)]
    ppermute x8 -> x19, starting transfers between devices: 5.94 us -> 16.1 us  [flip(): return lax.ppermute(value, axis, [(i, i ^ bit) for i in range(count)])]
    unnamed x105 -> x132, local copies, waits for them, and re-layouts: 12.5 us -> 18.7 us
    add x2 -> x4, other arithmetic: 2.02 us -> 5.92 us  [reduce_relative(): value = value[0] + flip(value[1].astype(bf16), axis, bit).astype(f32)]
    ppermute x8 -> x19, waiting for transfers between devices: 41 us -> 42.7 us  [flip(): return lax.ppermute(value, axis, [(i, i ^ bit) for i in range(count)])]
  transfers between devices with their start and end apart: 19 -> 25, of which waited for: 14 -> 11; matrix products, arithmetic and copies ran while one was open for 20% -> 29% of each run, Pallas kernels for 0% -> 0%
where the time goes in v2:
time: 252 us; the launch traced here: 250 us
  waiting for transfers between devices  88.1 us (35%)
  starting transfers between devices  44.1 us (18%)
  local copies, waits for them, and re-layouts  40.1 us (16%)
  other arithmetic  32.7 us (13%)
  matrix products  25.4 us (10%)
  blocking collectives  18.1 us (7%)
    all_to_all x6, waiting for transfers between devices, exchange(): return lax.all_to_all(blocks, axis, split_axis=0, concat_axis=0, tiled=True)  45.4 us
    ppermute x19, waiting for transfers between devices, flip(): return lax.ppermute(value, axis, [(i, i ^ bit) for i in range(count)])  42.7 us
    all_to_all x6, starting transfers between devices, exchange(): return lax.all_to_all(blocks, axis, split_axis=0, concat_axis=0, tiled=True)  28 us
    unnamed x132, local copies, waits for them, and re-layouts  18.7 us
    ppermute x19, starting transfers between devices, flip(): return lax.ppermute(value, axis, [(i, i ^ bit) for i in range(count)])  16.1 us
    all_gather x1, blocking collectives, body(): lax.all_gather(jnp.concatenate([(grad_hidden_one + input_term).astype(bf1...  6.85 us
    another operation x4, other arithmetic, gather_relative(): value = jnp.stack([value, flip(value, axis, bit)])  6.71 us
    all_gather x1, blocking collectives, body(): lax.all_gather(jnp.concatenate([grad_hidden_one.astype(bf16), ffn_rows],...  6.14 us
  transfers between devices with their start and end apart: 25, of which 11 were waited for; matrix products, arithmetic and copies ran while one was open for 29% of the time, Pallas kernels for 0%

profile of v2, /device:TPU:0, one launch (start us, length us, event | category | flops | bytes accessed | tf_op | source)
XLA Modules:
  0.0 250.4 jit_solution(12672890032645777485)
XLA Ops:
  1.9 3.0 %collective-permute-start = (bf16[128,1024]{0,1:T(8,128)(2,1)S(1)}, bf16[128,1024]{0,1:T(8,128)(2,1)S(1)}, u32[]{:S(2)}, u32[]{:S(2)}) collective-permute-start(bf16[128,1024]{0,1:T(8,128)(2,1)S(1)} %copy.199), channel_id=1, source_target_pairs={{0,4},{4,0},{1,5},{5,1},{2,6},{6,2},{3,7},{7,3},{8,12},{12,8},{9,1... | collective-permute-start | bytes 786440 | tf_op jit(solution)/shard_map/ppermute | solution.py:69
  7.5 4.9 %all-to-all-start = ((bf16[4,144,768]{2,1,0:T(8,128)(2,1)}), bf16[4,144,768]{2,1,0:T(8,128)(2,1)S(1)}, u32[]{:S(2)}, u32[]{:S(2)}) async-start(bf16[4,144,768]{2,1,0:T(8,128)(2,1)} %broadcast_in_dim.24), calls=%async_computation | async-start | bytes 1769472 | tf_op jit(solution)/shard_map/all_to_all | solution.py:59
  15.1 19.2 %all-to-all-done = bf16[4,144,768]{2,1,0:T(8,128)(2,1)S(1)} async-done(((bf16[4,144,768]{2,1,0:T(8,128)(2,1)}), bf16[4,144,768]{2,1,0:T(8,128)(2,1)S(1)}, u32[]{:S(2)}, u32[]{:S(2)}) %all-to-all-start) | async-done | bytes 884768 | tf_op jit(solution)/shard_map/all_to_all | solution.py:59
  38.6 4.2 %collective-permute-done.1 = bf16[128,512]{1,0:T(8,128)(2,1)S(1)} collective-permute-done((bf16[128,512]{1,0:T(8,128)(2,1)S(1)}, bf16[128,512]{1,0:T(8,128)(2,1)S(1)}, u32[]{:S(2)}, u32[]{:S(2)}) %collective-permute-start.1) | collective-permute-done | bytes 131104 | tf_op jit(solution)/shard_map/ppermute | solution.py:69
  49.6 3.5 %all-to-all-start.1 = ((bf16[8,32,1152]{2,1,0:T(8,128)(2,1)}), bf16[8,32,1152]{2,1,0:T(8,128)(2,1)S(1)}, u32[]{:S(2)}, u32[]{:S(2)}) async-start(bf16[8,32,1152]{2,1,0:T(8,128)(2,1)} %fusion.14), calls=%async_computation.1 | async-start | bytes 1179648 | tf_op jit(solution)/shard_map/all_to_all | solution.py:59
  55.4 2.4 collective-permute-done.4
  58.8 11.1 %all-to-all-done.1 = bf16[8,32,1152]{2,1,0:T(8,128)(2,1)S(1)} async-done(((bf16[8,32,1152]{2,1,0:T(8,128)(2,1)}), bf16[8,32,1152]{2,1,0:T(8,128)(2,1)S(1)}, u32[]{:S(2)}, u32[]{:S(2)}) %all-to-all-start.1) | async-done | bytes 589856 | tf_op jit(solution)/shard_map/all_to_all | solution.py:59
  72.3 3.7 %all-to-all-start.2 = ((bf16[8,32,1024]{2,1,0:T(8,128)(2,1)}), bf16[8,32,1024]{2,1,0:T(8,128)(2,1)S(1)}, u32[]{:S(2)}, u32[]{:S(2)}) async-start(bf16[8,32,1024]{2,1,0:T(8,128)(2,1)} %broadcast_in_dim.30), calls=%async_computation.2 | async-start | bytes 1048576 | tf_op jit(solution)/shard_map/all_to_all | solution.py:59
  76.0 8.8 %collective-permute-done.5 = bf16[8,32,1152]{2,1,0:T(8,128)(2,1)S(1)} collective-permute-done((bf16[8,32,1152]{2,1,0:T(8,128)(2,1)S(1)}, bf16[8,32,1152]{2,1,0:T(8,128)(2,1)S(1)}, u32[]{:S(2)}, u32[]{:S(2)}) %collective-permute-start.5) | collective-permute-done | bytes 589856 | tf_op jit(solution)/shard_map/ppermute | solution.py:69
  85.6 2.2 fusion.80
  87.9 2.5 all-to-all-done.2
  90.9 11.8 %collective-permute-done.7 = bf16[8,32,1024]{2,1,0:T(8,128)(2,1)S(1)} collective-permute-done((bf16[8,32,1024]{2,1,0:T(8,128)(2,1)S(1)}, bf16[8,32,1024]{2,1,0:T(8,128)(2,1)S(1)}, u32[]{:S(2)}, u32[]{:S(2)}) %collective-permute-start.7) | collective-permute-done | bytes 524320 | tf_op jit(solution)/shard_map/ppermute | solution.py:69
  110.8 2.6 %fusion.3 = f32[1024,4,128]{2,0,1:T(8,128)S(1)} fusion(bf16[4,128,1024]{2,1,0:T(8,128)(2,1)} %param.26, bf16[1024,1152]{1,0:T(8,128)(2,1)S(1)} %bitcast.219), kind=kOutput, calls=%fused_computation.19 | convolution fusion | flops 1073741824 | bytes 5242880 | tf_op jit(solution)/shard_map/td,efd->tef/dot_general | solution.py:258
  116.2 3.3 %multiply_convert_fusion = (bf16[1024,4,128]{2,0,1:T(8,128)(2,1)}, bf16[1024,4,128]{2,0,1:T(8,128)(2,1)S(1)}, bf16[1024,4,128]{2,0,1:T(8,128)(2,1)S(1)}) fusion(f32[1024,4]{0,1:T(4,128)S(1)} %convert_add_fusion.4, f32[1024,4,128]{2,0,1:T(8,128)S(1)} %fusion.87, f32[1024,4,128]{2,0,1:T(8,128)S(1)} %fusion.3, bf16[1024,1024,1]{1,0,2:T(8,128)(2,1)S(1)} %bitcast.214, ...), kind=kOutput, calls=%fused_computation.8 | convolution fusion | flops 1082654720 | bytes 10502144 | tf_op jit(solution)/shard_map/td,edf->tef/dot_general | solution.py:252
  122.2 1.9 copy-done.2
  130.2 1.7 convert_add_fusion.1
  137.2 2.6 %fusion.2 = f32[4,128,1024]{2,1,0:T(8,128)} fusion(bf16[1024,4,128]{2,0,1:T(8,128)(2,1)S(1)} %copy-done.16, bf16[1024,1152]{1,0:T(8,128)(2,1)S(1)} %bitcast.220), kind=kOutput, calls=%fused_computation.18 | convolution fusion | flops 1073741824 | bytes 5242880 | tf_op jit(solution)/shard_map/tef,td->efd/dot_general | solution.py:272
  141.2 6.4 %collective-permute-done.10 = bf16[8,32,1024]{2,1,0:T(8,128)(2,1)S(1)} collective-permute-done((bf16[8,32,1024]{2,1,0:T(8,128)(2,1)S(1)}, bf16[8,32,1024]{2,1,0:T(8,128)(2,1)S(1)}, u32[]{:S(2)}, u32[]{:S(2)}) %collective-permute-start.10) | collective-permute-done | bytes 524320 | tf_op jit(solution)/shard_map/ppermute | solution.py:69
  148.6 5.1 %all-to-all-start.3 = ((bf16[8,32,1024]{2,1,0:T(8,128)(2,1)}), bf16[8,32,1024]{2,1,0:T(8,128)(2,1)}, u32[]{:S(2)}, u32[]{:S(2)}) async-start(bf16[8,32,1024]{2,1,0:T(8,128)(2,1)} %fusion.12), calls=%async_computation.3 | async-start | bytes 1048576 | tf_op jit(solution)/shard_map/all_to_all | solution.py:59
  153.7 2.3 convert_add_fusion
  156.6 2.6 %convolution_bitcast_fusion.2 = f32[4,1024,128]{1,2,0:T(8,128)} fusion(bf16[1024,4,128]{2,0,1:T(8,128)(2,1)S(1)} %copy-done.20, bf16[1024,1024,1]{1,0,2:T(8,128)(2,1)S(1)} %bitcast.215), kind=kOutput, calls=%fused_computation.17 | convolution fusion | flops 1073741824 | bytes 5242880 | tf_op jit(solution)/shard_map/td,tef->edf/dot_general | solution.py:273
  159.3 2.6 %convolution_bitcast_fusion.1 = f32[4,1024,128]{1,2,0:T(8,128)} fusion(bf16[1024,4,128]{2,0,1:T(8,128)(2,1)S(1)} %copy-done.12, bf16[1024,1024,1]{1,0,2:T(8,128)(2,1)S(1)} %bitcast.216), kind=kOutput, calls=%fused_computation.16 | convolution fusion | flops 1073741824 | bytes 5242880 | tf_op jit(solution)/shard_map/td,tef->edf/dot_general | solution.py:274
  161.9 7.5 %collective-permute-done.12 = bf16[8,32,1024]{2,1,0:T(8,128)(2,1)S(1)} collective-permute-done((bf16[8,32,1024]{2,1,0:T(8,128)(2,1)S(1)}, bf16[8,32,1024]{2,1,0:T(8,128)(2,1)S(1)}, u32[]{:S(2)}, u32[]{:S(2)}) %collective-permute-start.12) | collective-permute-done | bytes 524320 | tf_op jit(solution)/shard_map/ppermute | solution.py:69
  172.8 6.1 %all-gather = bf16[192,1024]{1,0:T(8,128)(2,1)S(1)} all-gather(bf16[48,1024]{1,0:T(8,128)(2,1)S(1)} %pad_maximum_fusion.8), channel_id=2, replica_groups=mesh['z'=4,'x'=2,'y'=2,'c'=2] {'y','c'}, dimensions={0}, use_global_device_ids=true | all-gather | bytes 491520 | tf_op jit(solution)/shard_map/all_gather | solution.py:283
  181.8 5.7 %all-to-all-start.4 = ((bf16[8,32,1024]{2,1,0:T(8,128)(2,1)}), bf16[8,32,1024]{2,1,0:T(8,128)(2,1)S(1)}, u32[]{:S(2)}, u32[]{:S(2)}) async-start(bf16[8,32,1024]{2,1,0:T(8,128)(2,1)} %bitcast_add_fusion.1), calls=%async_computation.4 | async-start | bytes 1048576 | tf_op jit(solution)/shard_map/all_to_all | solution.py:59
  191.2 2.1 collective-permute-start.16
  203.2 1.8 copy.227
  205.0 2.9 %copy.228 = f32[4,1024,128]{2,1,0:T(8,128)} copy(f32[4,1024,128]{1,2,0:T(8,128)} %convolution_bitcast_fusion.1) | data formatting | bytes 4194304
  215.2 5.1 %all-to-all-start.5 = ((bf16[4,144,768]{2,1,0:T(8,128)(2,1)}), bf16[4,144,768]{2,1,0:T(8,128)(2,1)S(1)}, u32[]{:S(2)}, u32[]{:S(2)}) async-start(bf16[4,144,768]{2,1,0:T(8,128)(2,1)} %fusion.13), calls=%async_computation.5 | async-start | bytes 1769472 | tf_op jit(solution)/shard_map/all_to_all | solution.py:59
  221.5 6.9 %all-gather.1 = bf16[256,1024]{1,0:T(8,128)(2,1)S(1)} all-gather(bf16[64,1024]{1,0:T(8,128)(2,1)S(1)} %pad_maximum_fusion.7), channel_id=3, replica_groups=mesh['z'=4,'x'=2,'y'=2,'c'=2] {'y','c'}, dimensions={0}, use_global_device_ids=true | all-gather | bytes 655360 | tf_op jit(solution)/shard_map/all_gather | solution.py:356
  229.9 12.7 %all-to-all-done.5 = bf16[4,144,768]{2,1,0:T(8,128)(2,1)S(1)} async-done(((bf16[4,144,768]{2,1,0:T(8,128)(2,1)}), bf16[4,144,768]{2,1,0:T(8,128)(2,1)S(1)}, u32[]{:S(2)}, u32[]{:S(2)}) %all-to-all-start.5) | async-done | bytes 884768 | tf_op jit(solution)/shard_map/all_to_all | solution.py:59
  242.8 5.1 %all-gather.3 = f32[4,1,128]{2,1,0:T(1,128)S(1)} all-gather(f32[1,1,128]{2,1,0:T(1,128)S(1)} %fusion.70), channel_id=4, replica_groups=mesh['z'=4,'x'=2,'y'=2,'c'=2] {'y','c'}, dimensions={0}, use_global_device_ids=true | all-gather | bytes 2560 | tf_op jit(solution)/shard_map/all_gather | solution.py:366
  (300 shorter events, 84.1 us)
Async XLA Ops:
  0.6 115.6 %copy-start = (bf16[4,1024,128]{2,1,0:T(8,128)(2,1)S(1)}, bf16[4,1024,128]{2,1,0:T(8,128)(2,1)}, u32[]{:S(2)}) copy-start(bf16[4,1024,128]{2,1,0:T(8,128)(2,1)} %param.25) | copy-start | bytes 3145732
  1.9 13.0 %collective-permute-start = (bf16[128,1024]{0,1:T(8,128)(2,1)S(1)}, bf16[128,1024]{0,1:T(8,128)(2,1)S(1)}, u32[]{:S(2)}, u32[]{:S(2)}) collective-permute-start(bf16[128,1024]{0,1:T(8,128)(2,1)S(1)} %copy.199), channel_id=1, source_target_pairs={{0,4},{4,0},{1,5},{5,1},{2,6},{6,2},{3,7},{7,3},{8,12},{12,8},{9,1... | collective-permute-start | bytes 786440 | tf_op jit(solution)/shard_map/ppermute | solution.py:69
  7.5 26.8 %all-to-all-start = ((bf16[4,144,768]{2,1,0:T(8,128)(2,1)}), bf16[4,144,768]{2,1,0:T(8,128)(2,1)S(1)}, u32[]{:S(2)}, u32[]{:S(2)}) async-start(bf16[4,144,768]{2,1,0:T(8,128)(2,1)} %broadcast_in_dim.24), calls=%async_computation | async-start | bytes 1769472 | tf_op jit(solution)/shard_map/all_to_all | solution.py:59
  36.4 6.4 %collective-permute-start.1 = (bf16[128,512]{1,0:T(8,128)(2,1)S(1)}, bf16[128,512]{1,0:T(8,128)(2,1)S(1)}, u32[]{:S(2)}, u32[]{:S(2)}) collective-permute-start(bf16[128,512]{1,0:T(8,128)(2,1)S(1)} %slice.286), channel_id=1, source_target_pairs={{0,4},{4,0},{1,5},{5,1},{2,6},{6,2},{3,7},{7,3},{8,12},{12,8},{9,1... | collective-permute-start | bytes 393224 | tf_op jit(solution)/shard_map/ppermute | solution.py:69
  37.0 10.3 %collective-permute-start.2 = (bf16[4,144,256]{2,1,0:T(8,128)(2,1)S(1)}, bf16[4,144,256]{2,1,0:T(8,128)(2,1)S(1)}, u32[]{:S(2)}, u32[]{:S(2)}) collective-permute-start(bf16[4,144,256]{2,1,0:T(8,128)(2,1)S(1)} %get-tuple-element.132), channel_id=1, source_target_pairs={{0,4},{4,0},{1,5},{5,1},{2,6},{6,2},{3,7},{7,3},{8,12},{12,8},{9,1... | collective-permute-start | bytes 884744 | tf_op jit(solution)/shard_map/ppermute | solution.py:69
  48.6 4.6 %collective-permute-start.3 = (bf16[2,32,1024]{2,1,0:T(8,128)(2,1)S(1)}, bf16[2,32,1024]{2,1,0:T(8,128)(2,1)S(1)}, u32[]{:S(2)}, u32[]{:S(2)}) collective-permute-start(bf16[2,32,1024]{2,1,0:T(8,128)(2,1)S(1)} %fusion.39), channel_id=1, source_target_pairs={{0,1},{1,0},{2,3},{3,2},{4,5},{5,4},{6,7},{7,6},{8,9},{9,8},{10,11... | collective-permute-start | bytes 393224 | tf_op jit(solution)/shard_map/ppermute | solution.py:69
  49.6 20.3 %all-to-all-start.1 = ((bf16[8,32,1152]{2,1,0:T(8,128)(2,1)}), bf16[8,32,1152]{2,1,0:T(8,128)(2,1)S(1)}, u32[]{:S(2)}, u32[]{:S(2)}) async-start(bf16[8,32,1152]{2,1,0:T(8,128)(2,1)} %fusion.14), calls=%async_computation.1 | async-start | bytes 1179648 | tf_op jit(solution)/shard_map/all_to_all | solution.py:59
  53.2 4.6 %collective-permute-start.4 = (bf16[1,32,1024]{2,1,0:T(8,128)(2,1)S(1)}, bf16[1,32,1024]{2,1,0:T(8,128)(2,1)S(1)}, u32[]{:S(2)}, u32[]{:S(2)}) collective-permute-start(bf16[1,32,1024]{2,1,0:T(8,128)(2,1)S(1)} %dynamic-slice_convert_fusion.3), channel_id=1, source_target_pairs={{0,2},{2,0},{1,3},{3,1},{4,6},{6,4},{5,7},{7,5},{8,10},{10,8},{9,1... | collective-permute-start | bytes 196616 | tf_op jit(solution)/shard_map/ppermute | solution.py:69
  55.4 29.4 %copy-start.36 = (f32[4,2,1,128]{3,2,1,0:T(1,128)}, f32[4,2,1,128]{3,2,1,0:T(1,128)S(1)}, u32[]{:S(2)}) copy-start(f32[4,2,1,128]{3,2,1,0:T(1,128)S(1)} %get-tuple-element.134) | copy-start | bytes 12292
  58.7 26.1 %copy-start.50 = (f32[32]{0:T(128)}, f32[32]{0:T(128)S(1)}, u32[]{:S(2)}) copy-start(f32[32]{0:T(128)S(1)} %add_rsqrt_fusion.1) | copy-start | bytes 388
  69.9 14.9 %collective-permute-start.5 = (bf16[8,32,1152]{2,1,0:T(8,128)(2,1)S(1)}, bf16[8,32,1152]{2,1,0:T(8,128)(2,1)S(1)}, u32[]{:S(2)}, u32[]{:S(2)}) collective-permute-start(bf16[8,32,1152]{2,1,0:T(8,128)(2,1)S(1)} %all-to-all-done.1), channel_id=1, source_target_pairs={{0,2},{2,0},{1,3},{3,1},{4,6},{6,4},{5,7},{7,5},{8,10},{10,8},{9,1... | collective-permute-start | bytes 1769480 | tf_op jit(solution)/shard_map/ppermute | solution.py:69
  72.3 18.1 %all-to-all-start.2 = ((bf16[8,32,1024]{2,1,0:T(8,128)(2,1)}), bf16[8,32,1024]{2,1,0:T(8,128)(2,1)S(1)}, u32[]{:S(2)}, u32[]{:S(2)}) async-start(bf16[8,32,1024]{2,1,0:T(8,128)(2,1)} %broadcast_in_dim.30), calls=%async_computation.2 | async-start | bytes 1048576 | tf_op jit(solution)/shard_map/all_to_all | solution.py:59
  87.9 16.3 %collective-permute-start.6 = (bf16[2,8,32,1152]{3,2,1,0:T(8,128)(2,1)S(1)}, bf16[2,8,32,1152]{3,2,1,0:T(8,128)(2,1)}, u32[]{:S(2)}, u32[]{:S(2)}) collective-permute-start(bf16[2,8,32,1152]{3,2,1,0:T(8,128)(2,1)S(1)} %get-tuple-element.128), channel_id=1, source_target_pairs={{0,1},{1,0},{2,3},{3,2},{4,5},{5,4},{6,7},{7,6},{8,9},{9,8},{10,11... | collective-permute-start | bytes 3538952 | tf_op jit(solution)/shard_map/ppermute | solution.py:69
  90.4 12.3 %collective-permute-start.7 = (bf16[8,32,1024]{2,1,0:T(8,128)(2,1)S(1)}, bf16[8,32,1024]{2,1,0:T(8,128)(2,1)S(1)}, u32[]{:S(2)}, u32[]{:S(2)}) collective-permute-start(bf16[8,32,1024]{2,1,0:T(8,128)(2,1)S(1)} %all-to-all-done.2), channel_id=1, source_target_pairs={{0,2},{2,0},{1,3},{3,1},{4,6},{6,4},{5,7},{7,5},{8,10},{10,8},{9,1... | collective-permute-start | bytes 1572872 | tf_op jit(solution)/shard_map/ppermute | solution.py:69
  104.1 9.3 %collective-permute-start.8 = (bf16[2,8,32,1024]{3,2,1,0:T(8,128)(2,1)}, bf16[2,8,32,1024]{3,2,1,0:T(8,128)(2,1)}, u32[]{:S(2)}, u32[]{:S(2)}) collective-permute-start(bf16[2,8,32,1024]{3,2,1,0:T(8,128)(2,1)} %get-tuple-element.130), channel_id=1, source_target_pairs={{0,1},{1,0},{2,3},{3,2},{4,5},{5,4},{6,7},{7,6},{8,9},{9,8},{10,11... | collective-permute-start | bytes 3145736 | tf_op jit(solution)/shard_map/ppermute | solution.py:69
  125.3 3.9 %collective-permute-start.9 = (bf16[2,8,32,1024]{3,2,1,0:T(8,128)(2,1)}, bf16[2,8,32,1024]{3,2,1,0:T(8,128)(2,1)S(1)}, u32[]{:S(2)}, u32[]{:S(2)}) collective-permute-start(bf16[2,8,32,1024]{3,2,1,0:T(8,128)(2,1)} %bitcast.49), channel_id=1, source_target_pairs={{0,1},{1,0},{2,3},{3,2},{4,5},{5,4},{6,7},{7,6},{8,9},{9,8},{10,11... | collective-permute-start | bytes 3145736 | tf_op jit(solution)/shard_map/ppermute | solution.py:69
  133.1 20.6 %collective-permute-start.11 = (bf16[2,8,32,1024]{3,2,1,0:T(8,128)(2,1)}, bf16[2,8,32,1024]{3,2,1,0:T(8,128)(2,1)}, u32[]{:S(2)}, u32[]{:S(2)}) collective-permute-start(bf16[2,8,32,1024]{3,2,1,0:T(8,128)(2,1)} %bitcast.56), channel_id=1, source_target_pairs={{0,1},{1,0},{2,3},{3,2},{4,5},{5,4},{6,7},{7,6},{8,9},{9,8},{10,11... | collective-permute-start | bytes 3145736 | tf_op jit(solution)/shard_map/ppermute | solution.py:69
  133.2 14.4 %collective-permute-start.10 = (bf16[8,32,1024]{2,1,0:T(8,128)(2,1)S(1)}, bf16[8,32,1024]{2,1,0:T(8,128)(2,1)S(1)}, u32[]{:S(2)}, u32[]{:S(2)}) collective-permute-start(bf16[8,32,1024]{2,1,0:T(8,128)(2,1)S(1)} %fusion.15), channel_id=1, source_target_pairs={{0,2},{2,0},{1,3},{3,1},{4,6},{6,4},{5,7},{7,5},{8,10},{10,8},{9,1... | collective-permute-start | bytes 1572872 | tf_op jit(solution)/shard_map/ppermute | solution.py:69
  135.1 77.7 %collective-permute-start.18 = (bf16[128,256]{0,1:T(8,128)(2,1)}, bf16[128,256]{0,1:T(8,128)(2,1)}, u32[]{:S(2)}, u32[]{:S(2)}) collective-permute-start(bf16[128,256]{0,1:T(8,128)(2,1)} %bitcast.99), channel_id=1, source_target_pairs={{0,4},{4,0},{1,5},{5,1},{2,6},{6,2},{3,7},{7,3},{8,12},{12,8},{9,1... | collective-permute-start | bytes 196616 | tf_op jit(solution)/shard_map/ppermute | solution.py:69
  136.7 53.0 %collective-permute-start.13 = (bf16[512,512]{1,0:T(8,128)(2,1)S(1)}, bf16[512,512]{1,0:T(8,128)(2,1)}, u32[]{:S(2)}, u32[]{:S(2)}) collective-permute-start(bf16[512,512]{1,0:T(8,128)(2,1)S(1)} %bitcast.223), channel_id=1, source_target_pairs={{0,4},{4,0},{1,5},{5,1},{2,6},{6,2},{3,7},{7,3},{8,12},{12,8},{9,1... | collective-permute-start | bytes 1572872 | tf_op jit(solution)/shard_map/ppermute | solution.py:69
  148.6 21.9 %all-to-all-start.3 = ((bf16[8,32,1024]{2,1,0:T(8,128)(2,1)}), bf16[8,32,1024]{2,1,0:T(8,128)(2,1)}, u32[]{:S(2)}, u32[]{:S(2)}) async-start(bf16[8,32,1024]{2,1,0:T(8,128)(2,1)} %fusion.12), calls=%async_computation.3 | async-start | bytes 1048576 | tf_op jit(solution)/shard_map/all_to_all | solution.py:59
  156.1 13.4 %collective-permute-start.12 = (bf16[8,32,1024]{2,1,0:T(8,128)(2,1)S(1)}, bf16[8,32,1024]{2,1,0:T(8,128)(2,1)S(1)}, u32[]{:S(2)}, u32[]{:S(2)}) collective-permute-start(bf16[8,32,1024]{2,1,0:T(8,128)(2,1)S(1)} %fusion.16), channel_id=1, source_target_pairs={{0,2},{2,0},{1,3},{3,1},{4,6},{6,4},{5,7},{7,5},{8,10},{10,8},{9,1... | collective-permute-start | bytes 1572872 | tf_op jit(solution)/shard_map/ppermute | solution.py:69
  181.8 33.4 %all-to-all-start.4 = ((bf16[8,32,1024]{2,1,0:T(8,128)(2,1)}), bf16[8,32,1024]{2,1,0:T(8,128)(2,1)S(1)}, u32[]{:S(2)}, u32[]{:S(2)}) async-start(bf16[8,32,1024]{2,1,0:T(8,128)(2,1)} %bitcast_add_fusion.1), calls=%async_computation.4 | async-start | bytes 1048576 | tf_op jit(solution)/shard_map/all_to_all | solution.py:59
  191.2 18.7 %collective-permute-start.16 = (bf16[128,512]{1,0:T(8,128)(2,1)}, bf16[128,512]{1,0:T(8,128)(2,1)}, u32[]{:S(2)}, u32[]{:S(2)}) collective-permute-start(bf16[128,512]{1,0:T(8,128)(2,1)} %pad_maximum_fusion.6), channel_id=1, source_target_pairs={{0,4},{4,0},{1,5},{5,1},{2,6},{6,2},{3,7},{7,3},{8,12},{12,8},{9,1... | collective-permute-start | bytes 393224 | tf_op jit(solution)/shard_map/ppermute | solution.py:69
  196.7 11.2 %collective-permute-start.14 = (bf16[2,32,1024]{2,1,0:T(8,128)(2,1)}, bf16[2,32,1024]{2,1,0:T(8,128)(2,1)}, u32[]{:S(2)}, u32[]{:S(2)}) collective-permute-start(bf16[2,32,1024]{2,1,0:T(8,128)(2,1)} %fusion.40), channel_id=1, source_target_pairs={{0,1},{1,0},{2,3},{3,2},{4,5},{5,4},{6,7},{7,6},{8,9},{9,8},{10,11... | collective-permute-start | bytes 393224 | tf_op jit(solution)/shard_map/ppermute | solution.py:69
  203.1 8.0 %collective-permute-start.17 = (bf16[144,512]{1,0:T(8,128)(2,1)}, bf16[144,512]{1,0:T(8,128)(2,1)}, u32[]{:S(2)}, u32[]{:S(2)}) collective-permute-start(bf16[144,512]{1,0:T(8,128)(2,1)} %bitcast.212), channel_id=1, source_target_pairs={{0,4},{4,0},{1,5},{5,1},{2,6},{6,2},{3,7},{7,3},{8,12},{12,8},{9,1... | collective-permute-start | bytes 442376 | tf_op jit(solution)/shard_map/ppermute | solution.py:69
  208.9 6.1 %collective-permute-start.15 = (bf16[1,32,1024]{2,1,0:T(8,128)(2,1)S(1)}, bf16[1,32,1024]{2,1,0:T(8,128)(2,1)S(1)}, u32[]{:S(2)}, u32[]{:S(2)}) collective-permute-start(bf16[1,32,1024]{2,1,0:T(8,128)(2,1)S(1)} %dynamic-slice_convert_fusion.2), channel_id=1, source_target_pairs={{0,2},{2,0},{1,3},{3,1},{4,6},{6,4},{5,7},{7,5},{8,10},{10,8},{9,1... | collective-permute-start | bytes 196616 | tf_op jit(solution)/shard_map/ppermute | solution.py:69
  215.2 27.4 %all-to-all-start.5 = ((bf16[4,144,768]{2,1,0:T(8,128)(2,1)}), bf16[4,144,768]{2,1,0:T(8,128)(2,1)S(1)}, u32[]{:S(2)}, u32[]{:S(2)}) async-start(bf16[4,144,768]{2,1,0:T(8,128)(2,1)} %fusion.13), calls=%async_computation.5 | async-start | bytes 1769472 | tf_op jit(solution)/shard_map/all_to_all | solution.py:59
  220.4 22.3 %copy-start.27 = (bf16[128,256]{1,0:T(8,128)(2,1)S(1)}, bf16[128,256]{1,0:T(8,128)(2,1)}, u32[]{:S(2)}) copy-start(bf16[128,256]{1,0:T(8,128)(2,1)} %param.19) | copy-start | bytes 196612
  220.4 22.3 %copy-start.29 = (bf16[128,128]{1,0:T(8,128)(2,1)S(1)}, bf16[128,128]{1,0:T(8,128)(2,1)}, u32[]{:S(2)}) copy-start(bf16[128,128]{1,0:T(8,128)(2,1)} %param.21) | copy-start | bytes 98308
  220.4 22.3 %copy-start.30 = (bf16[128,128]{1,0:T(8,128)(2,1)S(1)}, bf16[128,128]{1,0:T(8,128)(2,1)}, u32[]{:S(2)}) copy-start(bf16[128,128]{1,0:T(8,128)(2,1)} %param.20) | copy-start | bytes 98308
  228.3 22.1 %copy-start.1 = (bf16[4,1024,128]{2,1,0:T(8,128)(2,1)S(1)}, bf16[4,1024,128]{2,1,0:T(8,128)(2,1)}, u32[]{:S(2)}) copy-start(bf16[4,1024,128]{2,1,0:T(8,128)(2,1)} %param.25) | copy-start | bytes 3145732
  (57 other events, 345.4 us)

commit v3 on v2

--- a/solution.py
+++ b/solution.py
@@ -1,6 +1,8 @@
 import jax
 import jax.numpy as jnp
 from jax import lax
+from jax.experimental import pallas as pl
+from jax.experimental.pallas import tpu as pltpu
 from jax.sharding import PartitionSpec as P
 
 HEAD_SIZE = 64
@@ -74,35 +76,149 @@
     return [1 << i for i in range(count.bit_length() - 1)]
 
 
-def gather_relative(value, axis):
+def contract(left, right, left_axis, right_axis):
+    return lax.dot_general(
+        left, right, (((left_axis,), (right_axis,)), ((), ())), preferred_element_type=f32
+    )
+
+
+def side_by_side(ref):
+    return jnp.concatenate([ref[i] for i in range(ref.shape[0])], axis=1)
+
+
+def expert_kernel(
+    x_a, x_b, c_a, c_b, gate, up, down,
+    grad_a, grad_b, moe_a, moe_b, hidden, grad_gate, grad_up,
+):
+    rows, width = x_a.shape
+    count, units, _ = down.shape
+    gate_all = side_by_side(gate)
+    up_all = side_by_side(up)
+    down_all = down[...].reshape(count * units, width)
+    for i, (x_ref, c_ref) in enumerate(((x_a, c_a), (x_b, c_b))):
+        part = pl.ds(i * rows, rows)
+        gate_pre = contract(x_ref[...], gate_all, 1, 0)
+        up_pre = contract(x_ref[...], up_all, 1, 0)
+        grad_hidden = contract(c_ref[:, :width], down_all, 1, 1)
+        pack = c_ref[:, width:].astype(f32)
+        weights = [
+            jnp.broadcast_to(pack[:, e : e + 1] + pack[:, count + e : count + e + 1], (rows, units))
+            for e in range(count)
+        ]
+        weight = jnp.concatenate(weights, axis=1)
+        grad_hidden = grad_hidden * weight
+        sigma = jax.nn.sigmoid(gate_pre)
+        active = gate_pre * sigma
+        low = (active * up_pre * weight).astype(bf16)
+        low_gate = (grad_hidden * up_pre * sigma * (1.0 + gate_pre * (1.0 - sigma))).astype(bf16)
+        low_up = (grad_hidden * active).astype(bf16)
+        hidden[part] = low
+        grad_gate[part] = low_gate
+        grad_up[part] = low_up
+        grad = contract(low_gate, gate_all, 1, 1) + contract(low_up, up_all, 1, 1)
+        moe = contract(low, down_all, 1, 0)
+        if i == 0:
+            grad_a[...] = grad
+            moe_a[...] = moe.astype(bf16)
+        else:
+            grad_b[...] = grad.astype(bf16)
+            moe_b[...] = moe.astype(bf16)
+
+
+def run_experts(x_a, x_b, c_a, c_b, gate, up, down):
+    rows, width = x_a.shape
+    count, _, units = gate.shape
+    whole = pl.BlockSpec(memory_space=pltpu.VMEM)
+    low = jax.ShapeDtypeStruct((rows, width), bf16)
+    held = jax.ShapeDtypeStruct((2 * rows, count * units), bf16)
+    return pl.pallas_call(
+        expert_kernel,
+        in_specs=[whole] * 7,
+        out_specs=[whole] * 7,
+        out_shape=[jax.ShapeDtypeStruct((rows, width), f32), low, low, low, held, held, held],
+    )(x_a, x_b, c_a, c_b, gate, up, down)
+
+
+def grads_kernel(*refs):
+    gate_out, up_out, down_out, turned = refs[-4:]
+    groups = (len(refs) - 4) // 7
+    x_refs, c_refs = refs[: 2 * groups], refs[2 * groups : 4 * groups]
+    hidden, grad_gate, grad_up = (refs[(4 + i) * groups : (5 + i) * groups] for i in range(3))
+    rows, width = x_refs[0].shape
+
+    @pl.when(pl.program_id(0) == 0)
+    def _():
+        for i, ref in enumerate(x_refs):
+            turned[:, i * rows : (i + 1) * rows] = ref[...].T
+
+    gate_sum = up_sum = down_sum = 0.0
+    for k in range(groups):
+        columns = turned[:, 2 * k * rows : 2 * (k + 1) * rows]
+        gate_sum = gate_sum + contract(columns, grad_gate[k][...], 1, 0)
+        up_sum = up_sum + contract(columns, grad_up[k][...], 1, 0)
+        for i in range(2):
+            low = hidden[k][i * rows : (i + 1) * rows]
+            down_sum = down_sum + contract(low, c_refs[2 * k + i][:, :width], 0, 0)
+    gate_out[0] = gate_sum
+    up_out[0] = up_sum
+    down_out[0] = down_sum
+
+
+def run_grads(x_parts, c_parts, hidden, grad_gate, grad_up, count):
+    rows, width = x_parts[0].shape
+    units = hidden[0].shape[1] // count
+    whole = pl.BlockSpec(memory_space=pltpu.VMEM)
+    tall = pl.BlockSpec((1, width, units), lambda e: (e, 0, 0))
+    wide = pl.BlockSpec((1, units, width), lambda e: (e, 0, 0))
+    per_expert = pl.BlockSpec((2 * rows, units), lambda e: (0, e))
+    parts = len(x_parts)
+    return pl.pallas_call(
+        grads_kernel,
+        grid=(count,),
+        in_specs=[whole] * (2 * parts) + [per_expert] * (3 * parts // 2),
+        out_specs=[tall, tall, wide],
+        out_shape=[
+            jax.ShapeDtypeStruct((count, width, units), f32),
+            jax.ShapeDtypeStruct((count, width, units), f32),
+            jax.ShapeDtypeStruct((count, units, width), f32),
+        ],
+        scratch_shapes=[pltpu.VMEM((width, parts * rows), bf16)],
+    )(*x_parts, *c_parts, *hidden, *grad_gate, *grad_up)
+
+
+def gather_offsets(value):
+    blocks = {0: value}
+    for bit in reversed(bits_of("y")):
+        blocks.update({k | bit: flip(v, "y", bit) for k, v in blocks.items()})
+    return blocks
+
+
+def reduce_offsets(blocks):
+    for bit in bits_of("y"):
+        for k in [k for k in blocks if k & bit]:
+            sent = flip(blocks.pop(k).astype(bf16), "y", bit)
+            blocks[k ^ bit] = blocks[k ^ bit] + sent.astype(f32)
+    return blocks[0]
+
+
+def reduce_axis(value, axis):
+    at = lax.axis_index(axis)
+    rest = value.shape[1:]
     for bit in reversed(bits_of(axis)):
-        value = jnp.stack([value, flip(value, axis, bit)])
-    return value
-
-
-def reduce_relative(value, axis):
-    for bit in bits_of(axis):
-        value = value[0] + flip(value[1].astype(bf16), axis, bit).astype(f32)
-    return value
+        side = (at // bit) % 2
+        value = value.reshape((2, bit) + rest)
+        sent = jnp.where(side == 0, value[1], value[0]).astype(bf16)
+        kept = jnp.where(side == 0, value[0], value[1])
+        received = flip(sent, axis, bit)
+        value = kept + received.astype(f32)
+    return value.reshape(rest)
 
 
 def reduce_own(value):
-    c_at = lax.axis_index("c")
-    y_at = lax.axis_index("y")
+    rows, width = value.shape
     n_y = lax.axis_size("y")
-
-    def step(value, at, axis, bit):
-        kept = lax.dynamic_index_in_dim(value, at, 0, False)
-        sent = lax.dynamic_index_in_dim(value.astype(bf16), 1 - at, 0, False)
-        return kept + flip(sent, axis, bit).astype(f32)
-
-    rows, width = value.shape
     value = value.reshape(n_y, 2, rows // (2 * n_y), width).swapaxes(0, 1)
-    value = step(value, c_at, "c", 1)
-    for bit in reversed(bits_of("y")):
-        value = value.reshape((2, bit) + value.shape[-2:])
-        value = step(value, (y_at // bit) % 2, "y", bit)
-    return value.reshape(value.shape[-2:])
+    return reduce_axis(reduce_axis(value, "c"), "y")
 
 
 def after(value, *others):
@@ -151,7 +267,6 @@
     half = width // 2
     local_experts, _, _ = gate_weight.shape
     experts = local_experts * n_ep
-    total = rows * n_ep
     scale = HEAD_SIZE ** (-0.5)
     q_cols = query_weight.shape[1]
     k_cols = key_projection_matrix.shape[1]
@@ -160,18 +275,20 @@
         return lax.dynamic_slice_in_dim(value, tp_at * sub, sub, 0)
 
     def features(value, at):
-        lead = value.shape[:-1]
-        value = value.reshape(lead + (n_z, 2, piece))
-        axis = len(lead) + 1
-        return lax.dynamic_index_in_dim(value, at, axis, False).reshape(lead + (half,))
+        pieces = []
+        for z in range(n_z):
+            first = value[..., 2 * z * piece : (2 * z + 1) * piece]
+            second = value[..., (2 * z + 1) * piece : (2 * z + 2) * piece]
+            pieces.append(jnp.where(at == 0, first, second))
+        return jnp.concatenate(pieces, axis=-1)
 
     def whole_features(own, other):
-        lead = own.shape[:-1]
-        own = own.reshape(lead + (n_z, 1, piece))
-        other = other.reshape(lead + (n_z, 1, piece))
-        first = jnp.where(x_at == 0, own, other)
-        second = jnp.where(x_at == 0, other, own)
-        return jnp.concatenate([first, second], axis=-2).reshape(lead + (width,))
+        pieces = []
+        for z in range(n_z):
+            mine = own[..., z * piece : (z + 1) * piece]
+            theirs = other[..., z * piece : (z + 1) * piece]
+            pieces += [jnp.where(x_at == 0, mine, theirs), jnp.where(x_at == 0, theirs, mine)]
+        return jnp.concatenate(pieces, axis=-1)
 
     shard = jnp.concatenate(
         [query_weight, key_projection_matrix, value_projection_matrix, out_weight], 1
@@ -208,12 +325,22 @@
     )
     dense = dense.reshape(sub, n_ep, local_experts).swapaxes(0, 1)
     dense_high, dense_low = split_pair(dense)
-    dense_pack = pad_to(jnp.concatenate([dense_high, dense_low], -1), 2, LANES)
+    dense_pack = jnp.concatenate([dense_high, dense_low], -1)
+    dense_pack = dense_pack.reshape(n_z, 2, sub, 2 * local_experts)
+    dense_pack = pad_to(jnp.concatenate([dense_pack[:, 0], dense_pack[:, 1]], -1), 2, LANES)
     cot_own = own_rows(cotangent)
     cot_pack = jnp.concatenate(
-        [jnp.broadcast_to(cot_own[None], (n_ep, sub, width)), dense_pack], axis=-1
-    )
-    cot_ep = exchange(after(cot_pack, packed), EP)
+        [jnp.broadcast_to(cot_own[None], (n_z, sub, width)), dense_pack], axis=-1
+    )
+    cot_z = exchange(after(cot_pack, packed), "z")
+    cot_x = flip(cot_z, "x", 1)
+    cot_ep = jnp.where(x_at == 0, jnp.stack([cot_z, cot_x], 1), jnp.stack([cot_x, cot_z], 1))
+    routed = cot_ep[..., width:]
+    routed = jnp.where(
+        x_at == 0, routed[..., : 2 * local_experts], routed[..., 2 * local_experts : 4 * local_experts]
+    )
+    cot_ep = jnp.concatenate([cot_ep[..., :width], pad_to(routed, 3, LANES)], axis=-1)
+    cot_ep = cot_ep.reshape(n_ep * sub, width + LANES)
 
     position, allowed = positions_and_mask(segment_ids[0])
     cosine, sine = rope_tables(position)
@@ -240,41 +367,32 @@
     inverse_two = rms_inverse(hidden_one)
     normed_two = (hidden_one * inverse_two * gain_two).astype(bf16)
 
-    rows_ep = gather_blocks(normed_two, EP)
-    cot_all = gather_relative(gather_relative(after(cot_ep, normed_two), "y"), "c")
-    rows_in = gather_relative(gather_relative(rows_ep, "y"), "c").reshape(total, width)
-    cot_all = cot_all.reshape(total, -1)
-    weights_all = cot_all[:, width : width + local_experts].astype(f32) + cot_all[
-        :, width + local_experts : width + 2 * local_experts
-    ].astype(f32)
-    cot_all = cot_all[:, :width]
-    gate_pre = jnp.einsum("td,edf->tef", rows_in, gate_weight, preferred_element_type=f32)
-    up_pre = jnp.einsum("td,edf->tef", rows_in, up_weight, preferred_element_type=f32)
-    sigma = jax.nn.sigmoid(gate_pre)
-    active = gate_pre * sigma
-    route = weights_all[:, :, None]
-    hidden = (active * up_pre * route).astype(bf16)
-    grad_hidden = (
-        jnp.einsum("td,efd->tef", cot_all, down_weight, preferred_element_type=f32) * route
-    )
-    grad_gate = (grad_hidden * up_pre * sigma * (1.0 + gate_pre * (1.0 - sigma))).astype(bf16)
-    grad_up = (grad_hidden * active).astype(bf16)
-    grad_in = jnp.einsum("tef,edf->td", grad_gate, gate_weight, preferred_element_type=f32)
-    grad_in = grad_in + jnp.einsum("tef,edf->td", grad_up, up_weight, preferred_element_type=f32)
-    blocks = (2,) * (n_tp.bit_length() - 1) + (n_ep, sub, width)
-    grad_c = reduce_relative(grad_in.reshape(blocks), "c")
-    grad_y = reduce_relative(grad_c, "y")
-    grad_ep = exchange(grad_y.astype(bf16), EP)
-
-    moe = jnp.einsum("tef,efd->td", hidden, down_weight, preferred_element_type=f32)
-    moe_c = reduce_relative(after(moe, grad_c).reshape(blocks), "c")
-    moe_y = reduce_relative(after(moe_c, grad_y), "y")
-    down_grad = jnp.einsum("tef,td->efd", hidden, cot_all, preferred_element_type=f32)
-    gate_grad = jnp.einsum("td,tef->edf", rows_in, grad_gate, preferred_element_type=f32)
-    up_grad = jnp.einsum("td,tef->edf", rows_in, grad_up, preferred_element_type=f32)
-    grad_ep, down_grad, gate_grad, up_grad, moe_y = lax.optimization_barrier(
-        (grad_ep, down_grad, gate_grad, up_grad, moe_y)
-    )
+    rows_ep = gather_blocks(normed_two, EP).reshape(n_ep * sub, width)
+    cot_parts = gather_offsets(cot_ep)
+    row_parts = gather_offsets(rows_ep)
+    offsets = sorted(row_parts)
+    results = {}
+    for k in offsets:
+        cot_other = flip(cot_parts[k], "c", 1)
+        row_other = flip(row_parts[k], "c", 1)
+        parts = (row_parts[k], row_other, cot_parts[k], cot_other)
+        results[k] = parts + tuple(run_experts(*parts, gate_weight, up_weight, down_weight))
+    grad_c = {k: r[4] + flip(r[5], "c", 1).astype(f32) for k, r in results.items()}
+    grad_c[0] = lax.optimization_barrier(grad_c[0])
+    grad_y = reduce_offsets(dict(grad_c)).astype(bf16)
+    moe_c = {k: r[6].astype(f32) + flip(r[7], "c", 1).astype(f32) for k, r in results.items()}
+    moe_y = reduce_offsets(moe_c).astype(bf16).reshape(n_ep, sub, width)
+    ordered_results = [results[k] for k in offsets]
+    gate_grad, up_grad, down_grad = run_grads(
+        [part for r in ordered_results for part in r[:2]],
+        [part for r in ordered_results for part in r[2:4]],
+        *([r[i] for r in ordered_results] for i in (8, 9, 10)),
+        local_experts,
+    )
+    grad_y, gate_grad, up_grad, down_grad = lax.optimization_barrier(
+        (grad_y, gate_grad, up_grad, down_grad)
+    )
+    grad_ep = exchange(grad_y.reshape(n_ep, sub, width), EP)
     grad_normed_two = jnp.sum(grad_ep.astype(f32), axis=0)
 
     norm_term, ffn_gain_part = rms_backward(hidden_one, inverse_two, gain_two, grad_normed_two)
@@ -287,26 +405,17 @@
     ffn_gain_part = jnp.sum(branch_rows[:, sub : sub + 2].astype(f32), axis=(0, 1))
 
     attended_other = flip(after(attended_flat, normed_two), "x", 1)
-    ffn_pair = pad_to(jnp.stack(split_pair(ffn_gain_part)), 0, SUBLANES)
-    branch_pack = jnp.concatenate([grad_branch, ffn_pair], 0)
-    branch_other = flip(features(branch_pack, 1 - x_at), "x", 1)
-    branch_half = features(branch_pack, x_at)
+    branch_other = flip(features(grad_branch, 1 - x_at), "x", 1)
+    branch_half = features(grad_branch, x_at)
     out_part = jnp.einsum(
         "td,tk->dk",
-        jnp.concatenate([branch_half[:rows], branch_other[:rows]], 0),
+        jnp.concatenate([branch_half, branch_other], 0),
         jnp.concatenate([attended_flat, attended_other], 0),
         preferred_element_type=f32,
     )
-    ffn_half = jnp.sum(
-        branch_half[rows : rows + 2].astype(f32) + branch_other[rows : rows + 2].astype(f32), axis=0
-    )
-    ffn_half = jnp.stack(split_pair(ffn_half)).reshape(2, n_z, piece).swapaxes(0, 1)
-
-    grad_attended = (
-        jnp.dot(grad_branch, out_full, preferred_element_type=f32)
-        .astype(bf16)
-        .reshape(attended.shape)
-    )
+
+    grad_attended = jnp.dot(grad_branch, out_full, preferred_element_type=f32)
+    grad_attended = grad_attended.astype(bf16).reshape(attended.shape)
     value_grad = jnp.einsum("hgtu,thgd->uhd", probs_low, grad_attended, preferred_element_type=f32)
     grad_probs = jnp.einsum("thgd,uhd->hgtu", grad_attended, value_rows, preferred_element_type=f32)
     delta = jnp.einsum("thgd,thgd->hgt", grad_attended, attended, preferred_element_type=f32)
@@ -332,14 +441,10 @@
         preferred_element_type=f32,
     )
     grad_part = jnp.concatenate([qkv_part, out_part], 1).astype(bf16)
-    ffn_half = pad_to(pad_to(ffn_half, 2, cols + out_cols), 1, SUBLANES)
-    grad_blocks = exchange(
-        jnp.concatenate([grad_part.reshape(n_z, piece, cols + out_cols), ffn_half], 1), "z"
-    )
-    ffn_gain_grad = jnp.sum(grad_blocks[:, piece : piece + 2, :piece].astype(f32), axis=(0, 1))
+    grad_blocks = exchange(grad_part.reshape(n_z, piece, cols + out_cols), "z")
 
     def block_sum(start, size):
-        return jnp.sum(grad_blocks[:, :piece, start : start + size].astype(f32), axis=0)
+        return jnp.sum(grad_blocks[:, :, start : start + size].astype(f32), axis=0)
 
     qkv_other_half = flip(after(qkv_half, rows_ep), "x", 1)
     normed_part = whole_features(
@@ -347,23 +452,31 @@
         jnp.einsum("tk,dk->td", qkv_grad, qkv_other_half, preferred_element_type=f32),
     )
     grad_normed_one = reduce_own(normed_part)
-    input_term = rms_backward(
+    input_term, attn_gain_part = rms_backward(
         tokens_own, own_rows(pair_inverse[:rows]), gain_one, grad_normed_one
-    )[0]
-    moe_ep = exchange(after(moe_y, grad_ep).astype(bf16), EP)
+    )
+    attn_rows = pad_to(jnp.stack(split_pair(attn_gain_part)), 0, SUBLANES)
+    moe_ep = exchange(after(moe_y, grad_ep), EP)
     moe_own = jnp.sum(moe_ep.astype(f32), axis=0)
     mixed_own = (hidden_one + moe_own).astype(bf16)
     last_rows = lax.all_gather(
-        jnp.concatenate([(grad_hidden_one + input_term).astype(bf16), mixed_own], 0),
+        jnp.concatenate(
+            [(grad_hidden_one + input_term).astype(bf16), mixed_own, attn_rows], 0
+        ),
         TP,
         axis=0,
     )
     tokens_grad = last_rows[:, :sub].reshape(rows, width).astype(f32)
     mixed = last_rows[:, sub : 2 * sub].reshape(rows, width)
-
-    gain_part = jnp.sum(block_sum(0, cols) * shard[:, :cols].astype(f32), axis=1)
-    gain_part = (gain_part / attn_gain.astype(f32)).reshape(1, piece)
-    attn_gain_grad = jnp.sum(lax.all_gather(gain_part, TP, axis=0), axis=(0, 1))
+    gain_sum = jnp.sum(last_rows[:, 2 * sub : 2 * sub + 2].astype(f32), axis=(0, 1))
+    gain_sum = jnp.stack([gain_sum, ffn_gain_part]).reshape(2, -1, LANES)
+    gain_sum = gain_sum + flip(gain_sum, "x", 1)
+    for bit in bits_of("z"):
+        gain_sum = gain_sum + flip(gain_sum, "z", bit)
+    both_gains = lax.dynamic_slice_in_dim(
+        gain_sum.reshape(2, width), lax.axis_index(EP) * piece, piece, 1
+    )
+    attn_gain_grad, ffn_gain_grad = both_gains[0], both_gains[1]
     return (
         mixed,
         tokens_grad,

time: 252 us -> 223 us (0.88)
  local copies, waits for them, and re-layouts: 40.1 us -> 8.09 us
  Pallas kernels: 0 us -> 26 us
  matrix products: 25.4 us -> 4.18 us
  other arithmetic: 32.7 us -> 19.5 us
  starting transfers between devices: 44.1 us -> 55.1 us
  waiting for transfers between devices: 88.1 us -> 92.5 us
  blocking collectives: 18.1 us -> 14.3 us
    pallas_call x0 -> x3, Pallas kernels: none -> 26 us  [the longest x2 15.2 us: run_experts(): pl.pallas_call(expert_kernel, in_specs=[whole] * 7, out_specs=[whole] * 7...]
    dot_general x11 -> x2, matrix products: 20.2 us -> 1.34 us  [the longest x1 1.11 us: body(): jnp.einsum('td,tk->dk', jnp.concatenate([branch_half, branch_other], 0),...]
    ppermute x19 -> x27, waiting for transfers between devices: 42.7 us -> 60.3 us  [flip(): return lax.ppermute(value, axis, [(i, i ^ bit) for i in range(count)])]
    unnamed x132 -> x84, local copies, waits for them, and re-layouts: 18.7 us -> 2.2 us
    all_to_all x6, waiting for transfers between devices: 45.4 us -> 32.2 us  [exchange(): return lax.all_to_all(blocks, axis, split_axis=0, concat_axis=0, tiled=True)]
    ppermute x19 -> x27, starting transfers between devices: 16.1 us -> 27.6 us  [flip(): return lax.ppermute(value, axis, [(i, i ^ bit) for i in range(count)])]
    slice x10 -> x1, local copies, waits for them, and re-layouts: 8.53 us -> 0.05 us  [body(): cot_ep[..., :width]]
    add x7 -> x5, other arithmetic: 7.64 us -> 0.27 us  [the longest x1 0.18 us: body(): r[4] + flip(r[5], 'c', 1).astype(f32)]
  transfers between devices with their start and end apart: 25 -> 33, of which waited for: 11 -> 15; matrix products, arithmetic and copies ran while one was open for 29% -> 11% of each run, Pallas kernels for 0% -> 12%
where the time goes in v3:
time: 223 us; the launch traced here: 221 us
  waiting for transfers between devices  92.5 us (41%)
  starting transfers between devices  55.1 us (25%)
  Pallas kernels  26 us (12%)
  other arithmetic  19.5 us (9%)
  blocking collectives  14.3 us (6%)
  local copies, waits for them, and re-layouts  8.09 us (4%)
  matrix products  4.18 us (2%)
    ppermute x27, waiting for transfers between devices, flip(): return lax.ppermute(value, axis, [(i, i ^ bit) for i in range(count)])  60.3 us
    all_to_all x6, waiting for transfers between devices, exchange(): return lax.all_to_all(blocks, axis, split_axis=0, concat_axis=0, tiled=True)  32.2 us
    ppermute x27, starting transfers between devices, flip(): return lax.ppermute(value, axis, [(i, i ^ bit) for i in range(count)])  27.6 us
    all_to_all x6, starting transfers between devices, exchange(): return lax.all_to_all(blocks, axis, split_axis=0, concat_axis=0, tiled=True)  27.5 us
    pallas_call x2, Pallas kernels, run_experts(): pl.pallas_call(expert_kernel, in_specs=[whole] * 7, out_specs=[whole] * 7...  15.2 us
    pallas_call x1, Pallas kernels, run_grads(): pl.pallas_call(grads_kernel, grid=(count,), in_specs=[whole] * (2 * parts...  10.8 us
    all_gather x1, blocking collectives, body(): lax.all_gather(jnp.concatenate([(grad_hidden_one + input_term).astype(bf1...  7.57 us
    all_gather x1, blocking collectives, body(): lax.all_gather(jnp.concatenate([grad_hidden_one.astype(bf16), ffn_rows],...  6.71 us
  transfers between devices with their start and end apart: 33, of which 15 were waited for; matrix products, arithmetic and copies ran while one was open for 11% of the time, Pallas kernels for 12%

profile of v3, /device:TPU:0, one launch (start us, length us, event | category | flops | bytes accessed | tf_op | source)
XLA Modules:
  0.0 221.5 jit_solution(15050902560430092338)
XLA Ops:
  3.3 6.3 %all-to-all-start = ((bf16[4,144,768]{2,1,0:T(8,128)(2,1)}), bf16[4,144,768]{2,1,0:T(8,128)(2,1)S(1)}, u32[]{:S(2)}, u32[]{:S(2)}) async-start(bf16[4,144,768]{2,1,0:T(8,128)(2,1)} %broadcast_in_dim.24), calls=%async_computation | async-start | bytes 1769472 | tf_op jit(solution)/shard_map/all_to_all | solution.py:61
  13.1 4.3 %collective-permute-done = bf16[128,1024]{1,0:T(8,128)(2,1)S(1)} collective-permute-done((bf16[128,1024]{1,0:T(8,128)(2,1)S(1)}, bf16[128,1024]{1,0:T(8,128)(2,1)S(1)}, u32[]{:S(2)}, u32[]{:S(2)}) %collective-permute-start) | collective-permute-done | bytes 262176 | tf_op jit(solution)/shard_map/ppermute | solution.py:71
  17.9 14.0 %all-to-all-done = bf16[4,144,768]{2,1,0:T(8,128)(2,1)S(1)} async-done(((bf16[4,144,768]{2,1,0:T(8,128)(2,1)}), bf16[4,144,768]{2,1,0:T(8,128)(2,1)S(1)}, u32[]{:S(2)}, u32[]{:S(2)}) %all-to-all-start) | async-done | bytes 884768 | tf_op jit(solution)/shard_map/all_to_all | solution.py:61
  34.6 4.2 %collective-permute-done.1 = bf16[128,512]{1,0:T(8,128)(2,1)S(1)} collective-permute-done((bf16[128,512]{1,0:T(8,128)(2,1)S(1)}, bf16[128,512]{1,0:T(8,128)(2,1)S(1)}, u32[]{:S(2)}, u32[]{:S(2)}) %collective-permute-start.1) | collective-permute-done | bytes 131104 | tf_op jit(solution)/shard_map/ppermute | solution.py:71
  40.4 2.9 %collective-permute-done.2 = bf16[4,144,256]{2,1,0:T(8,128)(2,1)S(1)} collective-permute-done((bf16[4,144,256]{2,1,0:T(8,128)(2,1)S(1)}, bf16[4,144,256]{2,1,0:T(8,128)(2,1)S(1)}, u32[]{:S(2)}, u32[]{:S(2)}) %collective-permute-start.2) | collective-permute-done | bytes 294944 | tf_op jit(solution)/shard_map/ppermute | solution.py:71
  44.6 3.5 %all-to-all-start.2 = ((bf16[4,32,1152]{2,1,0:T(8,128)(2,1)}), bf16[4,32,1152]{2,1,0:T(8,128)(2,1)S(1)}, u32[]{:S(2)}, u32[]{:S(2)}) async-start(bf16[4,32,1152]{2,1,0:T(8,128)(2,1)} %fusion.12), calls=%async_computation.2 | async-start | bytes 589824 | tf_op jit(solution)/shard_map/all_to_all | solution.py:61
  48.1 1.6 collective-permute-start.4
  49.7 8.8 %all-to-all-done.2 = bf16[4,32,1152]{2,1,0:T(8,128)(2,1)S(1)} async-done(((bf16[4,32,1152]{2,1,0:T(8,128)(2,1)}), bf16[4,32,1152]{2,1,0:T(8,128)(2,1)S(1)}, u32[]{:S(2)}, u32[]{:S(2)}) %all-to-all-start.2) | async-done | bytes 294944 | tf_op jit(solution)/shard_map/all_to_all | solution.py:61
  61.1 3.7 %all-to-all-start.1 = ((bf16[8,32,1024]{2,1,0:T(8,128)(2,1)}), bf16[8,32,1024]{2,1,0:T(8,128)(2,1)S(1)}, u32[]{:S(2)}, u32[]{:S(2)}) async-start(bf16[8,32,1024]{2,1,0:T(8,128)(2,1)} %broadcast_in_dim.27), calls=%async_computation.1 | async-start | bytes 1048576 | tf_op jit(solution)/shard_map/all_to_all | solution.py:61
  64.8 2.7 %collective-permute-done.6 = bf16[4,32,1152]{2,1,0:T(8,128)(2,1)S(1)} collective-permute-done((bf16[4,32,1152]{2,1,0:T(8,128)(2,1)S(1)}, bf16[4,32,1152]{2,1,0:T(8,128)(2,1)S(1)}, u32[]{:S(2)}, u32[]{:S(2)}) %collective-permute-start.6) | collective-permute-done | bytes 294944 | tf_op jit(solution)/shard_map/ppermute | solution.py:71
  69.4 9.4 %all-to-all-done.1 = bf16[8,32,1024]{2,1,0:T(8,128)(2,1)S(1)} async-done(((bf16[8,32,1024]{2,1,0:T(8,128)(2,1)}), bf16[8,32,1024]{2,1,0:T(8,128)(2,1)S(1)}, u32[]{:S(2)}, u32[]{:S(2)}) %all-to-all-start.1) | async-done | bytes 524320 | tf_op jit(solution)/shard_map/all_to_all | solution.py:61
  80.3 2.7 %collective-permute-done.11.c_a.refs_6_ = bf16[256,1152]{1,0:T(8,128)(2,1)S(1)} collective-permute-done((bf16[256,1152]{1,0:T(8,128)(2,1)S(1)}, bf16[256,1152]{1,0:T(8,128)(2,1)S(1)}, u32[]{:S(2)}, u32[]{:S(2)}) %collective-permute-start.11) | collective-permute-done | bytes 589856 | tf_op jit(solution)/shard_map/ppermute | solution.py:71
  83.0 9.7 %collective-permute-done.9.x_a.refs_2_ = bf16[256,1024]{1,0:T(8,128)(2,1)S(1)} collective-permute-done((bf16[256,1024]{1,0:T(8,128)(2,1)S(1)}, bf16[256,1024]{1,0:T(8,128)(2,1)S(1)}, u32[]{:S(2)}, u32[]{:S(2)}) %collective-permute-start.9) | collective-permute-done | bytes 524320 | tf_op jit(solution)/shard_map/ppermute | solution.py:71
  94.7 7.6 %shard_map.222 = (f32[256,1024]{1,0:T(8,128)}, bf16[256,1024]{1,0:T(8,128)(2,1)}, bf16[256,1024]{1,0:T(8,128)(2,1)}, bf16[256,1024]{1,0:T(8,128)(2,1)}, bf16[512...) custom-call(bf16[256,1024]{1,0:T(8,128)(2,1)} %copy-done.7, ...), custom_call_target="tpu_custom_call" | custom-call | tf_op jit(solution)/shard_map/pallas_call | solution.py:134
  102.6 7.6 %shard_map.221 = (f32[256,1024]{1,0:T(8,128)}, bf16[256,1024]{1,0:T(8,128)(2,1)}, bf16[256,1024]{1,0:T(8,128)(2,1)}, bf16[256,1024]{1,0:T(8,128)(2,1)}, bf16[512...) custom-call(bf16[256,1024]{1,0:T(8,128)(2,1)} %bitcast.193, ...), custom_call_target="tpu_custom_call" | custom-call | tf_op jit(solution)/shard_map/pallas_call | solution.py:134
  110.5 2.0 add_convert_fusion.3
  114.7 10.8 %shard_map.223 = (f32[4,1024,128]{2,1,0:T(8,128)}, f32[4,1024,128]{2,1,0:T(8,128)}, f32[4,128,1024]{2,1,0:T(8,128)}) custom-call(bf16[256,1024]{1,0:T(8,128)(2,1)} %bitcast.194, bf16[256,1024]{1,0:T(8,128)(2,1)} %collective-permute-done.5.x_b.refs_1_, bf16[256,1024]{1,0:T(8,128)(2,1)} %copy-done.7, bf16[256,1024]{1,0:T(8,128)(2,1)} %collective-permute-done.10.x_b.refs_3_, ...), custom_call_target="tpu_custom_call" | custom-call | tf_op jit(solution)/shard_map/pallas_call | solution.py:175
  126.9 2.0 add_convert_fusion.2
  129.0 3.9 %all-to-all-start.3 = ((bf16[8,32,1024]{2,1,0:T(8,128)(2,1)}), bf16[8,32,1024]{2,1,0:T(8,128)(2,1)S(1)}, u32[]{:S(2)}, u32[]{:S(2)}) async-start(bf16[8,32,1024]{2,1,0:T(8,128)(2,1)} %bitcast.46), calls=%async_computation.3 | async-start | bytes 1048576 | tf_op jit(solution)/shard_map/all_to_all | solution.py:61
  137.1 2.0 collective-permute-start.26
  139.2 8.9 %collective-permute-done.20 = bf16[256,1024]{1,0:T(8,128)(2,1)} collective-permute-done((bf16[256,1024]{1,0:T(8,128)(2,1)S(1)}, bf16[256,1024]{1,0:T(8,128)(2,1)}, u32[]{:S(2)}, u32[]{:S(2)}) %collective-permute-start.20) | collective-permute-done | bytes 524320 | tf_op jit(solution)/shard_map/ppermute | solution.py:71
  148.1 2.4 %add_convert_fusion = bf16[256,1024]{1,0:T(8,128)(2,1)} fusion(bf16[256,1024]{1,0:T(8,128)(2,1)} %collective-permute-done.20, bf16[256,1024]{1,0:T(8,128)(2,1)} %collective-permute-done.18, bf16[256,1024]{1,0:T(8,128)(2,1)} %get-tuple-element.52), kind=kLoop, calls=%fused_computation.19 | loop fusion | flops 1572864 | bytes 2097152 | tf_op jit(solution)/shard_map/convert_element_type | solution.py:384
  152.6 6.7 %all-gather = bf16[192,1024]{1,0:T(8,128)(2,1)S(1)} all-gather(bf16[48,1024]{1,0:T(8,128)(2,1)S(1)} %pad_maximum_fusion.5), channel_id=2, replica_groups=mesh['z'=4,'x'=2,'y'=2,'c'=2] {'y','c'}, dimensions={0}, use_global_device_ids=true | all-gather | bytes 491520 | tf_op jit(solution)/shard_map/all_gather | solution.py:401
  162.6 5.7 %all-to-all-start.4 = ((bf16[8,32,1024]{2,1,0:T(8,128)(2,1)}), bf16[8,32,1024]{2,1,0:T(8,128)(2,1)S(1)}, u32[]{:S(2)}, u32[]{:S(2)}) async-start(bf16[8,32,1024]{2,1,0:T(8,128)(2,1)} %bitcast.77), calls=%async_computation.4 | async-start | bytes 1048576 | tf_op jit(solution)/shard_map/all_to_all | solution.py:61
  168.4 2.1 collective-permute-start.25
  171.9 10.3 %collective-permute-done.24 = bf16[128,512]{0,1:T(8,128)(2,1)S(1)} collective-permute-done((bf16[128,512]{0,1:T(8,128)(2,1)S(1)}, bf16[128,512]{0,1:T(8,128)(2,1)S(1)}, u32[]{:S(2)}, u32[]{:S(2)}) %collective-permute-start.24) | collective-permute-done | bytes 131104 | tf_op jit(solution)/shard_map/ppermute | solution.py:71
  185.2 7.6 %all-gather.1 = bf16[320,1024]{1,0:T(8,128)(2,1)S(1)} all-gather(bf16[80,1024]{1,0:T(8,128)(2,1)S(1)} %pad_maximum_fusion.2), channel_id=3, replica_groups=mesh['z'=4,'x'=2,'y'=2,'c'=2] {'y','c'}, dimensions={0}, use_global_device_ids=true | all-gather | bytes 819200 | tf_op jit(solution)/shard_map/all_gather | solution.py:462
  194.4 4.4 %all-to-all-start.5 = ((bf16[4,128,768]{2,1,0:T(8,128)(2,1)}), bf16[4,128,768]{2,1,0:T(8,128)(2,1)S(1)}, u32[]{:S(2)}, u32[]{:S(2)}) async-start(bf16[4,128,768]{2,1,0:T(8,128)(2,1)} %pad_maximum_fusion), calls=%async_computation.5 | async-start | bytes 1572864 | tf_op jit(solution)/shard_map/all_to_all | solution.py:61
  198.8 2.1 collective-permute-start.22
  201.6 10.4 %collective-permute-done.22 = f32[2,8,128]{2,1,0:T(8,128)S(1)} collective-permute-done((f32[2,8,128]{2,1,0:T(8,128)S(1)}, f32[2,8,128]{2,1,0:T(8,128)S(1)}, u32[]{:S(2)}, u32[]{:S(2)}) %collective-permute-start.22) | collective-permute-done | bytes 8224 | tf_op jit(solution)/shard_map/ppermute | solution.py:71
  212.1 4.6 %collective-permute-start.23 = (f32[2,8,128]{2,1,0:T(8,128)S(1)}, f32[2,8,128]{2,1,0:T(8,128)S(1)}, u32[]{:S(2)}, u32[]{:S(2)}) collective-permute-start(f32[2,8,128]{2,1,0:T(8,128)S(1)} %fusion.97), channel_id=1, source_target_pairs={{0,16},{8,24},{16,0},{24,8},{1,17},{9,25},{17,1},{25,9},{2,18},{10... | collective-permute-start | bytes 24584 | tf_op jit(solution)/shard_map/ppermute | solution.py:71
  217.5 2.0 collective-permute-done.23
  (249 shorter events, 42.7 us)
Async XLA Ops:
  3.3 28.6 %all-to-all-start = ((bf16[4,144,768]{2,1,0:T(8,128)(2,1)}), bf16[4,144,768]{2,1,0:T(8,128)(2,1)S(1)}, u32[]{:S(2)}, u32[]{:S(2)}) async-start(bf16[4,144,768]{2,1,0:T(8,128)(2,1)} %broadcast_in_dim.24), calls=%async_computation | async-start | bytes 1769472 | tf_op jit(solution)/shard_map/all_to_all | solution.py:61
  9.7 7.8 %collective-permute-start = (bf16[128,1024]{1,0:T(8,128)(2,1)S(1)}, bf16[128,1024]{1,0:T(8,128)(2,1)S(1)}, u32[]{:S(2)}, u32[]{:S(2)}) collective-permute-start(bf16[128,1024]{1,0:T(8,128)(2,1)S(1)} %copy-done.8), channel_id=1, source_target_pairs={{0,4},{4,0},{1,5},{5,1},{2,6},{6,2},{3,7},{7,3},{8,12},{12,8},{9,1... | collective-permute-start | bytes 786440 | tf_op jit(solution)/shard_map/ppermute | solution.py:71
  32.4 6.4 %collective-permute-start.1 = (bf16[128,512]{1,0:T(8,128)(2,1)S(1)}, bf16[128,512]{1,0:T(8,128)(2,1)S(1)}, u32[]{:S(2)}, u32[]{:S(2)}) collective-permute-start(bf16[128,512]{1,0:T(8,128)(2,1)S(1)} %slice.466), channel_id=1, source_target_pairs={{0,4},{4,0},{1,5},{5,1},{2,6},{6,2},{3,7},{7,3},{8,12},{12,8},{9,1... | collective-permute-start | bytes 393224 | tf_op jit(solution)/shard_map/ppermute | solution.py:71
  34.0 9.3 %collective-permute-start.2 = (bf16[4,144,256]{2,1,0:T(8,128)(2,1)S(1)}, bf16[4,144,256]{2,1,0:T(8,128)(2,1)S(1)}, u32[]{:S(2)}, u32[]{:S(2)}) collective-permute-start(bf16[4,144,256]{2,1,0:T(8,128)(2,1)S(1)} %get-tuple-element.77), channel_id=1, source_target_pairs={{0,4},{4,0},{1,5},{5,1},{2,6},{6,2},{3,7},{7,3},{8,12},{12,8},{9,1... | collective-permute-start | bytes 884744 | tf_op jit(solution)/shard_map/ppermute | solution.py:71
  43.7 4.3 %collective-permute-start.3 = (bf16[1,2,32,1024]{3,2,0,1:T(8,128)(2,1)S(1)}, bf16[1,2,32,1024]{3,2,0,1:T(8,128)(2,1)S(1)}, u32[]{:S(2)}, u32[]{:S(2)}) collective-permute-start(bf16[1,2,32,1024]{3,2,0,1:T(8,128)(2,1)S(1)} %select_convert_fusion.1), channel_id=1, source_target_pairs={{0,1},{1,0},{2,3},{3,2},{4,5},{5,4},{6,7},{7,6},{8,9},{9,8},{10,11... | collective-permute-start | bytes 393224 | tf_op jit(solution)/shard_map/ppermute | solution.py:71
  44.6 13.9 %all-to-all-start.2 = ((bf16[4,32,1152]{2,1,0:T(8,128)(2,1)}), bf16[4,32,1152]{2,1,0:T(8,128)(2,1)S(1)}, u32[]{:S(2)}, u32[]{:S(2)}) async-start(bf16[4,32,1152]{2,1,0:T(8,128)(2,1)} %fusion.12), calls=%async_computation.2 | async-start | bytes 589824 | tf_op jit(solution)/shard_map/all_to_all | solution.py:61
  48.1 11.9 %collective-permute-start.4 = (bf16[1,32,1024]{2,1,0:T(8,128)(2,1)S(1)}, bf16[1,32,1024]{2,1,0:T(8,128)(2,1)S(1)}, u32[]{:S(2)}, u32[]{:S(2)}) collective-permute-start(bf16[1,32,1024]{2,1,0:T(8,128)(2,1)S(1)} %fusion.49), channel_id=1, source_target_pairs={{0,2},{2,0},{1,3},{3,1},{4,6},{6,4},{5,7},{7,5},{8,10},{10,8},{9,1... | collective-permute-start | bytes 196616 | tf_op jit(solution)/shard_map/ppermute | solution.py:71
  58.5 9.0 %collective-permute-start.6 = (bf16[4,32,1152]{2,1,0:T(8,128)(2,1)S(1)}, bf16[4,32,1152]{2,1,0:T(8,128)(2,1)S(1)}, u32[]{:S(2)}, u32[]{:S(2)}) collective-permute-start(bf16[4,32,1152]{2,1,0:T(8,128)(2,1)S(1)} %all-to-all-done.2), channel_id=1, source_target_pairs={{0,4},{4,0},{1,5},{5,1},{2,6},{6,2},{3,7},{7,3},{8,12},{12,8},{9,1... | collective-permute-start | bytes 884744 | tf_op jit(solution)/shard_map/ppermute | solution.py:71
  61.1 17.7 %all-to-all-start.1 = ((bf16[8,32,1024]{2,1,0:T(8,128)(2,1)}), bf16[8,32,1024]{2,1,0:T(8,128)(2,1)S(1)}, u32[]{:S(2)}, u32[]{:S(2)}) async-start(bf16[8,32,1024]{2,1,0:T(8,128)(2,1)} %broadcast_in_dim.27), calls=%async_computation.1 | async-start | bytes 1048576 | tf_op jit(solution)/shard_map/all_to_all | solution.py:61
  67.8 15.2 %collective-permute-start.11 = (bf16[256,1152]{1,0:T(8,128)(2,1)S(1)}, bf16[256,1152]{1,0:T(8,128)(2,1)S(1)}, u32[]{:S(2)}, u32[]{:S(2)}) collective-permute-start(bf16[256,1152]{1,0:T(8,128)(2,1)S(1)} %bitcast.185), channel_id=1, source_target_pairs={{0,2},{2,0},{1,3},{3,1},{4,6},{6,4},{5,7},{7,5},{8,10},{10,8},{9,1... | collective-permute-start | bytes 1769480 | tf_op jit(solution)/shard_map/ppermute | solution.py:71
  78.8 13.9 %collective-permute-start.9 = (bf16[256,1024]{1,0:T(8,128)(2,1)S(1)}, bf16[256,1024]{1,0:T(8,128)(2,1)S(1)}, u32[]{:S(2)}, u32[]{:S(2)}) collective-permute-start(bf16[256,1024]{1,0:T(8,128)(2,1)S(1)} %bitcast.191), channel_id=1, source_target_pairs={{0,2},{2,0},{1,3},{3,1},{4,6},{6,4},{5,7},{7,5},{8,10},{10,8},{9,1... | collective-permute-start | bytes 1572872 | tf_op jit(solution)/shard_map/ppermute | solution.py:71
  83.0 10.2 %collective-permute-start.12 = (bf16[256,1152]{1,0:T(8,128)(2,1)S(1)}, bf16[256,1152]{1,0:T(8,128)(2,1)S(1)}, u32[]{:S(2)}, u32[]{:S(2)}) collective-permute-start(bf16[256,1152]{1,0:T(8,128)(2,1)S(1)} %collective-permute-done.11.c_a.refs_6_), channel_id=1, source_target_pairs={{0,1},{1,0},{2,3},{3,2},{4,5},{5,4},{6,7},{7,6},{8,9},{9,8},{10,11... | collective-permute-start | bytes 1769480 | tf_op jit(solution)/shard_map/ppermute | solution.py:71
  92.7 9.9 %collective-permute-start.7 = (bf16[256,1152]{1,0:T(8,128)(2,1)S(1)}, bf16[256,1152]{1,0:T(8,128)(2,1)}, u32[]{:S(2)}, u32[]{:S(2)}) collective-permute-start(bf16[256,1152]{1,0:T(8,128)(2,1)S(1)} %bitcast.186), channel_id=1, source_target_pairs={{0,1},{1,0},{2,3},{3,2},{4,5},{5,4},{6,7},{7,6},{8,9},{9,8},{10,11... | collective-permute-start | bytes 1769480 | tf_op jit(solution)/shard_map/ppermute | solution.py:71
  93.2 9.4 %collective-permute-start.5 = (bf16[256,1024]{1,0:T(8,128)(2,1)S(1)}, bf16[256,1024]{1,0:T(8,128)(2,1)}, u32[]{:S(2)}, u32[]{:S(2)}) collective-permute-start(bf16[256,1024]{1,0:T(8,128)(2,1)S(1)} %bitcast.192), channel_id=1, source_target_pairs={{0,1},{1,0},{2,3},{3,2},{4,5},{5,4},{6,7},{7,6},{8,9},{9,8},{10,11... | collective-permute-start | bytes 1572872 | tf_op jit(solution)/shard_map/ppermute | solution.py:71
  102.4 8.1 %collective-permute-start.13 = (bf16[256,1024]{1,0:T(8,128)(2,1)}, bf16[256,1024]{1,0:T(8,128)(2,1)}, u32[]{:S(2)}, u32[]{:S(2)}) collective-permute-start(bf16[256,1024]{1,0:T(8,128)(2,1)} %get-tuple-element.40), channel_id=1, source_target_pairs={{0,1},{1,0},{2,3},{3,2},{4,5},{5,4},{6,7},{7,6},{8,9},{9,8},{10,11... | collective-permute-start | bytes 1572872 | tf_op jit(solution)/shard_map/ppermute | solution.py:71
  110.2 4.4 %collective-permute-start.8 = (bf16[256,1024]{1,0:T(8,128)(2,1)}, bf16[256,1024]{1,0:T(8,128)(2,1)S(1)}, u32[]{:S(2)}, u32[]{:S(2)}) collective-permute-start(bf16[256,1024]{1,0:T(8,128)(2,1)} %get-tuple-element.38), channel_id=1, source_target_pairs={{0,1},{1,0},{2,3},{3,2},{4,5},{5,4},{6,7},{7,6},{8,9},{9,8},{10,11... | collective-permute-start | bytes 1572872 | tf_op jit(solution)/shard_map/ppermute | solution.py:71
  112.5 14.4 %collective-permute-start.14 = (bf16[256,1024]{1,0:T(8,128)(2,1)}, bf16[256,1024]{1,0:T(8,128)(2,1)}, u32[]{:S(2)}, u32[]{:S(2)}) collective-permute-start(bf16[256,1024]{1,0:T(8,128)(2,1)} %add_convert_fusion.3), channel_id=1, source_target_pairs={{0,2},{2,0},{1,3},{3,1},{4,6},{6,4},{5,7},{7,5},{8,10},{10,8},{9,1... | collective-permute-start | bytes 1572872 | tf_op jit(solution)/shard_map/ppermute | solution.py:71
  114.0 25.1 %collective-permute-start.18 = (bf16[256,1024]{1,0:T(8,128)(2,1)}, bf16[256,1024]{1,0:T(8,128)(2,1)}, u32[]{:S(2)}, u32[]{:S(2)}) collective-permute-start(bf16[256,1024]{1,0:T(8,128)(2,1)} %get-tuple-element.53), channel_id=1, source_target_pairs={{0,1},{1,0},{2,3},{3,2},{4,5},{5,4},{6,7},{7,6},{8,9},{9,8},{10,11... | collective-permute-start | bytes 1572872 | tf_op jit(solution)/shard_map/ppermute | solution.py:71
  114.0 18.8 %collective-permute-start.19 = (bf16[256,1024]{1,0:T(8,128)(2,1)}, bf16[256,1024]{1,0:T(8,128)(2,1)S(1)}, u32[]{:S(2)}, u32[]{:S(2)}) collective-permute-start(bf16[256,1024]{1,0:T(8,128)(2,1)} %get-tuple-element.55), channel_id=1, source_target_pairs={{0,1},{1,0},{2,3},{3,2},{4,5},{5,4},{6,7},{7,6},{8,9},{9,8},{10,11... | collective-permute-start | bytes 1572872 | tf_op jit(solution)/shard_map/ppermute | solution.py:71
  129.0 21.5 %all-to-all-start.3 = ((bf16[8,32,1024]{2,1,0:T(8,128)(2,1)}), bf16[8,32,1024]{2,1,0:T(8,128)(2,1)S(1)}, u32[]{:S(2)}, u32[]{:S(2)}) async-start(bf16[8,32,1024]{2,1,0:T(8,128)(2,1)} %bitcast.46), calls=%async_computation.3 | async-start | bytes 1048576 | tf_op jit(solution)/shard_map/all_to_all | solution.py:61
  134.9 13.1 %collective-permute-start.20 = (bf16[256,1024]{1,0:T(8,128)(2,1)S(1)}, bf16[256,1024]{1,0:T(8,128)(2,1)}, u32[]{:S(2)}, u32[]{:S(2)}) collective-permute-start(bf16[256,1024]{1,0:T(8,128)(2,1)S(1)} %add_convert_fusion.1), channel_id=1, source_target_pairs={{0,2},{2,0},{1,3},{3,1},{4,6},{6,4},{5,7},{7,5},{8,10},{10,8},{9,1... | collective-permute-start | bytes 1572872 | tf_op jit(solution)/shard_map/ppermute | solution.py:71
  137.1 45.7 %collective-permute-start.26 = (bf16[128,256]{0,1:T(8,128)(2,1)S(1)}, bf16[128,256]{0,1:T(8,128)(2,1)}, u32[]{:S(2)}, u32[]{:S(2)}) collective-permute-start(bf16[128,256]{0,1:T(8,128)(2,1)S(1)} %bitcast.217), channel_id=1, source_target_pairs={{0,4},{4,0},{1,5},{5,1},{2,6},{6,2},{3,7},{7,3},{8,12},{12,8},{9,1... | collective-permute-start | bytes 196616 | tf_op jit(solution)/shard_map/ppermute | solution.py:71
  139.1 22.4 %collective-permute-start.15 = (bf16[512,512]{1,0:T(8,128)(2,1)S(1)}, bf16[512,512]{1,0:T(8,128)(2,1)S(1)}, u32[]{:S(2)}, u32[]{:S(2)}) collective-permute-start(bf16[512,512]{1,0:T(8,128)(2,1)S(1)} %bitcast.202), channel_id=1, source_target_pairs={{0,4},{4,0},{1,5},{5,1},{2,6},{6,2},{3,7},{7,3},{8,12},{12,8},{9,1... | collective-permute-start | bytes 1572872 | tf_op jit(solution)/shard_map/ppermute | solution.py:71
  162.2 8.4 %collective-permute-start.16 = (bf16[1,2,32,1024]{3,2,1,0:T(8,128)(2,1)S(1)}, bf16[1,2,32,1024]{3,2,1,0:T(8,128)(2,1)S(1)}, u32[]{:S(2)}, u32[]{:S(2)}) collective-permute-start(bf16[1,2,32,1024]{3,2,1,0:T(8,128)(2,1)S(1)} %select_convert_fusion), channel_id=1, source_target_pairs={{0,1},{1,0},{2,3},{3,2},{4,5},{5,4},{6,7},{7,6},{8,9},{9,8},{10,11... | collective-permute-start | bytes 393224 | tf_op jit(solution)/shard_map/ppermute | solution.py:71
  162.6 21.5 %all-to-all-start.4 = ((bf16[8,32,1024]{2,1,0:T(8,128)(2,1)}), bf16[8,32,1024]{2,1,0:T(8,128)(2,1)S(1)}, u32[]{:S(2)}, u32[]{:S(2)}) async-start(bf16[8,32,1024]{2,1,0:T(8,128)(2,1)} %bitcast.77), calls=%async_computation.4 | async-start | bytes 1048576 | tf_op jit(solution)/shard_map/all_to_all | solution.py:61
  168.4 14.4 %collective-permute-start.25 = (bf16[128,512]{1,0:T(8,128)(2,1)S(1)}, bf16[128,512]{1,0:T(8,128)(2,1)S(1)}, u32[]{:S(2)}, u32[]{:S(2)}) collective-permute-start(bf16[128,512]{1,0:T(8,128)(2,1)S(1)} %pad_maximum_fusion.4), channel_id=1, source_target_pairs={{0,4},{4,0},{1,5},{5,1},{2,6},{6,2},{3,7},{7,3},{8,12},{12,8},{9,1... | collective-permute-start | bytes 393224 | tf_op jit(solution)/shard_map/ppermute | solution.py:71
  170.5 11.8 %collective-permute-start.24 = (bf16[128,512]{0,1:T(8,128)(2,1)S(1)}, bf16[128,512]{0,1:T(8,128)(2,1)S(1)}, u32[]{:S(2)}, u32[]{:S(2)}) collective-permute-start(bf16[128,512]{0,1:T(8,128)(2,1)S(1)} %copy-done.21), channel_id=1, source_target_pairs={{0,4},{4,0},{1,5},{5,1},{2,6},{6,2},{3,7},{7,3},{8,12},{12,8},{9,1... | collective-permute-start | bytes 393224 | tf_op jit(solution)/shard_map/ppermute | solution.py:71
  170.7 13.2 %collective-permute-start.17 = (bf16[1,32,1024]{2,1,0:T(8,128)(2,1)S(1)}, bf16[1,32,1024]{2,1,0:T(8,128)(2,1)S(1)}, u32[]{:S(2)}, u32[]{:S(2)}) collective-permute-start(bf16[1,32,1024]{2,1,0:T(8,128)(2,1)S(1)} %fusion.48), channel_id=1, source_target_pairs={{0,2},{2,0},{1,3},{3,1},{4,6},{6,4},{5,7},{7,5},{8,10},{10,8},{9,1... | collective-permute-start | bytes 196616 | tf_op jit(solution)/shard_map/ppermute | solution.py:71
  192.9 5.9 %collective-permute-start.21 = (f32[2,8,128]{2,1,0:T(8,128)S(1)}, f32[2,8,128]{2,1,0:T(8,128)S(1)}, u32[]{:S(2)}, u32[]{:S(2)}) collective-permute-start(f32[2,8,128]{2,1,0:T(8,128)S(1)} %pad_maximum_fusion.13), channel_id=1, source_target_pairs={{0,4},{4,0},{1,5},{5,1},{2,6},{6,2},{3,7},{7,3},{8,12},{12,8},{9,1... | collective-permute-start | bytes 24584 | tf_op jit(solution)/shard_map/ppermute | solution.py:71
  194.4 25.7 %all-to-all-start.5 = ((bf16[4,128,768]{2,1,0:T(8,128)(2,1)}), bf16[4,128,768]{2,1,0:T(8,128)(2,1)S(1)}, u32[]{:S(2)}, u32[]{:S(2)}) async-start(bf16[4,128,768]{2,1,0:T(8,128)(2,1)} %pad_maximum_fusion), calls=%async_computation.5 | async-start | bytes 1572864 | tf_op jit(solution)/shard_map/all_to_all | solution.py:61
  198.8 13.3 %collective-permute-start.22 = (f32[2,8,128]{2,1,0:T(8,128)S(1)}, f32[2,8,128]{2,1,0:T(8,128)S(1)}, u32[]{:S(2)}, u32[]{:S(2)}) collective-permute-start(f32[2,8,128]{2,1,0:T(8,128)S(1)} %fusion.75), channel_id=1, source_target_pairs={{0,8},{8,0},{16,24},{24,16},{1,9},{9,1},{17,25},{25,17},{2,10},{10... | collective-permute-start | bytes 24584 | tf_op jit(solution)/shard_map/ppermute | solution.py:71
  212.1 7.4 %collective-permute-start.23 = (f32[2,8,128]{2,1,0:T(8,128)S(1)}, f32[2,8,128]{2,1,0:T(8,128)S(1)}, u32[]{:S(2)}, u32[]{:S(2)}) collective-permute-start(f32[2,8,128]{2,1,0:T(8,128)S(1)} %fusion.97), channel_id=1, source_target_pairs={{0,16},{8,24},{16,0},{24,8},{1,17},{9,25},{17,1},{25,9},{2,18},{10... | collective-permute-start | bytes 24584 | tf_op jit(solution)/shard_map/ppermute | solution.py:71
  (43 other events, 437.2 us)

commit v4 on v3

--- a/solution.py
+++ b/solution.py
@@ -10,7 +10,7 @@
 ROPE_BASE = 10000.0
 MASKED = -1e30
 LANES = 128
-SUBLANES = 16
+SUBLANES = 8
 bf16 = jnp.bfloat16
 f32 = jnp.float32
 
@@ -88,7 +88,7 @@
 
 def expert_kernel(
     x_a, x_b, c_a, c_b, gate, up, down,
-    grad_a, grad_b, moe_a, moe_b, hidden, grad_gate, grad_up,
+    grad_a, grad_b, hidden, grad_gate, grad_up,
 ):
     rows, width = x_a.shape
     count, units, _ = down.shape
@@ -116,26 +116,23 @@
         grad_gate[part] = low_gate
         grad_up[part] = low_up
         grad = contract(low_gate, gate_all, 1, 1) + contract(low_up, up_all, 1, 1)
-        moe = contract(low, down_all, 1, 0)
         if i == 0:
             grad_a[...] = grad
-            moe_a[...] = moe.astype(bf16)
         else:
             grad_b[...] = grad.astype(bf16)
-            moe_b[...] = moe.astype(bf16)
 
 
 def run_experts(x_a, x_b, c_a, c_b, gate, up, down):
     rows, width = x_a.shape
     count, _, units = gate.shape
     whole = pl.BlockSpec(memory_space=pltpu.VMEM)
-    low = jax.ShapeDtypeStruct((rows, width), bf16)
+    low = pltpu.VMEM((rows, width), bf16)
     held = jax.ShapeDtypeStruct((2 * rows, count * units), bf16)
     return pl.pallas_call(
         expert_kernel,
         in_specs=[whole] * 7,
-        out_specs=[whole] * 7,
-        out_shape=[jax.ShapeDtypeStruct((rows, width), f32), low, low, low, held, held, held],
+        out_specs=[whole] * 5,
+        out_shape=[pltpu.VMEM((rows, width), f32), low, held, held, held],
     )(x_a, x_b, c_a, c_b, gate, up, down)
 
 
@@ -184,6 +181,33 @@
         ],
         scratch_shapes=[pltpu.VMEM((width, parts * rows), bf16)],
     )(*x_parts, *c_parts, *hidden, *grad_gate, *grad_up)
+
+
+def pack_kernel(query, keys, values, out, attn_gain, ffn_gain, packed):
+    copies = packed.shape[0]
+    piece = query.shape[0]
+    spare = packed.shape[1] - piece
+    row = lax.broadcasted_iota(jnp.int32, (spare, piece), 0)
+    first = jnp.broadcast_to(attn_gain[...].astype(f32), (spare, piece))
+    second = jnp.broadcast_to(ffn_gain[...].astype(f32), (spare, piece))
+    gains = jnp.where(row == 0, first, jnp.where(row == 1, second, 0.0)).astype(bf16)
+    for i in range(copies):
+        start = 0
+        for ref in (query, keys, values, out):
+            packed[i, :piece, start : start + ref.shape[1]] = ref[...]
+            start += ref.shape[1]
+        start -= out.shape[1]
+        packed[i, piece:] = jnp.zeros((spare, packed.shape[2]), bf16)
+        packed[i, piece:, start : start + piece] = gains
+
+
+def pack_weights(copies, query, keys, values, out, attn_gain, ffn_gain):
+    piece = query.shape[0]
+    width = query.shape[1] + keys.shape[1] + values.shape[1] + out.shape[1]
+    return pl.pallas_call(
+        pack_kernel,
+        out_shape=jax.ShapeDtypeStruct((copies, piece + SUBLANES, width), bf16),
+    )(query, keys, values, out, attn_gain[None], ffn_gain[None])
 
 
 def gather_offsets(value):
@@ -290,15 +314,15 @@
             pieces += [jnp.where(x_at == 0, mine, theirs), jnp.where(x_at == 0, theirs, mine)]
         return jnp.concatenate(pieces, axis=-1)
 
-    shard = jnp.concatenate(
-        [query_weight, key_projection_matrix, value_projection_matrix, out_weight], 1
-    )
     cols = q_cols + 2 * k_cols
     out_cols = out_weight.shape[1]
-    gain_rows = jnp.pad(
-        jnp.stack([attn_gain, ffn_gain]), ((0, SUBLANES - 2), (cols, out_cols - piece))
-    )
-    packed = gather_blocks(jnp.concatenate([shard, gain_rows], 0), "z")
+    packed = exchange(
+        pack_weights(
+            n_z, query_weight, key_projection_matrix, value_projection_matrix, out_weight,
+            attn_gain, ffn_gain,
+        ),
+        "z",
+    )
     other_tokens = flip(tokens, "x", 1)
     qkv_half = packed[:, :piece, :cols].reshape(half, cols)
     gain_half = packed[:, piece, cols : cols + piece].reshape(half).astype(f32)
@@ -380,19 +404,27 @@
     grad_c = {k: r[4] + flip(r[5], "c", 1).astype(f32) for k, r in results.items()}
     grad_c[0] = lax.optimization_barrier(grad_c[0])
     grad_y = reduce_offsets(dict(grad_c)).astype(bf16)
-    moe_c = {k: r[6].astype(f32) + flip(r[7], "c", 1).astype(f32) for k, r in results.items()}
+    moe_c = {}
+    for k, r in results.items():
+        moe = jnp.dot(r[6], down_weight.reshape(-1, width), preferred_element_type=f32)
+        own_moe, other_moe = jnp.split(moe, 2)
+        received = flip(other_moe.astype(bf16), "c", 1)
+        moe_c[k] = own_moe + received.astype(f32)
+    sent_moe = {k: v.astype(bf16) for k, v in moe_c.items() if k}
+    for k, v in sent_moe.items():
+        moe_c[k], grad_y = lax.optimization_barrier((v, grad_y))
     moe_y = reduce_offsets(moe_c).astype(bf16).reshape(n_ep, sub, width)
+    grad_ep = exchange(grad_y.reshape(n_ep, sub, width), EP)
     ordered_results = [results[k] for k in offsets]
     gate_grad, up_grad, down_grad = run_grads(
         [part for r in ordered_results for part in r[:2]],
         [part for r in ordered_results for part in r[2:4]],
-        *([r[i] for r in ordered_results] for i in (8, 9, 10)),
+        *([r[i] for r in ordered_results] for i in (6, 7, 8)),
         local_experts,
     )
-    grad_y, gate_grad, up_grad, down_grad = lax.optimization_barrier(
-        (grad_y, gate_grad, up_grad, down_grad)
-    )
-    grad_ep = exchange(grad_y.reshape(n_ep, sub, width), EP)
+    grad_ep, gate_grad, up_grad, down_grad = lax.optimization_barrier(
+        (grad_ep, gate_grad, up_grad, down_grad)
+    )
     grad_normed_two = jnp.sum(grad_ep.astype(f32), axis=0)
 
     norm_term, ffn_gain_part = rms_backward(hidden_one, inverse_two, gain_two, grad_normed_two)

time: 223 us -> 223 us (level)
  matrix products: 4.18 us -> 9.76 us
  waiting for transfers between devices: 92.5 us -> 88.9 us
    dot_general x0 -> x2, matrix products: none -> 3.88 us  [body(): jnp.dot(r[6], down_weight.reshape(-1, width), preferred_element_type=f32)]
    ppermute x27, waiting for transfers between devices: 60.3 us -> 57.7 us  [flip(): return lax.ppermute(value, axis, [(i, i ^ bit) for i in range(count)])]
    pallas_call x2 -> x3, Pallas kernels: 15.2 us -> 14.4 us  [the longest x2 12.5 us: run_experts(): pl.pallas_call(expert_kernel, in_specs=[whole] * 7, out_specs=[whole] * 5...]
  transfers between devices with their start and end apart: 33 -> 33, of which waited for: 15 -> 14; matrix products, arithmetic and copies ran while one was open for 11% -> 14% of each run, Pallas kernels for 12% -> 10%
where the time goes in v4:
time: 223 us; the launch traced here: 222 us
  waiting for transfers between devices  88.9 us (40%)
  starting transfers between devices  55.5 us (25%)
  Pallas kernels  25.2 us (11%)
  other arithmetic  17.9 us (8%)
  blocking collectives  13.3 us (6%)
  local copies, waits for them, and re-layouts  9.82 us (4%)
  matrix products  9.76 us (4%)
    ppermute x27, waiting for transfers between devices, flip(): return lax.ppermute(value, axis, [(i, i ^ bit) for i in range(count)])  57.7 us
    all_to_all x6, waiting for transfers between devices, exchange(): return lax.all_to_all(blocks, axis, split_axis=0, concat_axis=0, tiled=True)  31.2 us
    all_to_all x6, starting transfers between devices, exchange(): return lax.all_to_all(blocks, axis, split_axis=0, concat_axis=0, tiled=True)  28.1 us
    ppermute x27, starting transfers between devices, flip(): return lax.ppermute(value, axis, [(i, i ^ bit) for i in range(count)])  27.4 us
    pallas_call x2, Pallas kernels, run_experts(): pl.pallas_call(expert_kernel, in_specs=[whole] * 7, out_specs=[whole] * 5...  12.5 us
    pallas_call x1, Pallas kernels, run_grads(): pl.pallas_call(grads_kernel, grid=(count,), in_specs=[whole] * (2 * parts...  10.8 us
    all_gather x1, blocking collectives, body(): lax.all_gather(jnp.concatenate([(grad_hidden_one + input_term).astype(bf1...  7.18 us
    all_gather x1, blocking collectives, body(): lax.all_gather(jnp.concatenate([grad_hidden_one.astype(bf16), ffn_rows],...  6.09 us
  transfers between devices with their start and end apart: 33, of which 14 were waited for; matrix products, arithmetic and copies ran while one was open for 14% of the time, Pallas kernels for 10%

profile of v4, /device:TPU:0, one launch (start us, length us, event | category | flops | bytes accessed | tf_op | source)
XLA Modules:
  0.0 222.3 jit_solution(12946119149250645819)
XLA Ops:
  0.7 1.9 shard_map.221
  2.6 6.3 %all-to-all-start = ((bf16[4,136,768]{2,1,0:T(8,128)(2,1)}), bf16[4,136,768]{2,1,0:T(8,128)(2,1)S(1)}, u32[]{:S(2)}, u32[]{:S(2)}) async-start(bf16[4,136,768]{2,1,0:T(8,128)(2,1)} %shard_map.221), calls=%async_computation | async-start | bytes 1671168 | tf_op jit(solution)/shard_map/all_to_all | solution.py:61
  13.0 3.7 %collective-permute-done = bf16[128,1024]{1,0:T(8,128)(2,1)S(1)} collective-permute-done((bf16[128,1024]{1,0:T(8,128)(2,1)S(1)}, bf16[128,1024]{1,0:T(8,128)(2,1)S(1)}, u32[]{:S(2)}, u32[]{:S(2)}) %collective-permute-start) | collective-permute-done | bytes 262176 | tf_op jit(solution)/shard_map/ppermute | solution.py:71
  17.1 13.0 %all-to-all-done = bf16[4,136,768]{2,1,0:T(8,128)(2,1)S(1)} async-done(((bf16[4,136,768]{2,1,0:T(8,128)(2,1)}), bf16[4,136,768]{2,1,0:T(8,128)(2,1)S(1)}, u32[]{:S(2)}, u32[]{:S(2)}) %all-to-all-start) | async-done | bytes 835616 | tf_op jit(solution)/shard_map/all_to_all | solution.py:61
  32.8 4.2 %collective-permute-done.1 = bf16[128,512]{1,0:T(8,128)(2,1)S(1)} collective-permute-done((bf16[128,512]{1,0:T(8,128)(2,1)S(1)}, bf16[128,512]{1,0:T(8,128)(2,1)S(1)}, u32[]{:S(2)}, u32[]{:S(2)}) %collective-permute-start.1) | collective-permute-done | bytes 131104 | tf_op jit(solution)/shard_map/ppermute | solution.py:71
  43.3 3.5 %all-to-all-start.2 = ((bf16[4,32,1152]{2,1,0:T(8,128)(2,1)}), bf16[4,32,1152]{2,1,0:T(8,128)(2,1)S(1)}, u32[]{:S(2)}, u32[]{:S(2)}) async-start(bf16[4,32,1152]{2,1,0:T(8,128)(2,1)} %fusion.15), calls=%async_computation.2 | async-start | bytes 589824 | tf_op jit(solution)/shard_map/all_to_all | solution.py:61
  49.1 8.2 %all-to-all-done.2 = bf16[4,32,1152]{2,1,0:T(8,128)(2,1)S(1)} async-done(((bf16[4,32,1152]{2,1,0:T(8,128)(2,1)}), bf16[4,32,1152]{2,1,0:T(8,128)(2,1)S(1)}, u32[]{:S(2)}, u32[]{:S(2)}) %all-to-all-start.2) | async-done | bytes 294944 | tf_op jit(solution)/shard_map/all_to_all | solution.py:61
  60.5 3.5 %all-to-all-start.1 = ((bf16[8,32,1024]{2,1,0:T(8,128)(2,1)}), bf16[8,32,1024]{2,1,0:T(8,128)(2,1)S(1)}, u32[]{:S(2)}, u32[]{:S(2)}) async-start(bf16[8,32,1024]{2,1,0:T(8,128)(2,1)} %broadcast_in_dim.32), calls=%async_computation.1 | async-start | bytes 1048576 | tf_op jit(solution)/shard_map/all_to_all | solution.py:61
  64.0 2.3 %collective-permute-done.7 = bf16[4,32,1152]{2,1,0:T(8,128)(2,1)S(1)} collective-permute-done((bf16[4,32,1152]{2,1,0:T(8,128)(2,1)S(1)}, bf16[4,32,1152]{2,1,0:T(8,128)(2,1)S(1)}, u32[]{:S(2)}, u32[]{:S(2)}) %collective-permute-start.7) | collective-permute-done | bytes 294944 | tf_op jit(solution)/shard_map/ppermute | solution.py:71
  66.6 1.6 collective-permute-start.8
  68.2 10.0 %all-to-all-done.1 = bf16[8,32,1024]{2,1,0:T(8,128)(2,1)S(1)} async-done(((bf16[8,32,1024]{2,1,0:T(8,128)(2,1)}), bf16[8,32,1024]{2,1,0:T(8,128)(2,1)S(1)}, u32[]{:S(2)}, u32[]{:S(2)}) %all-to-all-start.1) | async-done | bytes 524320 | tf_op jit(solution)/shard_map/all_to_all | solution.py:61
  81.1 10.3 %collective-permute-done.5.x_a.refs_2_ = bf16[256,1024]{1,0:T(8,128)(2,1)S(1)} collective-permute-done((bf16[256,1024]{1,0:T(8,128)(2,1)S(1)}, bf16[256,1024]{1,0:T(8,128)(2,1)S(1)}, u32[]{:S(2)}, u32[]{:S(2)}) %collective-permute-start.5) | collective-permute-done | bytes 524320 | tf_op jit(solution)/shard_map/ppermute | solution.py:71
  93.5 6.3 %shard_map.222 = (f32[256,1024]{1,0:T(8,128)S(1)}, bf16[256,1024]{1,0:T(8,128)(2,1)S(1)}, bf16[512,512]{1,0:T(8,128)(2,1)}, bf16[512,512]{1,0:T(8,128)(2,1)}, bf16[512,512]{1,0:T(8,128)(2,1)}) custom-call(bf16[256,1024]{1,0:T(8,128)(2,1)} %copy-done.12, bf16[256,1024]{1,0:T(8,128)(2,1)} %collective-permute-done.6.x_b.refs_3_, bf16[256,1152]{1,0:T(8,128)(2,1)} %copy-done.8, ...), custom_call_target="tpu_custom_call" | custom-call | tf_op jit(solution)/shard_map/pallas_call | solution.py:131
  100.0 6.2 %shard_map.223 = (f32[256,1024]{1,0:T(8,128)S(1)}, bf16[256,1024]{1,0:T(8,128)(2,1)S(1)}, bf16[512,512]{1,0:T(8,128)(2,1)}, bf16[512,512]{1,0:T(8,128)(2,1)}, bf16[512,512]{1,0:T(8,128)(2,1)}) custom-call(bf16[256,1024]{1,0:T(8,128)(2,1)} %bitcast.200, bf16[256,1024]{1,0:T(8,128)(2,1)} %collective-permute-done.11.x_b.refs_1_, bf16[256,1152]{1,0:T(8,128)(2,1)} %bitcast.194, ...), custom_call_target="tpu_custom_call" | custom-call | tf_op jit(solution)/shard_map/pallas_call | solution.py:131
  106.6 2.1 fusion.80
  110.2 1.6 collective-permute-start.15
  113.0 11.5 %collective-permute-done.15 = bf16[256,1024]{1,0:T(8,128)(2,1)S(1)} collective-permute-done((bf16[256,1024]{1,0:T(8,128)(2,1)S(1)}, bf16[256,1024]{1,0:T(8,128)(2,1)S(1)}, u32[]{:S(2)}, u32[]{:S(2)}) %collective-permute-start.15) | collective-permute-done | bytes 524320 | tf_op jit(solution)/shard_map/ppermute | solution.py:71
  125.4 4.4 %all-to-all-start.3 = ((bf16[8,32,1024]{2,1,0:T(8,128)(2,1)}), bf16[8,32,1024]{2,1,0:T(8,128)(2,1)}, u32[]{:S(2)}, u32[]{:S(2)}) async-start(bf16[8,32,1024]{2,1,0:T(8,128)(2,1)} %bitcast.47), calls=%async_computation.3 | async-start | bytes 1048576 | tf_op jit(solution)/shard_map/all_to_all | solution.py:61
  129.9 1.8 fusion.81
  134.6 2.0 collective-permute-start.26
  136.7 10.8 %shard_map.224 = (f32[4,1024,128]{2,1,0:T(8,128)}, f32[4,1024,128]{2,1,0:T(8,128)}, f32[4,128,1024]{2,1,0:T(8,128)}) custom-call(bf16[256,1024]{1,0:T(8,128)(2,1)} %bitcast.201, bf16[256,1024]{1,0:T(8,128)(2,1)} %collective-permute-done.11.x_b.refs_1_, bf16[256,1024]{1,0:T(8,128)(2,1)} %copy-done.12, bf16[256,1024]{1,0:T(8,128)(2,1)} %collective-permute-done.6.x_b.refs_3_, ...), custom_call_target="tpu_custom_call" | custom-call | tf_op jit(solution)/shard_map/pallas_call | solution.py:172
  147.5 2.2 fusion.9
  152.8 6.1 %all-gather = bf16[160,1024]{1,0:T(8,128)(2,1)S(1)} all-gather(bf16[40,1024]{1,0:T(8,128)(2,1)S(1)} %pad_maximum_fusion.4), channel_id=2, replica_groups=mesh['z'=4,'x'=2,'y'=2,'c'=2] {'y','c'}, dimensions={0}, use_global_device_ids=true | all-gather | bytes 409600 | tf_op jit(solution)/shard_map/all_gather | solution.py:433
  163.5 5.9 %all-to-all-start.4 = ((bf16[8,32,1024]{2,1,0:T(8,128)(2,1)}), bf16[8,32,1024]{2,1,0:T(8,128)(2,1)S(1)}, u32[]{:S(2)}, u32[]{:S(2)}) async-start(bf16[8,32,1024]{2,1,0:T(8,128)(2,1)} %bitcast.78), calls=%async_computation.4 | async-start | bytes 1048576 | tf_op jit(solution)/shard_map/all_to_all | solution.py:61
  169.6 2.1 collective-permute-start.25
  173.1 10.3 %collective-permute-done.24 = bf16[128,512]{0,1:T(8,128)(2,1)S(1)} collective-permute-done((bf16[128,512]{0,1:T(8,128)(2,1)S(1)}, bf16[128,512]{0,1:T(8,128)(2,1)S(1)}, u32[]{:S(2)}, u32[]{:S(2)}) %collective-permute-start.24) | collective-permute-done | bytes 131104 | tf_op jit(solution)/shard_map/ppermute | solution.py:71
  186.4 7.2 %all-gather.1 = bf16[288,1024]{1,0:T(8,128)(2,1)S(1)} all-gather(bf16[72,1024]{1,0:T(8,128)(2,1)S(1)} %pad_maximum_fusion.1), channel_id=3, replica_groups=mesh['z'=4,'x'=2,'y'=2,'c'=2] {'y','c'}, dimensions={0}, use_global_device_ids=true | all-gather | bytes 737280 | tf_op jit(solution)/shard_map/all_gather | solution.py:494
  195.1 4.5 %all-to-all-start.5 = ((bf16[4,128,768]{2,1,0:T(8,128)(2,1)}), bf16[4,128,768]{2,1,0:T(8,128)(2,1)S(1)}, u32[]{:S(2)}, u32[]{:S(2)}) async-start(bf16[4,128,768]{2,1,0:T(8,128)(2,1)} %pad_maximum_fusion), calls=%async_computation.5 | async-start | bytes 1572864 | tf_op jit(solution)/shard_map/all_to_all | solution.py:61
  199.6 2.1 collective-permute-start.22
  202.4 10.4 %collective-permute-done.22 = f32[2,8,128]{2,1,0:T(8,128)S(1)} collective-permute-done((f32[2,8,128]{2,1,0:T(8,128)S(1)}, f32[2,8,128]{2,1,0:T(8,128)S(1)}, u32[]{:S(2)}, u32[]{:S(2)}) %collective-permute-start.22) | collective-permute-done | bytes 8224 | tf_op jit(solution)/shard_map/ppermute | solution.py:71
  212.9 4.6 %collective-permute-start.23 = (f32[2,8,128]{2,1,0:T(8,128)S(1)}, f32[2,8,128]{2,1,0:T(8,128)S(1)}, u32[]{:S(2)}, u32[]{:S(2)}) collective-permute-start(f32[2,8,128]{2,1,0:T(8,128)S(1)} %fusion.99), channel_id=1, source_target_pairs={{0,16},{8,24},{16,0},{24,8},{1,17},{9,25},{17,1},{25,9},{2,18},{10... | collective-permute-start | bytes 24584 | tf_op jit(solution)/shard_map/ppermute | solution.py:71
  218.3 2.0 collective-permute-done.23
  (264 shorter events, 47.8 us)
Async XLA Ops:
  2.6 27.5 %all-to-all-start = ((bf16[4,136,768]{2,1,0:T(8,128)(2,1)}), bf16[4,136,768]{2,1,0:T(8,128)(2,1)S(1)}, u32[]{:S(2)}, u32[]{:S(2)}) async-start(bf16[4,136,768]{2,1,0:T(8,128)(2,1)} %shard_map.221), calls=%async_computation | async-start | bytes 1671168 | tf_op jit(solution)/shard_map/all_to_all | solution.py:61
  8.9 7.8 %collective-permute-start = (bf16[128,1024]{1,0:T(8,128)(2,1)S(1)}, bf16[128,1024]{1,0:T(8,128)(2,1)S(1)}, u32[]{:S(2)}, u32[]{:S(2)}) collective-permute-start(bf16[128,1024]{1,0:T(8,128)(2,1)S(1)} %copy-done.13), channel_id=1, source_target_pairs={{0,4},{4,0},{1,5},{5,1},{2,6},{6,2},{3,7},{7,3},{8,12},{12,8},{9,1... | collective-permute-start | bytes 786440 | tf_op jit(solution)/shard_map/ppermute | solution.py:71
  30.6 6.4 %collective-permute-start.1 = (bf16[128,512]{1,0:T(8,128)(2,1)S(1)}, bf16[128,512]{1,0:T(8,128)(2,1)S(1)}, u32[]{:S(2)}, u32[]{:S(2)}) collective-permute-start(bf16[128,512]{1,0:T(8,128)(2,1)S(1)} %slice.466), channel_id=1, source_target_pairs={{0,4},{4,0},{1,5},{5,1},{2,6},{6,2},{3,7},{7,3},{8,12},{12,8},{9,1... | collective-permute-start | bytes 393224 | tf_op jit(solution)/shard_map/ppermute | solution.py:71
  32.2 8.9 %collective-permute-start.2 = (bf16[4,136,256]{2,1,0:T(8,128)(2,1)S(1)}, bf16[4,136,256]{2,1,0:T(8,128)(2,1)S(1)}, u32[]{:S(2)}, u32[]{:S(2)}) collective-permute-start(bf16[4,136,256]{2,1,0:T(8,128)(2,1)S(1)} %get-tuple-element.73), channel_id=1, source_target_pairs={{0,4},{4,0},{1,5},{5,1},{2,6},{6,2},{3,7},{7,3},{8,12},{12,8},{9,1... | collective-permute-start | bytes 835592 | tf_op jit(solution)/shard_map/ppermute | solution.py:71
  42.5 4.3 %collective-permute-start.3 = (bf16[1,2,32,1024]{3,2,0,1:T(8,128)(2,1)S(1)}, bf16[1,2,32,1024]{3,2,0,1:T(8,128)(2,1)S(1)}, u32[]{:S(2)}, u32[]{:S(2)}) collective-permute-start(bf16[1,2,32,1024]{3,2,0,1:T(8,128)(2,1)S(1)} %select_convert_fusion.1), channel_id=1, source_target_pairs={{0,1},{1,0},{2,3},{3,2},{4,5},{5,4},{6,7},{7,6},{8,9},{9,8},{10,11... | collective-permute-start | bytes 393224 | tf_op jit(solution)/shard_map/ppermute | solution.py:71
  43.3 13.9 %all-to-all-start.2 = ((bf16[4,32,1152]{2,1,0:T(8,128)(2,1)}), bf16[4,32,1152]{2,1,0:T(8,128)(2,1)S(1)}, u32[]{:S(2)}, u32[]{:S(2)}) async-start(bf16[4,32,1152]{2,1,0:T(8,128)(2,1)} %fusion.15), calls=%async_computation.2 | async-start | bytes 589824 | tf_op jit(solution)/shard_map/all_to_all | solution.py:61
  46.9 11.9 %collective-permute-start.4 = (bf16[1,32,1024]{2,1,0:T(8,128)(2,1)S(1)}, bf16[1,32,1024]{2,1,0:T(8,128)(2,1)S(1)}, u32[]{:S(2)}, u32[]{:S(2)}) collective-permute-start(bf16[1,32,1024]{2,1,0:T(8,128)(2,1)S(1)} %fusion.52), channel_id=1, source_target_pairs={{0,2},{2,0},{1,3},{3,1},{4,6},{6,4},{5,7},{7,5},{8,10},{10,8},{9,1... | collective-permute-start | bytes 196616 | tf_op jit(solution)/shard_map/ppermute | solution.py:71
  57.3 9.0 %collective-permute-start.7 = (bf16[4,32,1152]{2,1,0:T(8,128)(2,1)S(1)}, bf16[4,32,1152]{2,1,0:T(8,128)(2,1)S(1)}, u32[]{:S(2)}, u32[]{:S(2)}) collective-permute-start(bf16[4,32,1152]{2,1,0:T(8,128)(2,1)S(1)} %all-to-all-done.2), channel_id=1, source_target_pairs={{0,4},{4,0},{1,5},{5,1},{2,6},{6,2},{3,7},{7,3},{8,12},{12,8},{9,1... | collective-permute-start | bytes 884744 | tf_op jit(solution)/shard_map/ppermute | solution.py:71
  60.5 17.7 %all-to-all-start.1 = ((bf16[8,32,1024]{2,1,0:T(8,128)(2,1)}), bf16[8,32,1024]{2,1,0:T(8,128)(2,1)S(1)}, u32[]{:S(2)}, u32[]{:S(2)}) async-start(bf16[8,32,1024]{2,1,0:T(8,128)(2,1)} %broadcast_in_dim.32), calls=%async_computation.1 | async-start | bytes 1048576 | tf_op jit(solution)/shard_map/all_to_all | solution.py:61
  66.6 14.5 %collective-permute-start.8 = (bf16[256,1152]{1,0:T(8,128)(2,1)S(1)}, bf16[256,1152]{1,0:T(8,128)(2,1)S(1)}, u32[]{:S(2)}, u32[]{:S(2)}) collective-permute-start(bf16[256,1152]{1,0:T(8,128)(2,1)S(1)} %bitcast.192), channel_id=1, source_target_pairs={{0,2},{2,0},{1,3},{3,1},{4,6},{6,4},{5,7},{7,5},{8,10},{10,8},{9,1... | collective-permute-start | bytes 1769480 | tf_op jit(solution)/shard_map/ppermute | solution.py:71
  78.2 13.2 %collective-permute-start.5 = (bf16[256,1024]{1,0:T(8,128)(2,1)S(1)}, bf16[256,1024]{1,0:T(8,128)(2,1)S(1)}, u32[]{:S(2)}, u32[]{:S(2)}) collective-permute-start(bf16[256,1024]{1,0:T(8,128)(2,1)S(1)} %bitcast.198), channel_id=1, source_target_pairs={{0,2},{2,0},{1,3},{3,1},{4,6},{6,4},{5,7},{7,5},{8,10},{10,8},{9,1... | collective-permute-start | bytes 1572872 | tf_op jit(solution)/shard_map/ppermute | solution.py:71
  81.1 10.8 %collective-permute-start.9 = (bf16[256,1152]{1,0:T(8,128)(2,1)S(1)}, bf16[256,1152]{1,0:T(8,128)(2,1)S(1)}, u32[]{:S(2)}, u32[]{:S(2)}) collective-permute-start(bf16[256,1152]{1,0:T(8,128)(2,1)S(1)} %collective-permute-done.8.c_a.refs_6_), channel_id=1, source_target_pairs={{0,1},{1,0},{2,3},{3,2},{4,5},{5,4},{6,7},{7,6},{8,9},{9,8},{10,11... | collective-permute-start | bytes 1769480 | tf_op jit(solution)/shard_map/ppermute | solution.py:71
  91.5 8.6 %collective-permute-start.12 = (bf16[256,1152]{1,0:T(8,128)(2,1)S(1)}, bf16[256,1152]{1,0:T(8,128)(2,1)}, u32[]{:S(2)}, u32[]{:S(2)}) collective-permute-start(bf16[256,1152]{1,0:T(8,128)(2,1)S(1)} %bitcast.193), channel_id=1, source_target_pairs={{0,1},{1,0},{2,3},{3,2},{4,5},{5,4},{6,7},{7,6},{8,9},{9,8},{10,11... | collective-permute-start | bytes 1769480 | tf_op jit(solution)/shard_map/ppermute | solution.py:71
  92.0 8.1 %collective-permute-start.11 = (bf16[256,1024]{1,0:T(8,128)(2,1)S(1)}, bf16[256,1024]{1,0:T(8,128)(2,1)}, u32[]{:S(2)}, u32[]{:S(2)}) collective-permute-start(bf16[256,1024]{1,0:T(8,128)(2,1)S(1)} %bitcast.199), channel_id=1, source_target_pairs={{0,1},{1,0},{2,3},{3,2},{4,5},{5,4},{6,7},{7,6},{8,9},{9,8},{10,11... | collective-permute-start | bytes 1572872 | tf_op jit(solution)/shard_map/ppermute | solution.py:71
  99.8 9.2 %collective-permute-start.14 = (bf16[256,1024]{1,0:T(8,128)(2,1)S(1)}, bf16[256,1024]{1,0:T(8,128)(2,1)}, u32[]{:S(2)}, u32[]{:S(2)}) collective-permute-start(bf16[256,1024]{1,0:T(8,128)(2,1)S(1)} %get-tuple-element.39), channel_id=1, source_target_pairs={{0,1},{1,0},{2,3},{3,2},{4,5},{5,4},{6,7},{7,6},{8,9},{9,8},{10,11... | collective-permute-start | bytes 1572872 | tf_op jit(solution)/shard_map/ppermute | solution.py:71
  106.2 5.6 %collective-permute-start.13 = (bf16[256,1024]{1,0:T(8,128)(2,1)S(1)}, bf16[256,1024]{1,0:T(8,128)(2,1)S(1)}, u32[]{:S(2)}, u32[]{:S(2)}) collective-permute-start(bf16[256,1024]{1,0:T(8,128)(2,1)S(1)} %get-tuple-element.37), channel_id=1, source_target_pairs={{0,1},{1,0},{2,3},{3,2},{4,5},{5,4},{6,7},{7,6},{8,9},{9,8},{10,11... | collective-permute-start | bytes 1572872 | tf_op jit(solution)/shard_map/ppermute | solution.py:71
  108.8 3.2 %collective-permute-start.10 = (bf16[256,1024]{1,0:T(8,128)(2,1)S(1)}, bf16[256,1024]{1,0:T(8,128)(2,1)S(1)}, u32[]{:S(2)}, u32[]{:S(2)}) collective-permute-start(bf16[256,1024]{1,0:T(8,128)(2,1)S(1)} %split.33), channel_id=1, source_target_pairs={{0,1},{1,0},{2,3},{3,2},{4,5},{5,4},{6,7},{7,6},{8,9},{9,8},{10,11... | collective-permute-start | bytes 1572872 | tf_op jit(solution)/shard_map/ppermute | solution.py:71
  110.2 14.3 %collective-permute-start.15 = (bf16[256,1024]{1,0:T(8,128)(2,1)S(1)}, bf16[256,1024]{1,0:T(8,128)(2,1)S(1)}, u32[]{:S(2)}, u32[]{:S(2)}) collective-permute-start(bf16[256,1024]{1,0:T(8,128)(2,1)S(1)} %add_convert_fusion.1), channel_id=1, source_target_pairs={{0,2},{2,0},{1,3},{3,1},{4,6},{6,4},{5,7},{7,5},{8,10},{10,8},{9,1... | collective-permute-start | bytes 1572872 | tf_op jit(solution)/shard_map/ppermute | solution.py:71
  125.4 24.3 %all-to-all-start.3 = ((bf16[8,32,1024]{2,1,0:T(8,128)(2,1)}), bf16[8,32,1024]{2,1,0:T(8,128)(2,1)}, u32[]{:S(2)}, u32[]{:S(2)}) async-start(bf16[8,32,1024]{2,1,0:T(8,128)(2,1)} %bitcast.47), calls=%async_computation.3 | async-start | bytes 1048576 | tf_op jit(solution)/shard_map/all_to_all | solution.py:61
  132.5 15.0 %collective-permute-start.19 = (bf16[256,1024]{1,0:T(8,128)(2,1)}, bf16[256,1024]{1,0:T(8,128)(2,1)S(1)}, u32[]{:S(2)}, u32[]{:S(2)}) collective-permute-start(bf16[256,1024]{1,0:T(8,128)(2,1)} %split.32), channel_id=1, source_target_pairs={{0,1},{1,0},{2,3},{3,2},{4,5},{5,4},{6,7},{7,6},{8,9},{9,8},{10,11... | collective-permute-start | bytes 1572872 | tf_op jit(solution)/shard_map/ppermute | solution.py:71
  132.5 15.0 %collective-permute-start.20 = (bf16[256,1024]{1,0:T(8,128)(2,1)}, bf16[256,1024]{1,0:T(8,128)(2,1)}, u32[]{:S(2)}, u32[]{:S(2)}) collective-permute-start(bf16[256,1024]{1,0:T(8,128)(2,1)} %fusion.10), channel_id=1, source_target_pairs={{0,2},{2,0},{1,3},{3,1},{4,6},{6,4},{5,7},{7,5},{8,10},{10,8},{9,1... | collective-permute-start | bytes 1572872 | tf_op jit(solution)/shard_map/ppermute | solution.py:71
  134.6 49.3 %collective-permute-start.26 = (bf16[128,256]{0,1:T(8,128)(2,1)}, bf16[128,256]{0,1:T(8,128)(2,1)}, u32[]{:S(2)}, u32[]{:S(2)}) collective-permute-start(bf16[128,256]{0,1:T(8,128)(2,1)} %bitcast.87), channel_id=1, source_target_pairs={{0,4},{4,0},{1,5},{5,1},{2,6},{6,2},{3,7},{7,3},{8,12},{12,8},{9,1... | collective-permute-start | bytes 196616 | tf_op jit(solution)/shard_map/ppermute | solution.py:71
  136.6 24.8 %collective-permute-start.16 = (bf16[512,512]{1,0:T(8,128)(2,1)}, bf16[512,512]{1,0:T(8,128)(2,1)}, u32[]{:S(2)}, u32[]{:S(2)}) collective-permute-start(bf16[512,512]{1,0:T(8,128)(2,1)} %bitcast.209), channel_id=1, source_target_pairs={{0,4},{4,0},{1,5},{5,1},{2,6},{6,2},{3,7},{7,3},{8,12},{12,8},{9,1... | collective-permute-start | bytes 1572872 | tf_op jit(solution)/shard_map/ppermute | solution.py:71
  163.1 8.6 %collective-permute-start.17 = (bf16[1,2,32,1024]{3,2,1,0:T(8,128)(2,1)S(1)}, bf16[1,2,32,1024]{3,2,1,0:T(8,128)(2,1)S(1)}, u32[]{:S(2)}, u32[]{:S(2)}) collective-permute-start(bf16[1,2,32,1024]{3,2,1,0:T(8,128)(2,1)S(1)} %select_convert_fusion), channel_id=1, source_target_pairs={{0,1},{1,0},{2,3},{3,2},{4,5},{5,4},{6,7},{7,6},{8,9},{9,8},{10,11... | collective-permute-start | bytes 393224 | tf_op jit(solution)/shard_map/ppermute | solution.py:71
  163.5 21.8 %all-to-all-start.4 = ((bf16[8,32,1024]{2,1,0:T(8,128)(2,1)}), bf16[8,32,1024]{2,1,0:T(8,128)(2,1)S(1)}, u32[]{:S(2)}, u32[]{:S(2)}) async-start(bf16[8,32,1024]{2,1,0:T(8,128)(2,1)} %bitcast.78), calls=%async_computation.4 | async-start | bytes 1048576 | tf_op jit(solution)/shard_map/all_to_all | solution.py:61
  169.6 14.4 %collective-permute-start.25 = (bf16[128,512]{1,0:T(8,128)(2,1)S(1)}, bf16[128,512]{1,0:T(8,128)(2,1)S(1)}, u32[]{:S(2)}, u32[]{:S(2)}) collective-permute-start(bf16[128,512]{1,0:T(8,128)(2,1)S(1)} %pad_maximum_fusion.3), channel_id=1, source_target_pairs={{0,4},{4,0},{1,5},{5,1},{2,6},{6,2},{3,7},{7,3},{8,12},{12,8},{9,1... | collective-permute-start | bytes 393224 | tf_op jit(solution)/shard_map/ppermute | solution.py:71
  171.6 11.8 %collective-permute-start.24 = (bf16[128,512]{0,1:T(8,128)(2,1)S(1)}, bf16[128,512]{0,1:T(8,128)(2,1)S(1)}, u32[]{:S(2)}, u32[]{:S(2)}) collective-permute-start(bf16[128,512]{0,1:T(8,128)(2,1)S(1)} %pad_maximum_fusion.2), channel_id=1, source_target_pairs={{0,4},{4,0},{1,5},{5,1},{2,6},{6,2},{3,7},{7,3},{8,12},{12,8},{9,1... | collective-permute-start | bytes 393224 | tf_op jit(solution)/shard_map/ppermute | solution.py:71
  171.9 13.2 %collective-permute-start.18 = (bf16[1,32,1024]{2,1,0:T(8,128)(2,1)S(1)}, bf16[1,32,1024]{2,1,0:T(8,128)(2,1)S(1)}, u32[]{:S(2)}, u32[]{:S(2)}) collective-permute-start(bf16[1,32,1024]{2,1,0:T(8,128)(2,1)S(1)} %fusion.51), channel_id=1, source_target_pairs={{0,2},{2,0},{1,3},{3,1},{4,6},{6,4},{5,7},{7,5},{8,10},{10,8},{9,1... | collective-permute-start | bytes 196616 | tf_op jit(solution)/shard_map/ppermute | solution.py:71
  193.6 6.0 %collective-permute-start.21 = (f32[2,8,128]{2,1,0:T(8,128)S(1)}, f32[2,8,128]{2,1,0:T(8,128)S(1)}, u32[]{:S(2)}, u32[]{:S(2)}) collective-permute-start(f32[2,8,128]{2,1,0:T(8,128)S(1)} %pad_maximum_fusion.12), channel_id=1, source_target_pairs={{0,4},{4,0},{1,5},{5,1},{2,6},{6,2},{3,7},{7,3},{8,12},{12,8},{9,1... | collective-permute-start | bytes 24584 | tf_op jit(solution)/shard_map/ppermute | solution.py:71
  195.1 25.7 %all-to-all-start.5 = ((bf16[4,128,768]{2,1,0:T(8,128)(2,1)}), bf16[4,128,768]{2,1,0:T(8,128)(2,1)S(1)}, u32[]{:S(2)}, u32[]{:S(2)}) async-start(bf16[4,128,768]{2,1,0:T(8,128)(2,1)} %pad_maximum_fusion), calls=%async_computation.5 | async-start | bytes 1572864 | tf_op jit(solution)/shard_map/all_to_all | solution.py:61
  199.6 13.3 %collective-permute-start.22 = (f32[2,8,128]{2,1,0:T(8,128)S(1)}, f32[2,8,128]{2,1,0:T(8,128)S(1)}, u32[]{:S(2)}, u32[]{:S(2)}) collective-permute-start(f32[2,8,128]{2,1,0:T(8,128)S(1)} %fusion.71), channel_id=1, source_target_pairs={{0,8},{8,0},{16,24},{24,16},{1,9},{9,1},{17,25},{25,17},{2,10},{10... | collective-permute-start | bytes 24584 | tf_op jit(solution)/shard_map/ppermute | solution.py:71
  212.9 7.4 %collective-permute-start.23 = (f32[2,8,128]{2,1,0:T(8,128)S(1)}, f32[2,8,128]{2,1,0:T(8,128)S(1)}, u32[]{:S(2)}, u32[]{:S(2)}) collective-permute-start(f32[2,8,128]{2,1,0:T(8,128)S(1)} %fusion.99), channel_id=1, source_target_pairs={{0,16},{8,24},{16,0},{24,8},{1,17},{9,25},{17,1},{25,9},{2,18},{10... | collective-permute-start | bytes 24584 | tf_op jit(solution)/shard_map/ppermute | solution.py:71
  (48 other events, 511.0 us)
